TPU v7x, 32 devices: a whole 2x2x4 slice. The times are simulated.
32 devices in a mesh: expert: 8 (over z, y), shard: 4 (over x, core).
Axes of the slice: x: 2, y: 2, z: 4, core: 2. Of those that a mesh axis runs over, the one named last changes fastest.
Arguments:
- inputs: bfloat16 [2048, 4, 1024], P('expert', 'shard'), may hold values from -6 to 6
- grad_out: bfloat16 [2048, 4, 1024], P('expert', 'shard'), may hold values from -6 to 6
- prefix: int32 [4], P('shard'), may hold values from 204 to 1024
- routes: int32 [2048, 4, 2], P('expert', 'shard'), may hold values from 0 to 31, all different within a row
- priority: int32 [8, 4, 256], P('expert', 'shard'), may hold values from 0 to 255, each once within a row
- loss_weights: float32 [2], replicated, may hold values from 4 to 32
- norm_attn: bfloat16 [1024], P('shard'), may hold values from 0.5 to 1.5
- norm_moe: bfloat16 [1024], P('shard'), may hold values from 0.5 to 1.5
- qkv_weight: bfloat16 [1024, 3072], P('shard'), may hold values from -0.1875 to 0.1875
- out_weight: bfloat16 [1024, 1024], P('shard'), may hold values from -3 to 3
- bias_table: bfloat16 [32, 16], P('shard'), may hold values from -5 to 5
- router_weight: bfloat16 [1024, 32], P('shard'), may hold values from -0.09375 to 0.09375
- gate_weight: bfloat16 [32, 1024, 2816], P('expert', None, 'shard'), may hold values from -0.1875 to 0.1875
- up_weight: bfloat16 [32, 1024, 2816], P('expert', None, 'shard'), may hold values from -0.1875 to 0.1875
- down_weight: bfloat16 [32, 1024, 2816], P('expert', None, 'shard'), may hold values from -0.109375 to 0.109375
Outputs:
- output: bfloat16 [2048, 4, 1024], P('expert', 'shard')
- input_grad: float32 [2048, 4, 1024], P('expert', 'shard')
- norm_attn_grad: float32 [1024], P('shard')
- norm_moe_grad: float32 [1024], P('shard')
- qkv_grad: float32 [1024, 3072], P('shard')
- out_grad: float32 [1024, 1024], P('shard')
- table_grad: float32 [32, 16], P('shard')
- router_grad: float32 [1024, 32], P('shard')
- gate_grad: float32 [32, 1024, 2816], P('expert', None, 'shard')
- up_grad: float32 [32, 1024, 2816], P('expert', None, 'shard')
- down_grad: float32 [32, 1024, 2816], P('expert', None, 'shard')
Inputs may be any that keep to these rules, and one draw needn't show every extreme that they name: `routes`: the 2 experts of a token differ. Each row priority[g, s] is a permutation of 0 to 255.
All inputs are finite; a program needn't handle non-finite values.
Results may differ from a plain program's by a relative error of at most 0.04.
Values may be sent and summed in bfloat16 or wider, within the bound.
A program may use at most 448 MiB of HBM per device.

v0:
```python
import jax
import jax.numpy as jnp
from jax import lax
from jax.sharding import PartitionSpec as P

D = 1024
HEADS = 16
HEAD = 64
FF = 2816
EXPERTS = 32
TOP = 2
BUCKETS = 32
CAP = 18


epsilon = 1e-06
masked_score = -1e30
group_heads = 2
far_bounds = (12, 16, 23, 32, 46, 64, 91)


def rms_norm(features, scales):
    factor = lax.rsqrt(jnp.mean(features * features, axis=-1, keepdims=True) + epsilon)
    return features * factor * scales


def geglu(gate_act, up_act):
    return jax.nn.gelu(gate_act, approximate=True) * up_act


def bucket_of(offsets):
    distance = jnp.abs(offsets)
    thresholds = jnp.array(far_bounds, dtype=jnp.int32)
    beyond = 8 + jnp.sum((distance[..., None] >= thresholds).astype(jnp.int32), axis=-1)
    nearby = jnp.where(distance < 8, distance, beyond)
    return nearby + 16 * (offsets > 0).astype(jnp.int32)


def pair_dest(token_routes, ranks):
    row_count = token_routes.shape[0]
    expert_pair = jnp.concatenate([token_routes[:, 0], token_routes[:, 1]])
    rank_pair = jnp.concatenate([ranks, ranks + row_count])
    earlier = (expert_pair[None, :] == expert_pair[:, None]) & (
        rank_pair[None, :] < rank_pair[:, None]
    )
    slot_index = jnp.sum(earlier.astype(jnp.int32), axis=1)
    return jnp.where(slot_index < CAP, expert_pair * CAP + slot_index, EXPERTS * CAP)


def router_head(logits, token_routes, weights):
    token_count = logits.shape[0]
    probabilities = jax.nn.softmax(logits, axis=-1)
    log_totals = jax.nn.logsumexp(logits, axis=-1)
    picked = (token_routes[:, :, None] == jnp.arange(EXPERTS, dtype=jnp.int32)).astype(jnp.float32)
    chosen = jnp.sum(picked * probabilities[:, None, :], axis=-1)
    gate_values = chosen / jnp.sum(chosen, axis=1, keepdims=True)
    shares = jnp.sum(picked, axis=(0, 1)) / (token_count * TOP)
    balance = EXPERTS * jnp.sum(shares * jnp.sum(probabilities, axis=0))
    return (gate_values, weights[0] * jnp.sum(log_totals * log_totals) + weights[1] * balance)


def bias_lookup(buckets, table_rows):
    bias = jnp.zeros((table_rows.shape[1],) + buckets.shape, jnp.float32)
    for bucket_id in range(BUCKETS):
        bias = jnp.where(buckets[None] == bucket_id, table_rows[bucket_id][:, None, None], bias)
    return bias


def bias_sums(buckets, grad_scores):
    return jnp.stack(
        [
            jnp.sum(jnp.where(buckets[None] == bucket_id, grad_scores, 0.0), axis=(1, 2))
            for bucket_id in range(BUCKETS)
        ],
        axis=0,
    )


def group_scores(query_rows, key_rows, table_rows, buckets, visible):
    raw_scores = jnp.einsum(
        "qhc,khc->hqk", query_rows, key_rows, preferred_element_type=jnp.float32
    )
    biased = raw_scores * HEAD ** (-0.5) + bias_lookup(buckets, table_rows)
    return jnp.where(visible[None], biased, masked_score)


def head_slice(matrix, head_group, row_count):
    columns = group_heads * HEAD
    return lax.dynamic_slice_in_dim(matrix, head_group * columns, columns, 1).reshape(
        row_count, group_heads, HEAD
    )


def attend_forward(queries, keys_all, values_all, table_wide, buckets, visible):
    row_count = queries.shape[0]
    key_count = keys_all.shape[0]
    columns = group_heads * HEAD

    def one_group(head_group, running):
        attended, log_totals = running
        query_rows = head_slice(queries, head_group, row_count)
        key_rows = head_slice(keys_all, head_group, key_count)
        value_rows = head_slice(values_all, head_group, key_count)
        table_rows = lax.dynamic_slice_in_dim(table_wide, head_group * group_heads, group_heads, 1)
        scores = group_scores(query_rows, key_rows, table_rows, buckets, visible)
        top_score = jnp.max(scores, axis=-1, keepdims=True)
        expos = jnp.exp(scores - top_score)
        total_sum = jnp.sum(expos, axis=-1, keepdims=True)
        weights_low = (expos / total_sum).astype(jnp.bfloat16)
        mixed = jnp.einsum(
            "hqk,khc->qhc", weights_low, value_rows, preferred_element_type=jnp.float32
        )
        attended = lax.dynamic_update_slice_in_dim(
            attended,
            mixed.astype(jnp.bfloat16).reshape(row_count, columns),
            head_group * columns,
            1,
        )
        log_totals = lax.dynamic_update_slice_in_dim(
            log_totals, (top_score + jnp.log(total_sum))[:, :, 0], head_group * group_heads, 0
        )
        return (attended, log_totals)

    start_state = (
        jnp.zeros((row_count, HEADS * HEAD), jnp.bfloat16),
        jnp.zeros((HEADS, row_count), jnp.float32),
    )
    return lax.fori_loop(0, HEADS // group_heads, one_group, start_state)


def attend_backward(
    queries, keys_all, values_all, table_wide, buckets, visible, log_totals, grad_mixed
):
    row_count = queries.shape[0]
    key_count = keys_all.shape[0]
    columns = group_heads * HEAD
    score_scale = HEAD ** (-0.5)

    def one_group(head_group, running):
        grad_queries, grad_keys, grad_values, grad_table, inner_all = running
        query_rows = head_slice(queries, head_group, row_count)
        key_rows = head_slice(keys_all, head_group, key_count)
        value_rows = head_slice(values_all, head_group, key_count)
        grad_rows = head_slice(grad_mixed, head_group, row_count)
        table_rows = lax.dynamic_slice_in_dim(table_wide, head_group * group_heads, group_heads, 1)
        totals_rows = lax.dynamic_slice_in_dim(log_totals, head_group * group_heads, group_heads, 0)
        scores = group_scores(query_rows, key_rows, table_rows, buckets, visible)
        attention = jnp.exp(scores - totals_rows[:, :, None])
        grad_weights = jnp.einsum(
            "qhc,khc->hqk", grad_rows, value_rows, preferred_element_type=jnp.float32
        )
        inner = jnp.sum(grad_weights * attention, axis=-1, keepdims=True)
        grad_scores = attention * (grad_weights - inner)
        grad_table = lax.dynamic_update_slice_in_dim(
            grad_table, bias_sums(buckets, grad_scores), head_group * group_heads, 1
        )
        scaled = (grad_scores * score_scale).astype(jnp.bfloat16)
        query_part = jnp.einsum(
            "hqk,khc->qhc", scaled, key_rows, preferred_element_type=jnp.float32
        )
        grad_queries = lax.dynamic_update_slice_in_dim(
            grad_queries, query_part.reshape(row_count, columns), head_group * columns, 1
        )
        key_part = jnp.einsum(
            "hqk,qhc->khc", scaled, query_rows, preferred_element_type=jnp.float32
        )
        value_part = jnp.einsum(
            "hqk,qhc->khc",
            attention.astype(jnp.bfloat16),
            grad_rows,
            preferred_element_type=jnp.float32,
        )
        grad_keys = lax.dynamic_update_slice_in_dim(
            grad_keys, key_part.reshape(key_count, columns), head_group * columns, 1
        )
        grad_values = lax.dynamic_update_slice_in_dim(
            grad_values, value_part.reshape(key_count, columns), head_group * columns, 1
        )
        inner_all = lax.dynamic_update_slice_in_dim(
            inner_all, inner[:, :, 0], head_group * group_heads, 0
        )
        return (grad_queries, grad_keys, grad_values, grad_table, inner_all)

    start_state = (
        jnp.zeros((row_count, HEADS * HEAD), jnp.float32),
        jnp.zeros((key_count, HEADS * HEAD), jnp.float32),
        jnp.zeros((key_count, HEADS * HEAD), jnp.float32),
        jnp.zeros((BUCKETS, HEADS), jnp.float32),
        jnp.zeros((HEADS, row_count), jnp.float32),
    )
    return lax.fori_loop(0, HEADS // group_heads, one_group, start_state)


def to_experts(slot_rows):
    return lax.all_to_all(slot_rows, "expert", split_axis=0, concat_axis=1, tiled=True)


def from_experts(expert_rows):
    return lax.all_to_all(expert_rows, "expert", split_axis=1, concat_axis=0, tiled=True)


def expert_forward_weights(received, gate_weight, up_weight, down_weight):
    experts_here, slot_count, width_in = received.shape

    def add_piece(running, pieces, first_unit):
        gate_piece, up_piece, down_piece = pieces
        gate_act = jnp.einsum(
            "erd,edf->erf", received, gate_piece, preferred_element_type=jnp.float32
        )
        up_act = jnp.einsum("erd,edf->erf", received, up_piece, preferred_element_type=jnp.float32)
        hidden = geglu(gate_act, up_act).astype(jnp.bfloat16)
        out_sum = jnp.einsum("erf,edf->erd", hidden, down_piece, preferred_element_type=jnp.float32)
        return (out_sum, gate_act, up_act)

    start_state = (
        jnp.zeros((experts_here, slot_count, width_in), jnp.float32),
        jnp.zeros((experts_here, slot_count, FF), jnp.float32),
        jnp.zeros((experts_here, slot_count, FF), jnp.float32),
    )
    out_sum, gate_keep, up_keep = add_piece(
        start_state,
        (
            lax.all_gather(gate_weight, "shard", axis=2, tiled=True),
            lax.all_gather(up_weight, "shard", axis=2, tiled=True),
            lax.all_gather(down_weight, "shard", axis=2, tiled=True),
        ),
        jnp.int32(0),
    )
    return (out_sum.astype(jnp.bfloat16), (received, gate_keep, up_keep))


def expert_backward_weights(grad_received, kept, gate_weight, up_weight, down_weight):
    received, gate_keep, up_keep = kept
    experts_here, slot_count, width_in = received.shape

    def add_piece(running, pieces, first_unit):
        gate_piece, up_piece, down_piece = pieces
        grad_hidden = jnp.einsum(
            "erd,edf->erf", grad_received, down_piece, preferred_element_type=jnp.float32
        )
        hidden, geglu_back = jax.vjp(geglu, gate_keep, up_keep)
        grad_gate, grad_up = geglu_back(grad_hidden)
        grad_gate = grad_gate.astype(jnp.bfloat16)
        grad_up = grad_up.astype(jnp.bfloat16)
        grad_sum = jnp.einsum(
            "erf,edf->erd", grad_gate, gate_piece, preferred_element_type=jnp.float32
        )
        grad_sum = grad_sum + jnp.einsum(
            "erf,edf->erd", grad_up, up_piece, preferred_element_type=jnp.float32
        )
        hidden_keep = hidden.astype(jnp.bfloat16)
        return (grad_sum, grad_gate, grad_up, hidden_keep)

    start_state = (
        jnp.zeros((experts_here, slot_count, width_in), jnp.float32),
        jnp.zeros((experts_here, slot_count, FF), jnp.bfloat16),
        jnp.zeros((experts_here, slot_count, FF), jnp.bfloat16),
        jnp.zeros((experts_here, slot_count, FF), jnp.bfloat16),
    )
    grad_sum, grad_gate_all, grad_up_all, hidden_all = add_piece(
        start_state,
        (
            lax.all_gather(gate_weight, "shard", axis=2, tiled=True),
            lax.all_gather(up_weight, "shard", axis=2, tiled=True),
            lax.all_gather(down_weight, "shard", axis=2, tiled=True),
        ),
        jnp.int32(0),
    )
    local_grads = lax.psum_scatter(
        jnp.stack(
            [
                jnp.einsum(
                    "erd,erf->fed", received, grad_gate_all, preferred_element_type=jnp.float32
                ),
                jnp.einsum(
                    "erd,erf->fed", received, grad_up_all, preferred_element_type=jnp.float32
                ),
                jnp.einsum(
                    "erd,erf->fed", grad_received, hidden_all, preferred_element_type=jnp.float32
                ),
            ],
            axis=1,
        ).astype(jnp.bfloat16),
        "shard",
        scatter_dimension=0,
        tiled=True,
    ).astype(jnp.float32)
    gate_grad = jnp.transpose(local_grads[:, 0], (1, 2, 0))
    up_grad = jnp.transpose(local_grads[:, 1], (1, 2, 0))
    down_grad = jnp.transpose(local_grads[:, 2], (1, 2, 0))
    return (grad_sum.astype(jnp.bfloat16), gate_grad, up_grad, down_grad)


def shards(
    inputs,
    grad_out,
    prefix,
    routes,
    priority,
    loss_weights,
    norm_attn,
    norm_moe,
    qkv_weight,
    out_weight,
    bias_table,
    router_weight,
    gate_weight,
    up_weight,
    down_weight,
):
    row_count = inputs.shape[0]
    length = row_count * lax.axis_size("expert")
    first_row = lax.axis_index("expert") * row_count
    gain_attn, gain_moe, qkv_full, out_full, table_full, router_full = (
        lax.all_gather(norm_attn, "shard", axis=0, tiled=True),
        lax.all_gather(norm_moe, "shard", axis=0, tiled=True),
        lax.all_gather(qkv_weight, "shard", axis=0, tiled=True),
        lax.all_gather(out_weight, "shard", axis=0, tiled=True),
        lax.all_gather(bias_table, "shard", axis=0, tiled=True),
        lax.all_gather(router_weight, "shard", axis=0, tiled=True),
    )
    tokens_in = inputs.reshape(row_count, D).astype(jnp.float32)
    normed_one, norm_one_back = jax.vjp(rms_norm, tokens_in, gain_attn.astype(jnp.float32))
    low_one = normed_one.astype(jnp.bfloat16)
    projected = jnp.dot(low_one, qkv_full, preferred_element_type=jnp.float32).astype(jnp.bfloat16)
    queries = projected[:, :D]
    keys_own = projected[:, D : 2 * D]
    values_own = projected[:, 2 * D :]
    keys_all, values_all = (
        lax.all_gather(keys_own, "expert", axis=0, tiled=True),
        lax.all_gather(values_own, "expert", axis=0, tiled=True),
    )
    row_pos = first_row + jnp.arange(row_count, dtype=jnp.int32)
    key_pos = jnp.arange(length, dtype=jnp.int32)
    visible = (key_pos[None, :] <= row_pos[:, None]) | (key_pos[None, :] < prefix[0])
    buckets = bucket_of(key_pos[None, :] - row_pos[:, None])
    table_wide = table_full.astype(jnp.float32)
    attended, log_totals = attend_forward(
        queries, keys_all, values_all, table_wide, buckets, visible
    )
    middle = tokens_in + jnp.dot(attended, out_full, preferred_element_type=jnp.float32)
    normed_two, norm_two_back = jax.vjp(rms_norm, middle, gain_moe.astype(jnp.float32))
    low_two = normed_two.astype(jnp.bfloat16)
    logits = jnp.dot(low_two, router_full, preferred_element_type=jnp.float32)
    token_routes = routes.reshape(row_count, TOP)
    router_out, router_back = jax.vjp(
        lambda logit_in: router_head(logit_in, token_routes, loss_weights), logits
    )
    gate_values = router_out[0]
    destination = pair_dest(token_routes, priority.reshape(row_count))
    slot_map = (
        (jnp.arange(EXPERTS * CAP, dtype=jnp.int32)[:, None] == destination[None, :])
        .astype(jnp.bfloat16)
        .reshape(EXPERTS * CAP, TOP, row_count)
    )
    outgoing = jnp.einsum(
        "skt,td->sd", slot_map, low_two, preferred_element_type=jnp.float32
    ).astype(jnp.bfloat16)
    received = to_experts(outgoing.reshape(EXPERTS, CAP, D))
    results, kept = expert_forward_weights(received, gate_weight, up_weight, down_weight)
    returned = from_experts(results).reshape(EXPERTS * CAP, D)
    pair_out = jnp.einsum("skt,sd->ktd", slot_map, returned, preferred_element_type=jnp.float32)
    mixture = gate_values[:, 0:1] * pair_out[0] + gate_values[:, 1:2] * pair_out[1]
    output = (middle + mixture).astype(jnp.bfloat16)
    grad_top = grad_out.reshape(row_count, D).astype(jnp.float32)
    grad_gates = jnp.transpose(jnp.sum(grad_top[None] * pair_out, axis=-1))
    grad_pairs = (jnp.transpose(gate_values)[:, :, None] * grad_top[None]).astype(jnp.bfloat16)
    grad_slots = jnp.einsum(
        "skt,ktd->sd", slot_map, grad_pairs, preferred_element_type=jnp.float32
    ).astype(jnp.bfloat16)
    grad_received = to_experts(grad_slots.reshape(EXPERTS, CAP, D))
    grad_results, gate_grad, up_grad, down_grad = expert_backward_weights(
        grad_received, kept, gate_weight, up_weight, down_weight
    )
    grad_returned = from_experts(grad_results).reshape(EXPERTS * CAP, D)
    grad_low_two = jnp.einsum(
        "skt,sd->td", slot_map, grad_returned, preferred_element_type=jnp.float32
    )
    grad_logits = router_back((grad_gates, jnp.ones((), jnp.float32)))[0]
    low_logits = grad_logits.astype(jnp.bfloat16)
    router_grad = jnp.dot(low_two.T, low_logits, preferred_element_type=jnp.float32)
    grad_low_two = grad_low_two + jnp.dot(
        low_logits, router_full.T, preferred_element_type=jnp.float32
    )
    grad_middle_norm, gain_moe_grad = norm_two_back(grad_low_two)
    grad_middle = grad_top + grad_middle_norm
    low_middle = grad_middle.astype(jnp.bfloat16)
    out_grad = jnp.dot(attended.T, low_middle, preferred_element_type=jnp.float32)
    grad_attended = jnp.dot(low_middle, out_full.T, preferred_element_type=jnp.float32).astype(
        jnp.bfloat16
    )
    grad_queries, grad_keys_all, grad_values_all, table_grad, inner_rows = attend_backward(
        queries, keys_all, values_all, table_wide, buckets, visible, log_totals, grad_attended
    )
    grad_keys, grad_values = (
        lax.psum_scatter(
            grad_keys_all.astype(jnp.bfloat16), "expert", scatter_dimension=0, tiled=True
        ).astype(jnp.float32),
        lax.psum_scatter(
            grad_values_all.astype(jnp.bfloat16), "expert", scatter_dimension=0, tiled=True
        ).astype(jnp.float32),
    )
    grad_projected = jnp.concatenate(
        [
            grad_queries.astype(jnp.bfloat16),
            grad_keys.astype(jnp.bfloat16),
            grad_values.astype(jnp.bfloat16),
        ],
        axis=1,
    )
    qkv_grad = jnp.dot(low_one.T, grad_projected, preferred_element_type=jnp.float32)
    grad_low_one = jnp.dot(grad_projected, qkv_full.T, preferred_element_type=jnp.float32)
    grad_tokens_norm, gain_attn_grad = norm_one_back(grad_low_one)
    input_grad = grad_middle + grad_tokens_norm
    attn_part, moe_part, qkv_part, out_part, table_part, router_part = (
        lax.psum_scatter(
            gain_attn_grad.astype(jnp.bfloat16), "shard", scatter_dimension=0, tiled=True
        ).astype(jnp.float32),
        lax.psum_scatter(
            gain_moe_grad.astype(jnp.bfloat16), "shard", scatter_dimension=0, tiled=True
        ).astype(jnp.float32),
        lax.psum_scatter(
            qkv_grad.astype(jnp.bfloat16), "shard", scatter_dimension=0, tiled=True
        ).astype(jnp.float32),
        lax.psum_scatter(
            out_grad.astype(jnp.bfloat16), "shard", scatter_dimension=0, tiled=True
        ).astype(jnp.float32),
        lax.psum_scatter(
            table_grad.astype(jnp.bfloat16), "shard", scatter_dimension=0, tiled=True
        ).astype(jnp.float32),
        lax.psum_scatter(
            router_grad.astype(jnp.bfloat16), "shard", scatter_dimension=0, tiled=True
        ).astype(jnp.float32),
    )
    attn_total, moe_total, qkv_total, out_total, table_total, router_total = (
        lax.psum(attn_part.astype(jnp.bfloat16), "expert").astype(jnp.float32),
        lax.psum(moe_part.astype(jnp.bfloat16), "expert").astype(jnp.float32),
        lax.psum(qkv_part.astype(jnp.bfloat16), "expert").astype(jnp.float32),
        lax.psum(out_part.astype(jnp.bfloat16), "expert").astype(jnp.float32),
        lax.psum(table_part.astype(jnp.bfloat16), "expert").astype(jnp.float32),
        lax.psum(router_part.astype(jnp.bfloat16), "expert").astype(jnp.float32),
    )
    return (
        output.reshape(row_count, 1, D),
        input_grad.reshape(row_count, 1, D),
        attn_total,
        moe_total,
        qkv_total,
        out_total,
        table_total,
        router_total,
        gate_grad,
        up_grad,
        down_grad,
    )


def solution(mesh):
    placed = (
        P("expert", "shard", None),
        P("expert", "shard", None),
        P("shard"),
        P("expert", "shard", None),
        P("expert", "shard", None),
        P(),
        P("shard"),
        P("shard"),
        P("shard", None),
        P("shard", None),
        P("shard", None),
        P("shard", None),
        P("expert", None, "shard"),
        P("expert", None, "shard"),
        P("expert", None, "shard"),
    )
    return jax.shard_map(
        shards,
        mesh=mesh,
        in_specs=placed,
        out_specs=(
            P("expert", "shard", None),
            P("expert", "shard", None),
            P("shard"),
            P("shard"),
            P("shard", None),
            P("shard", None),
            P("shard", None),
            P("shard", None),
            P("expert", None, "shard"),
            P("expert", None, "shard"),
            P("expert", None, "shard"),
        ),
        check_vma=False,
    )
```

profile of v0, /device:TPU:0, one launch (start us, length us, event | category | flops | bytes accessed | tf_op | source)
XLA Modules:
  0.0 2536.7 jit_solution(2461665313787327570)
XLA Ops:
  16.4 42.3 %all-gather.10.cloned.1.call-done = bf16[1024,3072]{1,0:T(8,128)(2,1)} async-done(((bf16[256,3072]{1,0:T(8,128)(2,1)}), bf16[1024,3072]{1,0:T(8,128)(2,1)}) %all-gather.10.cloned.1.call-update) | async-done | bytes 6291472 | tf_op jit(solution)/shard_map/all_gather | solution.py:317
  91.1 47.1 %all-gather.14.cloned.1.call-done = bf16[2048,1024]{1,0:T(8,128)(2,1)} async-done(((bf16[256,1024]{1,0:T(8,128)(2,1)}), bf16[2048,1024]{1,0:T(8,128)(2,1)}) %all-gather.14.cloned.1.call-update) | async-done | bytes 4194320 | tf_op jit(solution)/shard_map/all_gather | solution.py:330
  144.7 67.9 %all-gather.12.cloned.1.call-done = bf16[2048,1024]{1,0:T(8,128)(2,1)} async-done(((bf16[256,1024]{1,0:T(8,128)(2,1)}), bf16[2048,1024]{1,0:T(8,128)(2,1)}) %all-gather.12.cloned.1.call-update) | async-done | bytes 4194320 | tf_op jit(solution)/shard_map/all_gather | solution.py:331
  219.9 345.0 %while.36 = (s32[]{:T(128)}, bf16[256,1024]{0,1:T(8,128)(2,1)}, f32[16,256]{1,0:T(8,128)S(1)}, bf16[2048,1024]{0,1:T(8,128)(2,1)}, bf16[256,1024]{0,1:T(8,128)(2...) while((s32[]{:T(128)}, bf16[256,1024]{0,1:T(8,128)(2,1)}, ...), condition=%wide.region_5.6_spmd.clone, body=%wide.region_2.5_spmd.clone.sunk | while | flops 329285152 | bytes 69620496 | solution.py:128
  224.0 11.9 broadcast_compare_fusion.66
  235.9 21.8 fusion.170
  266.7 11.9 broadcast_compare_fusion.66
  278.6 21.8 fusion.170
  309.1 11.9 broadcast_compare_fusion.66
  321.0 21.8 fusion.170
  351.5 11.9 broadcast_compare_fusion.66
  363.4 21.8 fusion.170
  396.5 11.9 broadcast_compare_fusion.66
  408.4 21.8 fusion.170
  438.9 11.9 broadcast_compare_fusion.66
  450.8 21.8 fusion.170
  481.6 11.9 broadcast_compare_fusion.66
  493.5 21.8 fusion.170
  535.9 23.7 fusion.170
  582.9 30.8 %all-to-all-done.2 = bf16[32,18,1024]{2,1,0:T(8,128)(2,1)} async-done(((bf16[32,18,1024]{2,1,0:T(8,128)(2,1)}), bf16[32,18,1024]{2,1,0:T(8,128)(2,1)}, u32[]{:S(2)}, u32[]{:S(2)}) %all-to-all-start.2) | async-done | bytes 1179680 | tf_op jit(solution)/shard_map/all_to_all | solution.py:195
  621.4 33.0 %all-to-all-done = bf16[32,18,1024]{2,1,0:T(8,128)(2,1)} async-done(((bf16[32,18,1024]{2,1,0:T(8,128)(2,1)}), bf16[32,18,1024]{2,1,0:T(8,128)(2,1)}, u32[]{:S(2)}, u32[]{:S(2)}) %all-to-all-start) | async-done | bytes 1179680 | tf_op jit(solution)/shard_map/all_to_all | solution.py:195
  656.8 14.4 fusion.68
  671.1 14.0 fusion.70
  685.1 20.6 multiply_convert_fusion.3
  733.2 12.1 convolution_convert_fusion.4
  747.2 14.7 all-to-all-done.3
  773.7 20.8 all-to-all-done.1
  814.5 798.8 %while.37 = (s32[]{:T(128)}, bf16[256,1024]{0,1:T(8,128)(2,1)}, bf16[2048,1024]{0,1:T(8,128)(2,1)}, bf16[2048,1024]{0,1:T(8,128)(2,1)}, bf16[32,16]{0,1:T(8,128)...) while((s32[]{:T(128)}, bf16[256,1024]{0,1:T(8,128)(2,1)}, ...), condition=%wide.region_54.55_spmd.clone, body=%wide.region_20.54_spmd.clone.sunk | while | flops 1076895232 | bytes 126759440 | solution.py:191
  835.7 22.0 subtract_exponential_fusion.5
  857.7 17.9 select_reduce_fusion.37
  894.1 14.1 select_reduce_fusion.38
  935.5 22.0 subtract_exponential_fusion.5
  957.5 17.9 select_reduce_fusion.37
  993.9 14.1 select_reduce_fusion.38
  1035.3 22.0 subtract_exponential_fusion.5
  1057.3 17.9 select_reduce_fusion.37
  1093.6 14.1 select_reduce_fusion.38
  1135.0 22.0 subtract_exponential_fusion.5
  1157.0 17.9 select_reduce_fusion.37
  1193.4 14.1 select_reduce_fusion.38
  1234.8 22.0 subtract_exponential_fusion.5
  1256.8 17.9 select_reduce_fusion.37
  1293.2 14.1 select_reduce_fusion.38
  1334.6 22.0 subtract_exponential_fusion.5
  1356.6 17.9 select_reduce_fusion.37
  1393.0 14.1 select_reduce_fusion.38
  1434.4 22.0 subtract_exponential_fusion.5
  1456.4 17.9 select_reduce_fusion.37
  1492.7 14.1 select_reduce_fusion.38
  1534.1 22.0 subtract_exponential_fusion.5
  1556.1 17.9 select_reduce_fusion.37
  1592.5 14.1 select_reduce_fusion.38
  1616.7 83.7 %reduce-scatter.7.cloned.1.call-done = bf16[256,1024]{0,1:T(8,128)(2,1)} async-done(((bf16[2048,1024]{0,1:T(8,128)(2,1)}), bf16[256,1024]{0,1:T(8,128)(2,1)}) %reduce-scatter.7.cloned.1.call-update) | async-done | bytes 524304 | tf_op jit(solution)/shard_map/reduce_scatter | solution.py:396
  1700.5 92.7 %reduce-scatter.9.cloned.1.call-done = bf16[256,1024]{0,1:T(8,128)(2,1)} async-done(((bf16[2048,1024]{0,1:T(8,128)(2,1)}), bf16[256,1024]{0,1:T(8,128)(2,1)}) %reduce-scatter.9.cloned.1.call-update) | async-done | bytes 524304 | tf_op jit(solution)/shard_map/reduce_scatter | solution.py:399
  1800.4 13.6 convert_bitcast_fusion.1
  1814.0 13.1 convert_bitcast_fusion.2
  1828.1 15.6 convert_bitcast_fusion
  1843.7 45.3 %reduce-scatter.11.cloned.1.call-done = bf16[256,3072]{1,0:T(8,128)(2,1)} async-done(((bf16[1024,3072]{1,0:T(8,128)(2,1)}), bf16[256,3072]{1,0:T(8,128)(2,1)}) %reduce-scatter.11.cloned.1.call-update) | async-done | bytes 1572880 | tf_op jit(solution)/shard_map/reduce_scatter | solution.py:422
  1889.1 46.2 %pad_maximum_fusion = bf16[2816,3,4,1024]{3,0,2,1:T(8,128)(2,1)} fusion(bf16[2816,1,4,1024]{3,0,2,1:T(8,128)(2,1)} %convert_bitcast_fusion, bf16[2816,1,4,1024]{3,0,2,1:T(8,128)(2,1)} %convert_bitcast_fusion.1, bf16[2816,1,4,1024]{3,0,2,1:T(8,128)(2,1)} %convert_bitcast_fusion.2), kind=kLoop, calls=%fused_computation.203 | loop fusion | flops 69206016 | bytes 138412032 | tf_op jit(solution)/shard_map/stack | solution.py:270
  1955.6 37.9 %all-reduce.3 = (bf16[256]{0:T(256)(128)(2,1)S(1)}, bf16[256]{0:T(256)(128)(2,1)S(1)}, bf16[8,16]{1,0:T(8,128)(2,1)S(1)}, bf16[256,32]{0,1:T(8,128)(2,1)S(1)}) all-reduce(bf16[256]{0:T(256)(128)(2,1)S(1)} %dynamic-slice.1, bf16[256]{0:T(256)(128)(2,1)S(1)} %dynamic-slice.3, ...), channel_id=1, replica_groups=mesh['expert'=8,'shard'=4] {'expert'}, use_global_device_ids=true, to_apply=%region_60.61 | all-reduce | flops 8832 | bytes 35328 | tf_op jit(solution)/shard_map/psum | solution.py:436
  1995.8 22.0 all-reduce.8.cloned.1.call-done
  2023.4 461.8 %reduce-scatter.17.cloned.1.call-done = bf16[704,3,4,1024]{3,0,2,1:T(8,128)(2,1)} async-done(((bf16[2816,3,4,1024]{3,0,2,1:T(8,128)(2,1)}), bf16[704,3,4,1024]{3,0,2,1:T(8,128)(2,1)}) %reduce-scatter.17.cloned.1.call-update) | async-done | bytes 17301520 | tf_op jit(solution)/shard_map/reduce_scatter | solution.py:269
  2485.2 19.1 convert_element_type.227
  2504.4 25.6 %slice_bitcast_fusion = (f32[4,1024,704]{1,2,0:T(8,128)}, f32[4,1024,704]{1,2,0:T(8,128)}, f32[4,1024,704]{1,2,0:T(8,128)}) fusion(f32[704,3,4,1024]{3,0,2,1:T(8,128)} %convert_element_type.227), kind=kLoop, calls=%fused_computation.208 | loop fusion | bytes 69206016 | tf_op jit(solution)/shard_map/transpose | solution.py:290
  (800 shorter events, 631.2 us)
Async XLA Ops:
  7.2 51.5 %all-gather.10.cloned.1.call-start = ((), (), s32[]{:S(2)}) async-start(), calls=%async_computation.10 | async-start | bytes 7864320 | tf_op jit(solution)/shard_map/all_gather | solution.py:317
  7.9 130.3 %all-gather.14.cloned.1.call-start = ((), (), s32[]{:S(2)}) async-start(), calls=%async_computation.12 | async-start | bytes 4718592 | tf_op jit(solution)/shard_map/all_gather | solution.py:330
  14.6 48.9 %copy-start.40 = (f32[4,1,256]{2,1,0:T(1,128)}, f32[4,1,256]{2,1,0:T(1,128)S(1)}, u32[]{:S(2)}) copy-start(f32[4,1,256]{2,1,0:T(1,128)S(1)} %convert_element_type.230) | copy-start | bytes 12292
  16.4 47.2 %copy-start.52 = (f32[256]{0:T(256)}, f32[256]{0:T(256)S(1)}, u32[]{:S(2)}) copy-start(f32[256]{0:T(256)S(1)} %fusion.85) | copy-start | bytes 3076
  64.7 148.0 %all-gather.12.cloned.1.call-start = ((), (), s32[]{:S(2)}) async-start(), calls=%async_computation.11 | async-start | bytes 4718592 | tf_op jit(solution)/shard_map/all_gather | solution.py:331
  65.4 499.6 %all-gather.16.cloned.1.call-start = ((), (), s32[]{:S(2)}) async-start(), calls=%async_computation.13 | async-start | bytes 2621440 | tf_op jit(solution)/shard_map/all_gather | solution.py:318
  66.0 590.8 %all-gather.20.cloned.1.call-start = ((), (), s32[]{:S(2)}) async-start(), calls=%async_computation.15 | async-start | bytes 28835840 | tf_op jit(solution)/shard_map/all_gather | solution.py:224
  66.6 604.6 %all-gather.18.cloned.1.call-start = ((), (), s32[]{:S(2)}) async-start(), calls=%async_computation.14 | async-start | bytes 28835840 | tf_op jit(solution)/shard_map/all_gather | solution.py:223
  67.2 7.2 copy-start.35
  67.2 7.6 copy-start.54
  67.2 12.8 copy-start.39
  67.2 18.6 copy-start.20
  67.2 20.0 copy-start.56
  67.3 617.9 %all-gather.22.cloned.1.call-start = ((), (), s32[]{:S(2)}) async-start(), calls=%async_computation.16 | async-start | bytes 28835840 | tf_op jit(solution)/shard_map/all_gather | solution.py:225
  385.2 5.7 copy-start.1
  564.9 3.8 copy-start.31
  565.0 4.0 copy-start.24
  565.0 4.3 copy-start.36
  565.0 4.5 copy-start.34
  565.0 4.4 copy-start.17
  568.9 9.4 copy-start.13
  569.2 234.3 %copy-start.22 = (f32[256,32]{0,1:T(8,128)}, f32[256,32]{0,1:T(8,128)S(1)}, u32[]{:S(2)}) copy-start(f32[256,32]{0,1:T(8,128)S(1)} %get-tuple-element.875) | copy-start | bytes 98308
  569.2 234.3 %copy-start.29 = (f32[256]{0:T(256)}, f32[256]{0:T(256)S(1)}, u32[]{:S(2)}) copy-start(f32[256]{0:T(256)S(1)} %get-tuple-element.874) | copy-start | bytes 3076
  569.3 234.3 %copy-start.32 = (f32[256]{0:T(256)}, f32[256]{0:T(256)S(1)}, u32[]{:S(2)}) copy-start(f32[256]{0:T(256)S(1)} %fusion.82) | copy-start | bytes 3076
  573.8 40.0 %all-to-all-start.2 = ((bf16[32,18,1024]{2,1,0:T(8,128)(2,1)}), bf16[32,18,1024]{2,1,0:T(8,128)(2,1)}, u32[]{:S(2)}, u32[]{:S(2)}) async-start(bf16[32,18,1024]{2,1,0:T(8,128)(2,1)} %reshape.760), calls=%async_computation.2 | async-start | bytes 3145728 | tf_op jit(solution)/shard_map/all_to_all | solution.py:195
  613.7 40.7 %all-to-all-start = ((bf16[32,18,1024]{2,1,0:T(8,128)(2,1)}), bf16[32,18,1024]{2,1,0:T(8,128)(2,1)}, u32[]{:S(2)}, u32[]{:S(2)}) async-start(bf16[32,18,1024]{2,1,0:T(8,128)(2,1)} %reshape.757), calls=%async_computation | async-start | bytes 3145728 | tf_op jit(solution)/shard_map/all_to_all | solution.py:195
  656.7 14.4 copy-start.5
  705.7 10.8 copy-start.11
  729.5 32.4 %all-to-all-start.3 = ((bf16[4,144,1024]{2,0,1:T(4,128)(2,1)}), bf16[4,144,1024]{2,0,1:T(4,128)(2,1)S(1)}, u32[]{:S(2)}, u32[]{:S(2)}) async-start(bf16[4,144,1024]{2,0,1:T(4,128)(2,1)} %copy.215), calls=%async_computation.3 | async-start | bytes 2359296 | tf_op jit(solution)/shard_map/all_to_all | solution.py:199
  745.3 21.0 copy-start.55
  761.9 32.6 %all-to-all-start.1 = ((bf16[4,144,1024]{2,0,1:T(4,128)(2,1)}), bf16[4,144,1024]{2,0,1:T(4,128)(2,1)}, u32[]{:S(2)}, u32[]{:S(2)}) async-start(bf16[4,144,1024]{2,0,1:T(4,128)(2,1)} %copy.211), calls=%async_computation.1 | async-start | bytes 2359296 | tf_op jit(solution)/shard_map/all_to_all | solution.py:199
  766.2 934.3 %reduce-scatter.7.cloned.1.call-start = ((), (), s32[]{:S(2)}) async-start(), calls=%async_computation.17 | async-start | bytes 4718592 | tf_op jit(solution)/shard_map/reduce_scatter | solution.py:396
  767.5 36.1 %copy-start.49 = (f32[32]{0:T(128)}, f32[32]{0:T(128)S(1)}, u32[]{:S(2)}) copy-start(f32[32]{0:T(128)S(1)} %broadcast_multiply_fusion) | copy-start | bytes 388
  767.5 36.0 %copy-start.37 = (f32[256]{0:T(256)}, f32[256]{0:T(256)S(1)}, u32[]{:S(2)}) copy-start(f32[256]{0:T(256)S(1)} %get-tuple-element.882) | copy-start | bytes 3076
  797.4 6.2 copy-start.8
  799.9 4.9 copy-start.21
  835.7 22.0 copy-start.2
  935.5 22.0 copy-start.2
  1035.3 22.0 copy-start.2
  1135.0 22.0 copy-start.2
  1234.8 22.0 copy-start.2
  1334.6 22.0 copy-start.2
  1434.4 22.0 copy-start.2
  1534.1 22.0 copy-start.2
  1613.3 179.9 %reduce-scatter.9.cloned.1.call-start = ((), (), s32[]{:S(2)}) async-start(), calls=%async_computation.18 | async-start | bytes 4718592 | tf_op jit(solution)/shard_map/reduce_scatter | solution.py:399
  1613.4 179.8 %copy-start.16 = (bf16[256,1,1024]{2,0,1:T(8,128)(2,1)S(1)}, bf16[256,1,1024]{2,0,1:T(8,128)(2,1)}, u32[]{:S(2)}) copy-start(bf16[256,1,1024]{2,0,1:T(8,128)(2,1)} %param.20) | copy-start | bytes 1572868
  1613.4 179.8 %copy-start.27 = (bf16[256,1024]{0,1:T(8,128)(2,1)S(1)}, bf16[256,1024]{0,1:T(8,128)(2,1)}, u32[]{:S(2)}) copy-start(bf16[256,1024]{0,1:T(8,128)(2,1)} %get-tuple-element.385) | copy-start | bytes 1572868
  1613.4 179.8 %copy-start.41 = (f32[4,1,256]{2,1,0:T(1,128)S(1)}, f32[4,1,256]{2,1,0:T(1,128)}, u32[]{:S(2)}) copy-start(f32[4,1,256]{2,1,0:T(1,128)} %copy-done.40) | copy-start | bytes 12292
  1613.4 179.8 %copy-start.53 = (f32[256]{0:T(256)S(1)}, f32[256]{0:T(256)}, u32[]{:S(2)}) copy-start(f32[256]{0:T(256)} %copy-done.52) | copy-start | bytes 3076
  1614.1 229.7 %reduce-scatter.13.cloned.1.call-start = ((), (), s32[]{:S(2)}) async-start(), calls=%async_computation.20 | async-start | bytes 2621440 | tf_op jit(solution)/shard_map/reduce_scatter | solution.py:425
  1616.7 272.3 %reduce-scatter.11.cloned.1.call-start = ((), (), s32[]{:S(2)}) async-start(), calls=%async_computation.19 | async-start | bytes 7864320 | tf_op jit(solution)/shard_map/reduce_scatter | solution.py:422
  1799.2 156.4 %reduce-scatter.15.cloned.1.call-start = ((), (), s32[]{:S(2)}) async-start(), calls=%async_computation.21 | async-start | bytes 81920 | tf_op jit(solution)/shard_map/reduce_scatter | solution.py:431
  1814.0 13.1 copy-start.14
  1814.0 13.1 copy-start.23
  1814.0 13.1 copy-start.26
  1814.0 13.1 copy-start.30
  1814.0 13.2 copy-start.33
  1814.0 13.2 copy-start.38
  1814.0 13.2 copy-start.43
  1814.0 13.2 copy-start.45
  1814.0 13.2 copy-start.50
  1828.1 189.7 %all-reduce.8.cloned.1.call-start = ((), (), s32[]{:S(2)}) async-start(), calls=%async_computation.23 | async-start | bytes 4194304 | tf_op jit(solution)/shard_map/psum | solution.py:438
  1889.1 596.2 %reduce-scatter.17.cloned.1.call-start = ((), (), s32[]{:S(2)}) async-start(), calls=%async_computation.22 | async-start | bytes 86507520 | tf_op jit(solution)/shard_map/reduce_scatter | solution.py:269
  1937.9 5.0 copy-start.47
  (50 other events, 134.5 us)
Sparse Core Ops, SparseCore 0:
  9.6 49.0 all-gather.9
  64.8 73.3 all-gather.13
  141.0 71.6 all-gather.11
  214.1 20.8 all-gather.15
  236.4 141.8 all-gather.19
  379.7 141.8 all-gather.17
  523.2 141.8 all-gather.21
  1613.4 86.9 reduce-scatter.6
  1705.1 88.0 reduce-scatter.8
  1796.1 31.1 reduce-scatter.12
  1830.6 58.3 reduce-scatter.10
  1891.9 19.4 reduce-scatter.14
  1915.4 102.3 all-reduce.7
  2020.5 464.6 reduce-scatter.16
where the time goes:
time: 2550 us; the launch traced here: 2540 us
  waiting for transfers between devices  967 us (38%)
  matrix products  825 us (32%)
  other arithmetic  430 us (17%)
  local copies, waits for them, and re-layouts  207 us (8%)
  blocking collectives  70 us (3%)
    reduce_scatter x1, waiting for transfers between devices, expert_backward_weights(): lax.psum_scatter(jnp.stack([jnp.einsum('erd,erf->fed', received, grad_gat...  462 us
    dot_general x16, matrix products, group_scores(): jnp.einsum('qhc,khc->hqk', query_rows, key_rows, preferred_element_type=j...  352 us
    eq x16, other arithmetic, bias_lookup(): buckets[None] == bucket_id  190 us
    sub x8, matrix products, one_group(): grad_scores = attention * (grad_weights - inner)  143 us
    reduce_sum x8, other arithmetic, bias_sums(): jnp.sum(jnp.where(buckets[None] == bucket_id, grad_scores, 0.0), axis=(1,...  113 us
    reduce_scatter x1, waiting for transfers between devices, shards(): lax.psum_scatter(grad_values_all.astype(jnp.bfloat16), 'expert', scatter_...  92.7 us
    reduce_scatter x1, waiting for transfers between devices, shards(): lax.psum_scatter(grad_keys_all.astype(jnp.bfloat16), 'expert', scatter_di...  83.7 us
    all_gather x1, waiting for transfers between devices, shards(): lax.all_gather(values_own, 'expert', axis=0, tiled=True)  67.9 us
  transfers between devices with their start and end apart: 18, of which 12 were waited for; matrix products, arithmetic and copies ran while one was open for 21% of the time, Pallas kernels for 0%

commit v1 on v0

v1 whole, which is shorter than its diff:
```python
import functools
import math

import jax
import jax.numpy as jnp
import numpy as np
from jax import lax
from jax.experimental import pallas as pl
from jax.experimental.pallas import tpu as pltpu
from jax.sharding import PartitionSpec as P

D = 1024
HEADS = 16
HEAD = 64
FF = 2816
EXPERTS = 32
TOP = 2
BUCKETS = 32
CAP = 18

epsilon = 1e-06
masked_score = -1e30
far_bounds = (12, 16, 23, 32, 46, 64, 91)
tile = 256
main_slots = 16
tail_slots = CAP - main_slots
log2e = math.log2(math.e)
score_scale = HEAD ** (-0.5)
mega = 1024 * 1024
part_sources = 32
spare = 128


MESH = pl.DeviceIdType.MESH


def flip(index, key):
    out, bit = index, 1
    while bit <= key:
        if key & bit:
            out = out + bit * (1 - 2 * ((index // bit) % 2))
        bit *= 2
    return out


class Spot:
    def __init__(self, groups, columns):
        self.groups, self.columns = groups, columns
        self.place = lax.axis_index("expert")
        self.lane = lax.axis_index("shard")
        self.half = columns // 2
        self.chip = self.lane // 2
        self.core = self.lane % 2
        self.partner = self.chip * 2 + 1 - self.core

    def across(self, step):
        return ((self.chip + step) % self.half) * 2 + self.core

    def behind(self, step):
        return ((self.chip + self.half - step) % self.half) * 2 + self.core

    def lane_at(self, step, other):
        chip = (self.chip + step) % self.half
        return chip * 2 + ((1 - self.core) if other else self.core)

    def meet(self):
        barrier = pltpu.get_barrier_semaphore()
        for key in range(1, self.groups):
            peer = (flip(self.place, key), self.lane)
            pl.semaphore_signal(barrier, inc=1, device_id=peer, device_id_type=MESH)
        for step in range(1, self.columns):
            peer = (self.place, (self.lane + step) % self.columns)
            pl.semaphore_signal(barrier, inc=1, device_id=peer, device_id_type=MESH)
        pl.semaphore_wait(barrier, self.groups + self.columns - 2)


def remote(source, target, send_sem, recv_sem, peer):
    return pltpu.make_async_remote_copy(
        src_ref=source,
        dst_ref=target,
        send_sem=send_sem,
        recv_sem=recv_sem,
        device_id=peer,
        device_id_type=MESH,
    )


def line_shape(groups):
    across = groups // 4
    return 4, across


class LineGather:
    def __init__(self, spot, own, full, local_sem, send_sems, recv_sems):
        self.spot, self.own, self.full = spot, own, full
        self.local_sem, self.send_sems, self.recv_sems = local_sem, send_sems, recv_sems
        self.long, self.wide = line_shape(spot.groups)
        self.z = spot.place // self.wide
        self.y = spot.place % self.wide

    @staticmethod
    def sems(groups):
        long, wide = line_shape(groups)
        return [
            pltpu.SemaphoreType.DMA(()),
            pltpu.SemaphoreType.DMA((2 * long - 1, wide + 1)),
            pltpu.SemaphoreType.DMA((groups,)),
        ]

    def copy(self, job, way, origin, source, target):
        return remote(
            source,
            self.full.at[origin],
            self.send_sems.at[job, way],
            self.recv_sems.at[origin],
            (target, self.spot.lane),
        )

    def each(self, job, origin, source, up, down, act):
        place, wide = self.spot.place, self.wide
        if up:

            @pl.when(self.z + 1 < self.long)
            def _():
                act(self.copy(job, 0, origin, source, place + wide))

        if down:

            @pl.when(self.z >= 1)
            def _():
                act(self.copy(job, 1, origin, source, place - wide))

        for step in range(1, wide):
            target = self.z * wide + (self.y + step) % wide
            act(self.copy(job, 1 + step, origin, source, target))

    def begin(self):
        place = self.spot.place
        self.each(0, place, self.own, True, True, lambda copy: copy.start())
        pltpu.make_async_copy(self.own, self.full.at[place], self.local_sem).start()

    def arrive(self, origin):
        self.copy(0, 0, origin, self.own, self.spot.place).wait_recv()

    def hop(self, k):
        place, wide = self.spot.place, self.wide

        @pl.when(self.z >= k)
        def _():
            origin = place - k * wide
            self.arrive(origin)
            self.each(k, origin, self.full.at[origin], True, False, lambda copy: copy.start())

        @pl.when(self.z + k < self.long)
        def _():
            origin = place + k * wide
            self.arrive(origin)
            job = self.long - 1 + k
            self.each(job, origin, self.full.at[origin], False, True, lambda copy: copy.start())

    def finish(self):
        place, wide = self.spot.place, self.wide
        for row in range(self.long):
            for step in range(1, wide):
                self.arrive(row * wide + (self.y + step) % wide)
        stop = lambda copy: copy.wait_send()
        self.each(0, place, self.own, True, True, stop)
        for k in range(1, self.long):

            @pl.when(self.z >= k)
            def _():
                origin = place - k * wide
                self.each(k, origin, self.full.at[origin], True, False, stop)

            @pl.when(self.z + k < self.long)
            def _():
                origin = place + k * wide
                job = self.long - 1 + k
                self.each(job, origin, self.full.at[origin], False, True, stop)

        pltpu.make_async_copy(self.own, self.full.at[place], self.local_sem).wait()


class ColumnGather:
    def __init__(self, spot, own, full, local_sem, across_send, across_recv, core_send, core_recv):
        self.spot, self.own, self.full = spot, own, full
        self.local_sem = local_sem
        self.across_send, self.across_recv = across_send, across_recv
        self.core_send, self.core_recv = core_send, core_recv

    @staticmethod
    def sems(columns):
        return [pltpu.SemaphoreType.DMA(())] + [pltpu.SemaphoreType.DMA((columns // 2,))] * 4

    def across_copy(self, step):
        spot = self.spot
        return remote(
            self.own,
            self.full.at[spot.lane],
            self.across_send.at[step],
            self.across_recv.at[step],
            (spot.place, spot.across(step)),
        )

    def core_copy(self, step):
        spot = self.spot
        source = self.own if step == 0 else self.full.at[spot.behind(step)]
        target = spot.lane if step == 0 else spot.behind(step)
        return remote(
            source,
            self.full.at[target],
            self.core_send.at[step],
            self.core_recv.at[step],
            (spot.place, spot.partner),
        )

    def begin(self):
        for step in range(1, self.spot.half):
            self.across_copy(step).start()
        self.core_copy(0).start()
        pltpu.make_async_copy(self.own, self.full.at[self.spot.lane], self.local_sem).start()

    def forward(self):
        for step in range(1, self.spot.half):
            self.across_copy(step).wait_recv()
            self.core_copy(step).start()

    def finish(self):
        for step in range(self.spot.half):
            self.core_copy(step).wait_recv()
        for step in range(self.spot.half):
            self.core_copy(step).wait_send()
        for step in range(1, self.spot.half):
            self.across_copy(step).wait_send()
        pltpu.make_async_copy(self.own, self.full.at[self.spot.lane], self.local_sem).wait()


def comm_params(which, limit=16):
    return pltpu.CompilerParams(
        collective_id=which, has_side_effects=True, vmem_limit_bytes=limit * mega
    )


anywhere = pl.BlockSpec(memory_space=pl.ANY)


def entry_kernel(groups, columns, count, *refs):
    tokens, refs = refs[0], refs[1:]
    owns, refs = refs[:count], refs[count:]
    tokens_all, refs = refs[0], refs[1:]
    fulls, sems = refs[:count], refs[count:]
    spot = Spot(groups, columns)
    line = LineGather(spot, tokens, tokens_all, *sems[:3])
    across = [
        ColumnGather(spot, owns[i], fulls[i], *sems[3 + 5 * i : 8 + 5 * i]) for i in range(count)
    ]
    spot.meet()
    line.begin()
    for gather in across:
        gather.begin()
    for k in range(1, 4):
        line.hop(k)
        if k <= count:
            across[k - 1].forward()
    for gather in across[3:]:
        gather.forward()
    for gather in across:
        gather.finish()
    line.finish()


def entry_gather(tokens, owns, groups, columns):
    count = len(owns)
    sems = LineGather.sems(groups) + ColumnGather.sems(columns) * count
    shapes = [jax.ShapeDtypeStruct((groups,) + tokens.shape, tokens.dtype)] + [
        jax.ShapeDtypeStruct((columns,) + own.shape, own.dtype) for own in owns
    ]
    return pl.pallas_call(
        functools.partial(entry_kernel, groups, columns, count),
        out_shape=shapes,
        in_specs=[anywhere] * (1 + count),
        out_specs=[anywhere] * (1 + count),
        scratch_shapes=sems,
        compiler_params=comm_params(1),
        name="entry_gather",
    )(tokens, *owns)


class Dispatch:
    def __init__(self, spot, rows, full, sems):
        self.spot, self.rows, self.full = spot, rows, full
        self.local, self.send, self.recv = sems[:3]
        self.across_send, self.across_recv, self.core_send, self.core_recv = sems[3:]

    @staticmethod
    def sems(groups, columns):
        return (
            [pltpu.SemaphoreType.DMA(())]
            + [pltpu.SemaphoreType.DMA((groups,))] * 2
            + [pltpu.SemaphoreType.DMA((groups, columns // 2))] * 4
        )

    def own(self):
        spot = self.spot
        return pltpu.make_async_copy(
            self.rows.at[spot.place], self.full.at[spot.lane, spot.place], self.local
        )

    def swap(self, key):
        spot = self.spot
        peer = flip(spot.place, key)
        return remote(
            self.rows.at[peer],
            self.full.at[spot.lane, spot.place],
            self.send.at[key],
            self.recv.at[key],
            (peer, spot.lane),
        )

    def across(self, key, step):
        spot = self.spot
        block = self.full.at[spot.lane, flip(spot.place, key)]
        return remote(
            block,
            block,
            self.across_send.at[key, step],
            self.across_recv.at[key, step],
            (spot.place, spot.across(step)),
        )

    def core(self, key, step):
        spot = self.spot
        block = self.full.at[spot.behind(step), flip(spot.place, key)]
        return remote(
            block,
            block,
            self.core_send.at[key, step],
            self.core_recv.at[key, step],
            (spot.place, spot.partner),
        )

    def begin(self):
        self.own().start()
        for key in range(1, self.spot.groups):
            self.swap(key).start()

    def pass_on(self, key):
        for step in range(1, self.spot.half):
            self.across(key, step).wait_recv()
            self.core(key, step).start()

    def advance(self, key):
        if key == 0:
            self.own().wait()
        else:
            self.swap(key).wait_recv()
        for step in range(1, self.spot.half):
            self.across(key, step).start()
        self.core(key, 0).start()
        if key > 0:
            self.pass_on(key - 1)

    def finish(self):
        groups, half = self.spot.groups, self.spot.half
        self.pass_on(groups - 1)
        for key in range(groups):
            for step in range(half):
                self.core(key, step).wait_recv()
        for key in range(groups):
            if key > 0:
                self.swap(key).wait_send()
            for step in range(1, half):
                self.across(key, step).wait_send()
            for step in range(half):
                self.core(key, step).wait_send()


def dispatch_kernel(groups, columns, rows, full, *sems):
    spot = Spot(groups, columns)
    job = Dispatch(spot, rows, full, sems)
    spot.meet()
    job.begin()
    for key in range(groups):
        job.advance(key)
    job.finish()


def dispatch(rows, columns, which):
    groups = rows.shape[0]
    return pl.pallas_call(
        functools.partial(dispatch_kernel, groups, columns),
        out_shape=jax.ShapeDtypeStruct((columns,) + rows.shape, rows.dtype),
        in_specs=[anywhere],
        out_specs=anywhere,
        scratch_shapes=Dispatch.sems(groups, columns),
        compiler_params=comm_params(which),
        name="dispatch_rows",
    )(rows)


class Exchange:
    def __init__(self, spot, blocks, thirds, local, send, recv):
        self.spot, self.blocks, self.thirds = spot, blocks, range(thirds)
        self.local, self.send, self.recv = local, send, recv

    @staticmethod
    def sems(groups, thirds):
        return [pltpu.SemaphoreType.DMA((thirds,))] + [
            pltpu.SemaphoreType.DMA((groups, thirds))
        ] * 2

    def copy(self, key, third):
        spot = self.spot
        peer = flip(spot.place, key)
        source, target = self.blocks(peer, third)
        if key == 0:
            return pltpu.make_async_copy(source, target, self.local.at[third])
        return remote(
            source,
            target,
            self.send.at[key, third],
            self.recv.at[key, third],
            (peer, spot.lane),
        )

    def start(self, key):
        for third in self.thirds:
            self.copy(key, third).start()

    def begin(self):
        for key in range(self.spot.groups):
            self.start(key)

    def arrive(self):
        for key in range(self.spot.groups):
            for third in self.thirds:
                copy = self.copy(key, third)
                copy.wait() if key == 0 else copy.wait_recv()

    def finish(self):
        for key in range(1, self.spot.groups):
            for third in self.thirds:
                self.copy(key, third).wait_send()


class ColumnSum:
    def __init__(self, spot, chunks, order, part, bufs, sems):
        self.spot, self.chunks, self.order, self.part = spot, chunks, order, part
        self.pair_in, self.mine, self.across_out, self.across_in = bufs
        self.local, self.pair_send, self.pair_recv, self.across_send, self.across_recv = sems

    @staticmethod
    def scratch(columns, chunks, block):
        half = columns // 2
        return [pltpu.VMEM((half, chunks) + block, jnp.bfloat16)] * 4 + [
            pltpu.SemaphoreType.DMA((half, chunks))
        ] * 5

    def pair_copy(self, step, k):
        spot = self.spot
        return remote(
            self.part.at[spot.lane_at(step, True), self.order(k)],
            self.pair_in.at[step, k],
            self.pair_send.at[step, k],
            self.pair_recv.at[step, k],
            (spot.place, spot.partner),
        )

    def mine_copy(self, step, k):
        return pltpu.make_async_copy(
            self.part.at[self.spot.lane_at(step, False), self.order(k)],
            self.mine.at[step, k],
            self.local.at[step, k],
        )

    def across_copy(self, step, k):
        spot = self.spot
        return remote(
            self.across_out.at[step, k],
            self.across_in.at[step, k],
            self.across_send.at[step, k],
            self.across_recv.at[step, k],
            (spot.place, spot.across(step)),
        )

    def begin(self):
        half = self.spot.half
        for k in range(self.chunks):
            for step in list(range(1, half)) + [0]:
                self.pair_copy(step, k).start()
                self.mine_copy(step, k).start()

    def pair_sum(self, step, k):
        self.pair_copy(step, k).wait_recv()
        self.mine_copy(step, k).wait()
        return self.mine[step, k].astype(jnp.float32) + self.pair_in[step, k].astype(jnp.float32)

    def middle(self, k):
        for step in range(1, self.spot.half):
            self.across_out[step, k] = self.pair_sum(step, k).astype(jnp.bfloat16)
            self.across_copy(step, k).start()

    def last(self, k):
        total = self.pair_sum(0, k)
        for step in range(1, self.spot.half):
            self.across_copy(step, k).wait_recv()
            total = total + self.across_in[step, k].astype(jnp.float32)
        return total.astype(jnp.bfloat16)

    def finish(self):
        for k in range(self.chunks):
            for step in range(self.spot.half):
                self.pair_copy(step, k).wait_send()
                if step:
                    self.across_copy(step, k).wait_send()


class Collect:
    def __init__(self, spot, part, out, scratch):
        self.spot, self.total = spot, scratch[9]
        self.sums = ColumnSum(
            spot, spot.groups, lambda k: flip(spot.place, k), part, scratch[:4], scratch[4:9]
        )
        self.out = out
        self.local, self.send, self.recv = scratch[10:]

    @staticmethod
    def scratch(columns, groups, block):
        return (
            ColumnSum.scratch(columns, groups, block)
            + [pltpu.VMEM((groups,) + block, jnp.bfloat16)]
            + [pltpu.SemaphoreType.DMA(())]
            + [pltpu.SemaphoreType.DMA((groups,))] * 2
        )

    def copy(self, key):
        spot = self.spot
        target = self.out.at[spot.place]
        if key == 0:
            return pltpu.make_async_copy(self.total.at[0], target, self.local)
        peer = flip(spot.place, key)
        return remote(
            self.total.at[key], target, self.send.at[key], self.recv.at[key], (peer, spot.lane)
        )

    def begin(self):
        self.sums.begin()

    def middle(self, key):
        self.sums.middle(key)

    def last(self, key):
        self.total[key] = self.sums.last(key)
        self.copy(key).start()

    def finish(self):
        for key in range(1, self.spot.groups):
            self.copy(key).wait_recv()
        for key in range(1, self.spot.groups):
            self.copy(key).wait_send()
        self.copy(0).wait()
        self.sums.finish()


def collect_kernel(groups, columns, part, out, *scratch):
    spot = Spot(groups, columns)
    job = Collect(spot, part, out, scratch)
    spot.meet()
    job.begin()
    ahead = 2
    for key in range(ahead):
        job.middle(key)
    for key in range(groups):
        if key + ahead < groups:
            job.middle(key + ahead)
        job.last(key)
    job.finish()


def collect(part, which):
    columns, groups = part.shape[:2]
    block = part.shape[2:]
    return pl.pallas_call(
        functools.partial(collect_kernel, groups, columns),
        out_shape=jax.ShapeDtypeStruct((groups,) + block, part.dtype),
        in_specs=[anywhere],
        out_specs=anywhere,
        scratch_shapes=Collect.scratch(columns, groups, block),
        compiler_params=comm_params(which, 56),
        name="collect_rows",
    )(part)


def lanes_at(place, width):
    return pl.ds(pl.multiple_of(place * width, 128), width)


def mixed_kernel(groups, columns, mixed, attended, *sems):
    spot = Spot(groups, columns)
    width = mixed.shape[2]

    def blocks(at, third):
        if width % 128:
            return mixed.at[at], attended.at[spot.place]
        return mixed.at[at], attended.at[:, lanes_at(spot.place, width)]

    job = Exchange(spot, blocks, 1, *sems)
    spot.meet()
    job.begin()
    job.arrive()
    job.finish()


def exchange_mixed(mixed, columns, which):
    groups, rows, width = mixed.shape
    shape = mixed.shape if width % 128 else (rows, groups * width)
    out = pl.pallas_call(
        functools.partial(mixed_kernel, groups, columns),
        out_shape=jax.ShapeDtypeStruct(shape, mixed.dtype),
        in_specs=[anywhere],
        out_specs=anywhere,
        scratch_shapes=Exchange.sems(groups, 1),
        compiler_params=comm_params(which),
        name="exchange_mixed",
    )(mixed)
    if width % 128:
        out = jnp.transpose(out, (1, 0, 2)).reshape(rows, groups * width)
    return out


def grad_mixed_kernel(groups, columns, chunks, grads, part, out, part_out, *scratch):
    spot = Spot(groups, columns)
    width = out.shape[2]

    def blocks(at, third):
        if width % 128:
            return grads.at[at], out.at[spot.place]
        return grads.at[:, lanes_at(at, width)], out.at[spot.place]

    sums = ColumnSum(spot, chunks, lambda k: k, part, scratch[:4], scratch[4:9])
    total, total_sem = scratch[9:11]
    job = Exchange(spot, blocks, 1, *scratch[11:])
    spot.meet()
    job.begin()
    sums.begin()
    for k in range(chunks):
        sums.middle(k)
    stores = [pltpu.make_async_copy(total.at[k], part_out.at[k], total_sem.at[k]) for k in range(chunks)]
    for k in range(chunks):
        total[k] = sums.last(k)
        stores[k].start()
    job.arrive()
    job.finish()
    sums.finish()
    for store in stores:
        store.wait()


def exchange_grad_mixed(grads, part, groups, which):
    rows = grads.shape[0]
    width = grads.shape[1] // groups
    if width % 128:
        grads = jnp.transpose(grads.reshape(rows, groups, width), (1, 0, 2))
    columns, chunks = part.shape[:2]
    block = part.shape[2:]
    return pl.pallas_call(
        functools.partial(grad_mixed_kernel, groups, columns, chunks),
        out_shape=(
            jax.ShapeDtypeStruct((groups, rows, width), grads.dtype),
            jax.ShapeDtypeStruct((chunks,) + block, part.dtype),
        ),
        in_specs=[anywhere, anywhere],
        out_specs=(anywhere, anywhere),
        scratch_shapes=ColumnSum.scratch(columns, chunks, block)
        + [pltpu.VMEM((chunks,) + block, part.dtype), pltpu.SemaphoreType.DMA((chunks,))]
        + Exchange.sems(groups, 1),
        compiler_params=comm_params(which, 32),
        name="exchange_grad_mixed",
    )(grads, part)


class Tail:
    def __init__(self, spot, chunks, refs, scratch):
        grads, part, piece, weight, grads_out, sum_all, piece_all, weight_all = refs
        groups = spot.groups
        width = grads.shape[2] // 3
        thirds = 3 if width % 128 == 0 else 1

        def blocks(at, third):
            if thirds == 1:
                return grads.at[at], grads_out.at[spot.place]
            columns_to = pl.ds(pl.multiple_of(third * D + spot.place * width, 128), width)
            return grads.at[at, :, pl.ds(third * width, width)], grads_out.at[:, columns_to]

        self.chunks = chunks
        self.sums = ColumnSum(spot, chunks, lambda k: k, part, scratch[:4], scratch[4:9])
        self.own_sum = scratch[9]
        self.swap = Exchange(spot, blocks, thirds, *scratch[10:13])
        self.line = LineGather(spot, self.own_sum, sum_all, *scratch[13:16])
        self.side = LineGather(spot, piece, piece_all, *scratch[16:19])
        self.column = ColumnGather(spot, weight, weight_all, *scratch[19:24])

    @staticmethod
    def scratch(columns, groups, chunks, block, thirds):
        return (
            ColumnSum.scratch(columns, chunks, block)
            + [pltpu.VMEM((chunks,) + block, jnp.bfloat16)]
            + Exchange.sems(groups, thirds)
            + LineGather.sems(groups) * 2
            + ColumnGather.sems(columns)
        )

    def begin(self):
        self.sums.begin()
        self.side.begin()
        self.swap.begin()
        for k in range(self.chunks):
            self.sums.middle(k)
        self.column.begin()

    def gather(self):
        for k in range(self.chunks):
            self.own_sum[k] = self.sums.last(k)
        self.line.begin()
        self.side.hop(1)

    def hop(self, k):
        self.line.hop(k)
        if k + 1 < 4:
            self.side.hop(k + 1)

    def finish(self):
        self.column.forward()
        self.swap.arrive()
        self.side.finish()
        self.line.finish()
        self.column.finish()
        self.swap.finish()
        self.sums.finish()


def unpack_kernel(width, packed, out):
    for group in range(packed.shape[0]):
        out[:, group * width : (group + 1) * width] = packed[group].astype(jnp.float32)


def unpack_columns(packed, width):
    groups, rows = packed.shape[:2]
    if width % 128:
        blocks = packed[:, :, : 3 * width].reshape(groups, rows, 3, width).astype(jnp.float32)
        return jnp.transpose(blocks, (1, 2, 0, 3)).reshape(rows, 3 * groups * width)
    return pl.pallas_call(
        functools.partial(unpack_kernel, width),
        grid=(3,),
        out_shape=jax.ShapeDtypeStruct((rows, 3 * groups * width), jnp.float32),
        in_specs=[pl.BlockSpec((groups, rows, width), lambda t: (0, 0, t))],
        out_specs=pl.BlockSpec((rows, groups * width), lambda t: (0, t)),
        name="unpack_columns",
    )(packed)


def rms_norm(features, scales):
    factor = lax.rsqrt(jnp.mean(features * features, axis=-1, keepdims=True) + epsilon)
    return features * factor * scales


def buckets_of(offsets):
    distance = np.abs(offsets)
    beyond = 8 + np.sum(distance[..., None] >= np.array(far_bounds), axis=-1)
    return np.where(distance < 8, distance, beyond) + 16 * (offsets > 0)


def skew_buckets():
    lanes = np.arange(2 * tile)
    from_query = np.where(lanes < tile, -lanes, 2 * tile - lanes)
    return np.concatenate([buckets_of(near * tile + from_query) for near in (-1, 0, 1)])


def lane_row_mask(head, width, rows):
    lanes = lax.broadcasted_iota(jnp.int32, (rows, width), 1)
    return (lanes >= head * HEAD) & (lanes < (head + 1) * HEAD)


def fold_rows(block, op):
    return op(block.reshape(block.shape[0] // 8, 8, block.shape[1]), axis=0)


def nt_dot(left, right):
    return lax.dot_general(left, right, (((1,), (1,)), ((), ())), preferred_element_type=jnp.float32)


def tn_dot(left, right):
    return lax.dot_general(left, right, (((0,), (0,)), ((), ())), preferred_element_type=jnp.float32)


def nn_dot(left, right):
    return jnp.dot(left, right, preferred_element_type=jnp.float32)


def build_bias(base_ref, far_ref, bias_sc, heads_here):
    for head in range(heads_here):
        for near in range(3):
            row = base_ref[pl.ds(head * 3 + near, 1), :]
            wide = jnp.broadcast_to(row, (tile, 2 * tile))
            skewed = pltpu.roll(wide, 0, 1, stride=1, stride_axis=0)
            bias_sc[head, near] = skewed[:, :tile]
        bias_sc[head, 3] = jnp.full((tile, tile), far_ref[head, 1], jnp.float32)


def unskew_sum(wide):
    lanes = wide.shape[1]
    half = wide.shape[0] // 2
    while half >= 8:
        wide = wide[:half] + pltpu.roll(wide[half:], lanes - half, 1)
        half //= 2
    total = wide[0:1]
    for row in range(1, 8):
        total = total + pltpu.roll(wide[row : row + 1], lanes - row, 1)
    return total


def rows_at(index):
    return pl.ds(pl.multiple_of(index * tile, tile), tile)


def visible_tile(key_tile, query_tile, prefix_length):
    key_pos = key_tile * tile + lax.broadcasted_iota(jnp.int32, (tile, tile), 0)
    query_pos = query_tile * tile + lax.broadcasted_iota(jnp.int32, (tile, tile), 1)
    return (key_pos <= query_pos) | (key_pos < prefix_length)


def attend_forward_kernel(
    heads_here,
    groups,
    columns,
    prefix_ref,
    far_ref,
    base_ref,
    qkv_ref,
    rows_ref,
    mixed_ref,
    totals_ref,
    full_ref,
    bias_sc,
    score_sc,
    value_sc,
    *sems,
):
    width = heads_here * HEAD
    query_tile = pl.program_id(0)
    tiles = qkv_ref.shape[0] // tile
    spot = Spot(groups, columns)
    job = Dispatch(spot, rows_ref, full_ref, sems)

    @pl.when(query_tile == 0)
    def _():
        spot.meet()
        job.begin()

    prefix_length = prefix_ref[0]
    heads = range(heads_here)

    @pl.when(query_tile == 0)
    def _():
        build_bias(base_ref, far_ref, bias_sc, heads_here)
        for key_tile in range(value_sc.shape[1] // tile):
            rows = pl.ds(key_tile * tile, tile)
            values = qkv_ref[rows, 2 * width : 3 * width].astype(jnp.float32)
            value_sc[:, rows] = jnp.transpose(values).astype(jnp.bfloat16)

    queries = qkv_ref[rows_at(query_tile), :width]
    head_queries = [
        jnp.where(lane_row_mask(head, width, tile), queries, jnp.zeros_like(queries)) for head in heads
    ]

    def score_tiles(key_tile, tops, finish):
        keys = qkv_ref[rows_at(key_tile), width : 2 * width]
        out = []
        for head in heads:
            scores = finish(head, nt_dot(keys, head_queries[head]) * (score_scale * log2e))
            score_sc[head, rows_at(key_tile), :] = scores
            out.append(jnp.maximum(tops[head], fold_rows(scores, jnp.max)))
        return tuple(out)

    def far_body(key_tile, tops):
        return score_tiles(key_tile, tops, lambda head, raw: raw + far_ref[head, 0])

    def near_body(key_tile, tops):
        return score_tiles(key_tile, tops, lambda head, raw: raw + bias_sc[head, 0])

    def tail_body(key_tile, tops):
        shown = visible_tile(key_tile, query_tile, prefix_length)
        which = 1 + jnp.minimum(key_tile - query_tile, 2)
        return score_tiles(
            key_tile, tops, lambda head, raw: jnp.where(shown, raw + bias_sc[head, which], masked_score)
        )

    tile_count = jnp.maximum(query_tile + 1, tiles // 2)
    near_start = jnp.maximum(query_tile - 1, 0)
    tops = tuple(jnp.full((8, tile), masked_score, jnp.float32) for _ in heads)
    tops = lax.fori_loop(0, near_start, far_body, tops)
    tops = lax.fori_loop(near_start, query_tile, near_body, tops)
    tops = lax.fori_loop(query_tile, tile_count, tail_body, tops)
    tops = [jnp.max(top, axis=0, keepdims=True) for top in tops]

    def mix_body(key_tile, carry):
        sums, mixes = carry
        new_sums, new_mixes = [], []
        for head in heads:
            expos = jnp.exp2(score_sc[head, rows_at(key_tile), :] - tops[head])
            new_sums.append(sums[head] + fold_rows(expos, jnp.sum))
            values = value_sc[head * HEAD : (head + 1) * HEAD, rows_at(key_tile)]
            new_mixes.append(mixes[head] + nn_dot(values, expos.astype(jnp.bfloat16)))
        return (tuple(new_sums), tuple(new_mixes))

    sums, mixes = lax.fori_loop(
        0,
        tile_count,
        mix_body,
        (
            tuple(jnp.zeros((8, tile), jnp.float32) for _ in heads),
            tuple(jnp.zeros((HEAD, tile), jnp.float32) for _ in heads),
        ),
    )
    parts = []
    for head in heads:
        total = jnp.sum(sums[head], axis=0, keepdims=True)
        parts.append(mixes[head] / total)
        totals_ref[0, pl.ds(head, 1), :] = tops[head] + jnp.log2(total)
    mixed_ref[...] = jnp.transpose(jnp.concatenate(parts, axis=0)).astype(jnp.bfloat16)

    for key in range(groups):

        @pl.when(query_tile == key * tiles // groups)
        def _():
            job.advance(key)

    @pl.when(query_tile == tiles - 1)
    def _():
        job.finish()


def attend_forward(prefix, far_bias, base_bias, qkv, rows, columns):
    length = qkv.shape[0]
    groups = rows.shape[0]
    width = qkv.shape[1] // 3
    heads_here = width // HEAD
    tiles = length // tile
    return pl.pallas_call(
        functools.partial(attend_forward_kernel, heads_here, groups, columns),
        grid=(tiles,),
        out_shape=(
            jax.ShapeDtypeStruct((length, width), jnp.bfloat16),
            jax.ShapeDtypeStruct((tiles, heads_here, tile), jnp.float32),
            jax.ShapeDtypeStruct((columns,) + rows.shape, rows.dtype),
        ),
        in_specs=[
            pl.BlockSpec(memory_space=pltpu.SMEM),
            pl.BlockSpec(memory_space=pltpu.SMEM),
            pl.BlockSpec(base_bias.shape, lambda i: (0, 0)),
            pl.BlockSpec(qkv.shape, lambda i: (0, 0)),
            anywhere,
        ],
        out_specs=(
            pl.BlockSpec((tile, width), lambda i: (i, 0)),
            pl.BlockSpec((1, heads_here, tile), lambda i: (i, 0, 0)),
            anywhere,
        ),
        scratch_shapes=[
            pltpu.VMEM((heads_here, 4, tile, tile), jnp.float32),
            pltpu.VMEM((heads_here, length, tile), jnp.float32),
            pltpu.VMEM((width, length), jnp.bfloat16),
        ]
        + Dispatch.sems(groups, columns),
        compiler_params=comm_params(5, 40),
        cost_estimate=pl.CostEstimate(
            flops=40 * length * length * width, transcendentals=length * length * heads_here,
            bytes_accessed=8 * length * width,
        ),
        name="attend_forward",
    )(prefix, far_bias, base_bias, qkv, rows)


def attend_backward_kernel(
    heads_here,
    groups,
    columns,
    prefix_ref,
    far_ref,
    base_ref,
    qkv_ref,
    mixed_ref,
    grad_ref,
    totals_ref,
    part_ref,
    sums_ref,
    out_ref,
    near_ref,
    side_ref,
    result_ref,
    piece_ref,
    bias_sc,
    key_sc,
    grad_key_sc,
    grad_value_sc,
    near_sc,
    *scratch,
):
    width = heads_here * HEAD
    query_tile = pl.program_id(0)
    tiles = qkv_ref.shape[0] // tile
    spot = Spot(groups, columns)
    pieces = scratch[0]
    swap = Exchange(
        spot, lambda at, third: (sums_ref.at[at], pieces.at[spot.place]), 1, *scratch[1:4]
    )
    job = Collect(spot, part_ref, result_ref, scratch[4:])

    @pl.when(query_tile == 0)
    def _():
        spot.meet()
        job.begin()
        swap.begin()

    prefix_length = prefix_ref[0]
    heads = range(heads_here)

    @pl.when(query_tile == 0)
    def _():
        build_bias(base_ref, far_ref, bias_sc, heads_here)
        for key_tile in range(key_sc.shape[1] // tile):
            rows = pl.ds(key_tile * tile, tile)
            keys = qkv_ref[rows, width : 2 * width].astype(jnp.float32)
            key_sc[:, rows] = jnp.transpose(keys).astype(jnp.bfloat16)
        grad_key_sc[...] = jnp.zeros_like(grad_key_sc)
        grad_value_sc[...] = jnp.zeros_like(grad_value_sc)
        near_sc[...] = jnp.zeros_like(near_sc)
        side_ref[...] = jnp.zeros_like(side_ref)

    queries = qkv_ref[rows_at(query_tile), :width]
    grads = grad_ref[rows_at(query_tile), :]
    products = grads.astype(jnp.float32) * mixed_ref[rows_at(query_tile), :].astype(jnp.float32)
    head_queries, head_grads, inners, totals = [], [], [], []
    for head in heads:
        mask = lane_row_mask(head, width, tile)
        head_queries.append(jnp.where(mask, queries, jnp.zeros_like(queries)))
        head_grads.append(jnp.where(mask, grads, jnp.zeros_like(grads)))
        ones = jnp.where(lane_row_mask(head, width, 8), 1.0, 0.0)
        inner = lax.dot_general(
            ones,
            products,
            (((1,), (1,)), ((), ())),
            precision=lax.Precision.HIGHEST,
            preferred_element_type=jnp.float32,
        )
        inners.append(inner[0:1, :])
        totals.append(totals_ref[0, pl.ds(head, 1), :])

    def step(key_tile, carry, finish, keep):
        sides, grad_queries = carry
        keys = qkv_ref[rows_at(key_tile), width : 2 * width]
        values = qkv_ref[rows_at(key_tile), 2 * width : 3 * width]
        new_sides, new_queries = [], []
        key_part, value_part = None, None
        for head in heads:
            raw = nt_dot(keys, head_queries[head]) * (score_scale * log2e)
            attention = jnp.exp2(finish(head, raw))
            grad_weights = nt_dot(values, head_grads[head])
            grad_scores = attention * (grad_weights - inners[head])
            new_sides.append(keep(head, grad_scores, sides[head]))
            low_scores = grad_scores.astype(jnp.bfloat16)
            keys_across = key_sc[head * HEAD : (head + 1) * HEAD, rows_at(key_tile)]
            new_queries.append(grad_queries[head] + nn_dot(keys_across, low_scores))
            value_one = nn_dot(attention.astype(jnp.bfloat16), head_grads[head])
            key_one = nn_dot(low_scores, head_queries[head])
            value_part = value_one if value_part is None else value_part + value_one
            key_part = key_one if key_part is None else key_part + key_one
        grad_key_sc[rows_at(key_tile), :] += key_part
        grad_value_sc[rows_at(key_tile), :] += value_part
        return (tuple(new_sides), tuple(new_queries))

    def add_side(head, grad_scores, side):
        return side + fold_rows(grad_scores, jnp.sum)

    def far_body(key_tile, carry):
        return step(
            key_tile, carry, lambda head, raw: raw + (far_ref[head, 0] - totals[head]), add_side
        )

    def near_body(key_tile, carry):
        def keep(head, grad_scores, side):
            near_sc[head, 0] += grad_scores
            return side

        return step(
            key_tile, carry, lambda head, raw: raw + bias_sc[head, 0] - totals[head], keep
        )

    def tail_body(key_tile, carry):
        shown = visible_tile(key_tile, query_tile, prefix_length)
        which = 1 + jnp.minimum(key_tile - query_tile, 2)

        def keep(head, grad_scores, side):
            near_sc[head, which] += grad_scores
            return side

        return step(
            key_tile,
            carry,
            lambda head, raw: jnp.where(
                shown, raw + bias_sc[head, which] - totals[head], masked_score
            ),
            keep,
        )

    tile_count = jnp.maximum(query_tile + 1, tiles // 2)
    near_start = jnp.maximum(query_tile - 1, 0)
    carry = (
        tuple(jnp.zeros((8, tile), jnp.float32) for _ in heads),
        tuple(jnp.zeros((HEAD, tile), jnp.float32) for _ in heads),
    )
    carry = lax.fori_loop(0, near_start, far_body, carry)
    carry = lax.fori_loop(near_start, query_tile, near_body, carry)
    carry = lax.fori_loop(query_tile, tile_count, tail_body, carry)
    sides, grad_queries = carry
    for head in heads:
        side_ref[head, 0] += sides[head]
    across = jnp.concatenate(grad_queries, axis=0) * score_scale
    out_ref[rows_at(query_tile), :width] = jnp.transpose(across).astype(jnp.bfloat16)

    @pl.when(query_tile == tiles - 1)
    def _():
        out_ref[:, width : 2 * width] = (grad_key_sc[...] * score_scale).astype(jnp.bfloat16)
        out_ref[:, 2 * width : 3 * width] = grad_value_sc[...].astype(jnp.bfloat16)
        for head in heads:
            side_ref[head, 1] = fold_rows(near_sc[head, 3], jnp.sum)
            for near in range(3):
                wide = jnp.concatenate(
                    [near_sc[head, near], jnp.zeros((tile, tile), jnp.float32)], axis=1
                )
                near_ref[pl.ds(head * 3 + near, 1), :] = unskew_sum(wide)

    for step in range(tiles):
        middles = [key for key in range(groups) if key * 2 // groups == step]
        lasts = [key for key in range(groups) if min(tiles - 1, 2 + key * 3 // 4) == step]

        @pl.when(query_tile == step)
        def _():
            for key in middles:
                job.middle(key)
            for key in lasts:
                job.last(key)

    @pl.when(query_tile == tiles - 1)
    def _():
        swap.arrive()
        piece_ref[...] = jnp.sum(pieces[...].astype(jnp.float32), axis=0).astype(jnp.bfloat16)
        job.finish()
        swap.finish()


def attend_backward(
    prefix, far_bias, base_bias, qkv, mixed, grad_mixed, totals, part, sums, columns
):
    length = qkv.shape[0]
    groups, piece_rows, piece_width = sums.shape
    block = part.shape[2:]
    width = qkv.shape[1] // 3
    heads_here = width // HEAD
    tiles = length // tile
    whole = lambda i: (0, 0)
    return pl.pallas_call(
        functools.partial(attend_backward_kernel, heads_here, groups, columns),
        grid=(tiles,),
        out_shape=(
            jax.ShapeDtypeStruct((length, 3 * width), jnp.bfloat16),
            jax.ShapeDtypeStruct((heads_here * 3, 2 * tile), jnp.float32),
            jax.ShapeDtypeStruct((heads_here, 2, 8, tile), jnp.float32),
            jax.ShapeDtypeStruct((groups,) + block, jnp.bfloat16),
            jax.ShapeDtypeStruct((piece_rows, piece_width), jnp.bfloat16),
        ),
        in_specs=[
            pl.BlockSpec(memory_space=pltpu.SMEM),
            pl.BlockSpec(memory_space=pltpu.SMEM),
            pl.BlockSpec(base_bias.shape, whole),
            pl.BlockSpec(qkv.shape, whole),
            pl.BlockSpec(mixed.shape, whole),
            pl.BlockSpec(mixed.shape, whole),
            pl.BlockSpec((1, heads_here, tile), lambda i: (i, 0, 0)),
            anywhere,
            anywhere,
        ],
        out_specs=(
            pl.BlockSpec((length, 3 * width), whole),
            pl.BlockSpec((heads_here * 3, 2 * tile), whole),
            pl.BlockSpec((heads_here, 2, 8, tile), lambda i: (0, 0, 0, 0)),
            anywhere,
            pl.BlockSpec((piece_rows, piece_width), whole),
        ),
        scratch_shapes=[
            pltpu.VMEM((heads_here, 4, tile, tile), jnp.float32),
            pltpu.VMEM((width, length), jnp.bfloat16),
            pltpu.VMEM((length, width), jnp.float32),
            pltpu.VMEM((length, width), jnp.float32),
            pltpu.VMEM((heads_here, 4, tile, tile), jnp.float32),
            pltpu.VMEM(sums.shape, jnp.bfloat16),
        ]
        + Exchange.sems(groups, 1)
        + Collect.scratch(columns, groups, block),
        compiler_params=comm_params(6, 60),
        cost_estimate=pl.CostEstimate(
            flops=70 * length * length * width, transcendentals=length * length * heads_here,
            bytes_accessed=16 * length * width,
        ),
        name="attend_backward",
    )(prefix, far_bias, base_bias, qkv, mixed, grad_mixed, totals, part, sums)


def gelu_parts(act):
    inner = math.sqrt(2.0 / math.pi) * (act + 0.044715 * act * act * act)
    tanh = jnp.tanh(inner)
    half = 0.5 * (1.0 + tanh)
    slope = math.sqrt(2.0 / math.pi) * (1.0 + 3.0 * 0.044715 * act * act)
    return act * half, half + 0.5 * act * (1.0 - tanh * tanh) * slope


def slot_rows(experts_here):
    return experts_here * main_slots + -(-experts_here * tail_slots // 8) * 8


def tail_select(expert, sources, tail_height):
    rows = lax.broadcasted_iota(jnp.int32, (sources * tail_slots, sources * tail_height), 0)
    columns = lax.broadcasted_iota(jnp.int32, (sources * tail_slots, sources * tail_height), 1)
    wanted = (rows // tail_slots) * tail_height + expert * tail_slots + rows % tail_slots
    return jnp.where(columns == wanted, 1.0, 0.0).astype(jnp.bfloat16)


def expert_input(main_ref, tail_ref, select):
    width = main_ref.shape[-1]
    main = main_ref[...].reshape(-1, width)
    tail = nn_dot(select, tail_ref[...].reshape(-1, width)).astype(jnp.bfloat16)
    return jnp.concatenate([main, tail], axis=0)


def gates_of(wide_rows):
    return wide_rows[:, D : D + 1].astype(jnp.float32) + wide_rows[:, D + 1 : D + 2].astype(
        jnp.float32
    )


def expert_output(value, select, expert, main_sc, tail_sc):
    low = value.astype(jnp.bfloat16)
    main_count = main_sc.shape[0] * main_sc.shape[1] * main_slots
    main_sc[...] = low[:main_count].reshape(main_sc.shape)
    spread = tn_dot(select, low[main_count:]).astype(jnp.bfloat16).reshape(tail_sc.shape)

    @pl.when(expert == 0)
    def _():
        tail_sc[...] = spread

    @pl.when(expert > 0)
    def _():
        tail_sc[...] += spread


def expert_act_kernel(
    experts_here,
    row_main,
    row_tail,
    grad_main,
    grad_tail,
    gate_weight,
    up_weight,
    down_weight,
    hidden_ref,
    grad_gate_ref,
    grad_up_ref,
    result_ref,
    back_ref,
    result_main,
    result_tail,
    back_main,
    back_tail,
    sems,
):
    part, expert = pl.program_id(0), pl.program_id(1)
    shards_part = row_main.shape[0]
    sources = shards_part * row_main.shape[1]
    tail_height = row_tail.shape[2]
    sources_at = pl.ds(part * shards_part, shards_part)
    select = tail_select(expert, sources, tail_height)
    wide_rows = expert_input(row_main, row_tail, select)
    rows, gates = wide_rows[:, :D], gates_of(wide_rows)
    grads = expert_input(grad_main, grad_tail, select)
    gate_act = nt_dot(rows, gate_weight[0])
    up_act = nt_dot(rows, up_weight[0])
    gelu, slope = gelu_parts(gate_act)
    hidden = (gelu * up_act).astype(jnp.bfloat16)
    hidden_ref[0] = hidden
    raw_hidden = nt_dot(grads, down_weight[0])
    grad_gates = jnp.sum(raw_hidden * hidden.astype(jnp.float32), axis=1, keepdims=True)
    grad_hidden = raw_hidden * gates
    grad_gate = (grad_hidden * up_act * slope).astype(jnp.bfloat16)
    grad_up = (grad_hidden * gelu).astype(jnp.bfloat16)
    grad_gate_ref[0] = grad_gate
    grad_up_ref[0] = grad_up
    back = nn_dot(grad_gate, gate_weight[0]) + nn_dot(grad_up, up_weight[0])
    lanes = lax.broadcasted_iota(jnp.int32, (back.shape[0], spare), 1)
    back = jnp.concatenate([back, jnp.where(lanes == 0, grad_gates, 0.0)], axis=1)
    result = nn_dot(hidden, down_weight[0])

    def main_copies(at):
        place = pl.ds(pl.multiple_of(at * main_slots, main_slots), main_slots)
        return (
            pltpu.make_async_copy(result_main, result_ref.at[sources_at, :, place, :], sems.at[0]),
            pltpu.make_async_copy(back_main, back_ref.at[sources_at, :, place, :], sems.at[1]),
        )

    @pl.when(expert > 0)
    def _():
        for copy in main_copies(expert - 1):
            copy.wait()

    expert_output(result, select, expert, result_main, result_tail)
    expert_output(back, select, expert, back_main, back_tail)
    for copy in main_copies(expert):
        copy.start()

    @pl.when(expert == experts_here - 1)
    def _():
        place = pl.ds(experts_here * main_slots, tail_height)
        tails = (
            pltpu.make_async_copy(result_tail, result_ref.at[sources_at, :, place, :], sems.at[2]),
            pltpu.make_async_copy(back_tail, back_ref.at[sources_at, :, place, :], sems.at[3]),
        )
        for copy in tails:
            copy.start()
        for copy in main_copies(expert):
            copy.wait()
        for copy in tails:
            copy.wait()


def parts_of(rows):
    shards, groups = rows.shape[:2]
    return max(1, shards * groups // part_sources)


def row_specs(rows, experts_here, order):
    shards, groups, height, width = rows.shape
    shards_part = shards // parts_of(rows)
    tail_height = slot_rows(experts_here) - experts_here * main_slots
    tail_at = experts_here * main_slots // tail_height
    main_at = lambda e, c: (c, 0, e, 0)
    side_at = lambda e, c: (c, 0, tail_at, 0)
    return [
        pl.BlockSpec((shards_part, groups, main_slots, width), order(main_at)),
        pl.BlockSpec((shards_part, groups, tail_height, width), order(side_at)),
    ]


def expert_act(rows, grads, gate_weight, up_weight, down_weight):
    experts_here, units, width = gate_weight.shape
    shards, groups = rows.shape[:2]
    count = shards * groups * CAP
    parts = parts_of(rows)
    height = slot_rows(experts_here)
    tail_height = height - experts_here * main_slots
    order = lambda index: lambda c, e: index(e, c)
    weight_spec = pl.BlockSpec((1, units, width), lambda c, e: (e, 0, 0))
    act_spec = pl.BlockSpec((1, count // parts, units), lambda c, e: (e, c, 0))
    act_shape = jax.ShapeDtypeStruct((experts_here, count, units), jnp.bfloat16)
    slot_shape = lambda lanes: jax.ShapeDtypeStruct(
        (shards, groups, height, lanes), jnp.bfloat16
    )
    scratch = [
        pltpu.VMEM((shards // parts, groups, rows_of, lanes), jnp.bfloat16)
        for lanes in (width, width + spare)
        for rows_of in (main_slots, tail_height)
    ]
    return pl.pallas_call(
        functools.partial(expert_act_kernel, experts_here),
        grid=(parts, experts_here),
        out_shape=(act_shape, act_shape, act_shape, slot_shape(width), slot_shape(width + spare)),
        in_specs=row_specs(rows, experts_here, order)
        + row_specs(grads, experts_here, order)
        + [weight_spec] * 3,
        out_specs=(
            act_spec,
            act_spec,
            act_spec,
            pl.BlockSpec(memory_space=pl.ANY),
            pl.BlockSpec(memory_space=pl.ANY),
        ),
        scratch_shapes=scratch + [pltpu.SemaphoreType.DMA((4,))],
        compiler_params=pltpu.CompilerParams(vmem_limit_bytes=60 * mega),
        cost_estimate=pl.CostEstimate(
            flops=12 * experts_here * count * width * units,
            transcendentals=experts_here * count * units,
            bytes_accessed=6 * experts_here * width * units + 8 * experts_here * count * width,
        ),
        name="expert_act",
    )(rows, rows, grads, grads, gate_weight, up_weight, down_weight)


def expert_weight_kernel(
    parts,
    groups,
    columns,
    chunks,
    row_main,
    row_tail,
    grad_main,
    grad_tail,
    hidden_ref,
    grad_gate_ref,
    grad_up_ref,
    grads_qkv,
    grads_own,
    piece,
    qkv_rows,
    gate_out,
    up_out,
    down_out,
    grads_out,
    sum_all,
    piece_all,
    qkv_all,
    *scratch,
):
    expert, part = pl.program_id(0), pl.program_id(1)
    steps = EXPERTS // groups * parts
    now = expert * parts + part
    spot = Spot(groups, columns)
    tail = Tail(
        spot,
        chunks,
        (grads_qkv, grads_own, piece, qkv_rows, grads_out, sum_all, piece_all, qkv_all),
        scratch,
    )

    @pl.when(now == 0)
    def _():
        spot.meet()
        tail.begin()

    sources = row_main.shape[0] * row_main.shape[1]
    select = tail_select(expert, sources, row_tail.shape[2])
    wide_rows = expert_input(row_main, row_tail, select)
    rows = wide_rows[:, :D]
    grads = expert_input(grad_main, grad_tail, select)
    grad_low = (grads.astype(jnp.float32) * gates_of(wide_rows)).astype(jnp.bfloat16)

    @pl.when(part == 0)
    def _():
        gate_out[0] = tn_dot(grad_gate_ref[0], rows)
        up_out[0] = tn_dot(grad_up_ref[0], rows)
        down_out[0] = tn_dot(hidden_ref[0], grad_low)

    if parts > 1:

        @pl.when(part > 0)
        def _():
            gate_out[0] += tn_dot(grad_gate_ref[0], rows)
            up_out[0] += tn_dot(grad_up_ref[0], rows)
            down_out[0] += tn_dot(hidden_ref[0], grad_low)

    @pl.when(now == 0)
    def _():
        tail.gather()

    @pl.when(now == steps // 2)
    def _():
        tail.hop(1)

    @pl.when(now == steps - 1)
    def _():
        tail.hop(2)
        tail.hop(3)
        tail.finish()


def expert_weight_grads(
    rows, grads, hidden, grad_gate, grad_up, grads_qkv, grads_own, piece, qkv_rows
):
    groups, row_count, thirds = grads_qkv.shape
    apart = thirds // 3 % 128 != 0
    grads_shape = grads_qkv.shape if apart else (row_count, thirds * groups)
    columns, chunks = grads_own.shape[:2]
    block = grads_own.shape[2:]
    shape_of = lambda shape: jax.ShapeDtypeStruct(shape, jnp.bfloat16)
    experts_here, count, units = hidden.shape
    width = grads.shape[-1]
    parts = parts_of(rows)
    order = lambda index: index
    act_spec = pl.BlockSpec((1, count // parts, units), lambda e, c: (e, c, 0))
    out_spec = pl.BlockSpec((1, units, width), lambda e, c: (e, 0, 0))
    out_shape = jax.ShapeDtypeStruct((experts_here, units, width), jnp.float32)
    return pl.pallas_call(
        functools.partial(expert_weight_kernel, parts, groups, columns, chunks),
        grid=(experts_here, parts),
        out_shape=(
            out_shape,
            out_shape,
            out_shape,
            shape_of(grads_shape),
            shape_of((groups, chunks) + block),
            shape_of((groups,) + piece.shape),
            shape_of((columns,) + qkv_rows.shape),
        ),
        in_specs=row_specs(rows, experts_here, order)
        + row_specs(grads, experts_here, order)
        + [act_spec] * 3
        + [anywhere] * 4,
        out_specs=(out_spec, out_spec, out_spec) + (anywhere,) * 4,
        scratch_shapes=Tail.scratch(columns, groups, chunks, block, 1 if apart else 3),
        compiler_params=comm_params(7, 60),
        cost_estimate=pl.CostEstimate(
            flops=6 * experts_here * count * width * units,
            transcendentals=0,
            bytes_accessed=12 * experts_here * width * units + 10 * experts_here * count * width,
        ),
        name="expert_weight_grads",
    )(
        rows,
        rows,
        grads,
        grads,
        hidden,
        grad_gate,
        grad_up,
        grads_qkv,
        grads_own,
        piece,
        qkv_rows,
    )


def pair_slots(token_routes, ranks, experts_here):
    row_count = token_routes.shape[0]
    expert_pair = jnp.concatenate([token_routes[:, 0], token_routes[:, 1]])
    rank_pair = jnp.concatenate([ranks, ranks + row_count])
    earlier = (expert_pair[None, :] == expert_pair[:, None]) & (
        rank_pair[None, :] < rank_pair[:, None]
    )
    slot_index = jnp.sum(earlier.astype(jnp.int32), axis=1)
    height = slot_rows(experts_here)
    local = expert_pair % experts_here
    main_at = local * main_slots + slot_index
    tail_at = experts_here * main_slots + local * tail_slots + slot_index - main_slots
    row = jnp.where(slot_index < main_slots, main_at, tail_at)
    slots = (expert_pair // experts_here) * height + row
    return jnp.where(slot_index < CAP, slots, -1)


def router_head(logits, token_routes, weights):
    token_count = logits.shape[0]
    probabilities = jax.nn.softmax(logits, axis=-1)
    log_totals = jax.nn.logsumexp(logits, axis=-1)
    picked = (token_routes[:, :, None] == jnp.arange(EXPERTS, dtype=jnp.int32)).astype(jnp.float32)
    chosen = jnp.sum(picked * probabilities[:, None, :], axis=-1)
    gate_values = chosen / jnp.sum(chosen, axis=1, keepdims=True)
    shares = jnp.sum(picked, axis=(0, 1)) / (token_count * TOP)
    balance = EXPERTS * jnp.sum(shares * jnp.sum(probabilities, axis=0))
    return (gate_values, weights[0] * jnp.sum(log_totals * log_totals) + weights[1] * balance)


def column(values, rows):
    return jnp.pad(values, (0, rows - values.shape[0]))[:, None]


def shards(
    inputs,
    grad_out,
    prefix,
    routes,
    priority,
    loss_weights,
    norm_attn,
    norm_moe,
    qkv_weight,
    out_weight,
    bias_table,
    router_weight,
    gate_weight,
    up_weight,
    down_weight,
):
    row_count = inputs.shape[0]
    groups = lax.axis_size("expert")
    columns_of = lax.axis_size("shard")
    place = lax.axis_index("expert")
    length = row_count * groups
    heads_here = HEADS // groups
    width = heads_here * HEAD
    experts_here = EXPERTS // groups
    shard_rows = D // columns_of
    height = slot_rows(experts_here)

    own_columns = lax.dynamic_slice_in_dim(
        qkv_weight.reshape(shard_rows, 3, groups, width), place, 1, 2
    ).reshape(shard_rows, 3 * width)
    packed_small = jnp.concatenate(
        [
            own_columns,
            router_weight,
            norm_attn[:, None],
            norm_moe[:, None],
            column(bias_table.reshape(-1), shard_rows),
            jnp.zeros((shard_rows, spare - EXPERTS - 3), jnp.bfloat16),
        ],
        axis=1,
    )
    tokens_all, small_full, out_full = entry_gather(
        inputs.reshape(row_count, D), [packed_small, out_weight], groups, columns_of
    )
    tokens_all = tokens_all.reshape(length, D)
    small_full = small_full.reshape(D, 3 * width + spare)
    out_full = out_full.reshape(D, D)
    own_weight = small_full[:, : 3 * width]
    extra = small_full[:, 3 * width :]
    router_full = extra[:, :EXPERTS]
    gain_attn = extra[:, EXPERTS].astype(jnp.float32)
    gain_moe = extra[:, EXPERTS + 1].astype(jnp.float32)
    table_rows = BUCKETS // columns_of
    table_full = (
        extra[:, EXPERTS + 2].reshape(columns_of, shard_rows)[:, : table_rows * HEADS]
    ).reshape(BUCKETS, HEADS)
    table_own = lax.dynamic_slice_in_dim(
        table_full.astype(jnp.float32), place * heads_here, heads_here, 1
    )
    near_ids = jnp.asarray(skew_buckets(), jnp.int32)
    near_hot = (near_ids[:, None] == jnp.arange(BUCKETS, dtype=jnp.int32)).astype(jnp.float32)
    base_bias = (
        jnp.dot(near_hot, table_own, precision=lax.Precision.HIGHEST).reshape(3, 2 * tile, heads_here)
        * log2e
    )
    base_bias = jnp.transpose(base_bias, (2, 0, 1)).reshape(heads_here * 3, 2 * tile)
    far_bias = jnp.stack([table_own[15], table_own[31]], axis=1) * log2e

    token_routes = routes.reshape(row_count, TOP)
    slots = pair_slots(token_routes, priority.reshape(row_count), experts_here)
    slot_map = (
        jnp.arange(groups * height, dtype=jnp.int32)[:, None] == slots[None, :]
    ).reshape(groups * height, TOP, row_count)
    slot_any = jnp.any(slot_map, axis=1).astype(jnp.bfloat16)
    slot_pairs = slot_map.astype(jnp.bfloat16).reshape(groups * height, TOP * row_count)

    grad_low = grad_out.reshape(row_count, D)
    grad_slots = nn_dot(slot_any, grad_low).astype(jnp.bfloat16).reshape(groups, height, D)
    normed_all = rms_norm(tokens_all.astype(jnp.float32), gain_attn).astype(jnp.bfloat16)
    qkv_own = nn_dot(normed_all, own_weight).astype(jnp.bfloat16)
    mixed_own, totals, grads_received = attend_forward(
        prefix, far_bias, base_bias, qkv_own, grad_slots, columns_of
    )
    attended = exchange_mixed(mixed_own.reshape(groups, row_count, width), columns_of, 8)

    tokens_in = inputs.reshape(row_count, D).astype(jnp.float32)
    middle = tokens_in + nn_dot(attended, out_full)
    normed_two, norm_two_back = jax.vjp(rms_norm, middle, gain_moe)
    low_two = normed_two.astype(jnp.bfloat16)
    logits = nn_dot(low_two, router_full)
    router_out, router_back = jax.vjp(
        lambda logit_in: router_head(logit_in, token_routes, loss_weights), logits
    )
    gate_values = router_out[0]
    gate_high = lax.reduce_precision(gate_values, 8, 7)
    gate_parts = jnp.stack([gate_high, gate_values - gate_high], axis=-1).astype(jnp.bfloat16)
    wide_rows = jnp.concatenate(
        [
            jnp.broadcast_to(low_two[None], (TOP, row_count, D)),
            jnp.pad(jnp.transpose(gate_parts, (1, 0, 2)), ((0, 0), (0, 0), (0, spare - 2))),
        ],
        axis=2,
    ).reshape(TOP * row_count, D + spare)
    outgoing = nn_dot(slot_pairs, wide_rows).astype(jnp.bfloat16)
    rows_received = dispatch(outgoing.reshape(groups, height, D + spare), columns_of, 2)
    gate_across, up_across, down_across = (
        jnp.transpose(weight, (0, 2, 1)) for weight in (gate_weight, up_weight, down_weight)
    )
    hidden, grad_gate, grad_up, result_part, back_part = expert_act(
        rows_received, grads_received, gate_across, up_across, down_across
    )
    grad_returned = collect(back_part, 3).reshape(groups * height, D + spare)
    grad_low_two = tn_dot(slot_any, grad_returned[:, :D])
    grad_gates = jnp.transpose(
        tn_dot(slot_pairs, grad_returned[:, D:])[:, 0].reshape(TOP, row_count)
    )
    grad_top = grad_low.astype(jnp.float32)
    grad_logits = router_back((grad_gates, jnp.ones((), jnp.float32)))[0]
    low_logits = grad_logits.astype(jnp.bfloat16)
    router_grad = tn_dot(low_two, low_logits)
    grad_low_two = grad_low_two + nt_dot(low_logits, router_full)
    grad_middle_norm, gain_moe_grad = norm_two_back(grad_low_two)
    grad_middle = grad_top + grad_middle_norm
    low_middle = grad_middle.astype(jnp.bfloat16)
    out_grad = tn_dot(attended, low_middle)
    grad_attended = nt_dot(low_middle, out_full).astype(jnp.bfloat16)
    grad_mixed, out_sums = exchange_grad_mixed(
        grad_attended,
        out_grad.astype(jnp.bfloat16).reshape(columns_of, groups, shard_rows // groups, D),
        groups,
        9,
    )
    grad_qkv, near_sums, side_sums, returned, out_piece = attend_backward(
        prefix,
        far_bias,
        base_bias,
        qkv_own,
        mixed_own,
        grad_mixed.reshape(length, width),
        totals,
        result_part,
        out_sums,
        columns_of,
    )
    pair_out = tn_dot(slot_pairs, returned.reshape(groups * height, D)).reshape(
        TOP, row_count, D
    )
    mixture = gate_values[:, 0:1] * pair_out[0] + gate_values[:, 1:2] * pair_out[1]
    output = (middle + mixture).astype(jnp.bfloat16)

    table_grad = jnp.einsum(
        "hil,ilb->bh",
        near_sums.reshape(heads_here, 3, 2 * tile),
        near_hot.reshape(3, 2 * tile, BUCKETS),
        precision=lax.Precision.HIGHEST,
    )
    far_sums = jnp.sum(side_sums, axis=(2, 3))
    bucket_ids = jnp.arange(BUCKETS, dtype=jnp.int32)[:, None]
    table_grad = table_grad + jnp.where(bucket_ids == 15, far_sums[:, 0][None], 0.0)
    table_grad = table_grad + jnp.where(bucket_ids == 31, far_sums[:, 1][None], 0.0)
    table_column = jnp.pad(
        table_grad.reshape(columns_of, table_rows * heads_here),
        ((0, 0), (0, shard_rows - table_rows * heads_here)),
    ).reshape(D, 1)

    own_grad = tn_dot(normed_all, grad_qkv)
    gain_part = jnp.sum(own_grad * own_weight.astype(jnp.float32), axis=1) / gain_attn
    last_pack = jnp.concatenate(
        [
            own_grad,
            gain_part[:, None],
            table_column,
            gain_moe_grad[:, None],
            router_grad,
            jnp.zeros((D, spare - 3 - EXPERTS), jnp.float32),
        ],
        axis=1,
    ).astype(jnp.bfloat16)
    chunks = 2
    gate_grad, up_grad, down_grad, grad_projected, last_all, out_all, qkv_full = (
        expert_weight_grads(
            rows_received,
            grads_received,
            hidden,
            grad_gate,
            grad_up,
            grad_qkv.reshape(groups, row_count, 3 * width),
            last_pack.reshape(columns_of, chunks, shard_rows // chunks, 3 * width + spare),
            out_piece,
            qkv_weight,
        )
    )
    qkv_full = qkv_full.reshape(D, 3 * D)
    out_total = out_all.reshape(shard_rows, D).astype(jnp.float32)
    last_all = last_all.reshape(groups, shard_rows, 3 * width + spare)
    qkv_total = unpack_columns(last_all, width)
    last_extra = last_all[:, :, 3 * width :].astype(jnp.float32)
    extra_total = jnp.sum(last_extra, axis=0)
    table_total = jnp.transpose(
        last_extra[:, : table_rows * heads_here, 1].reshape(groups, table_rows, heads_here),
        (1, 0, 2),
    ).reshape(table_rows, HEADS)

    if width % 128:
        grad_projected = jnp.transpose(
            grad_projected.reshape(groups, row_count, 3, width), (1, 2, 0, 3)
        ).reshape(row_count, 3 * D)
    grad_low_one = nt_dot(grad_projected, qkv_full)
    _, norm_one_back = jax.vjp(lambda features: rms_norm(features, gain_attn), tokens_in)
    input_grad = grad_middle + norm_one_back(grad_low_one)[0]
    return (
        output.reshape(row_count, 1, D),
        input_grad.reshape(row_count, 1, D),
        extra_total[:, 0],
        extra_total[:, 2],
        qkv_total,
        out_total,
        table_total,
        extra_total[:, 3 : 3 + EXPERTS],
        jnp.transpose(gate_grad, (0, 2, 1)),
        jnp.transpose(up_grad, (0, 2, 1)),
        jnp.transpose(down_grad, (0, 2, 1)),
    )


def solution(mesh):
    placed = (
        P("expert", "shard", None),
        P("expert", "shard", None),
        P("shard"),
        P("expert", "shard", None),
        P("expert", "shard", None),
        P(),
        P("shard"),
        P("shard"),
        P("shard", None),
        P("shard", None),
        P("shard", None),
        P("shard", None),
        P("expert", None, "shard"),
        P("expert", None, "shard"),
        P("expert", None, "shard"),
    )
    return jax.shard_map(
        shards,
        mesh=mesh,
        in_specs=placed,
        out_specs=(
            P("expert", "shard", None),
            P("expert", "shard", None),
            P("shard"),
            P("shard"),
            P("shard", None),
            P("shard", None),
            P("shard", None),
            P("shard", None),
            P("expert", None, "shard"),
            P("expert", None, "shard"),
            P("expert", None, "shard"),
        ),
        check_vma=False,
    )
```

time: 2550 us -> 521 us (0.20)
  waiting for transfers between devices: 967 us -> 0 us
  matrix products: 825 us -> 34.4 us
  other arithmetic: 430 us -> 15 us
  Pallas kernels: 0 us -> 394 us
  local copies, waits for them, and re-layouts: 207 us -> 65.4 us
  blocking collectives: 70 us -> 0 us
    reduce_scatter x6 -> x0, waiting for transfers between devices: 684 us -> none  [the longest x1 462 us: expert_backward_weights(): lax.psum_scatter(jnp.stack([jnp.einsum('erd,erf->fed', received, grad_gat...]
    dot_general x78 -> x16, matrix products: 682 us -> 34.4 us  [the longest x6 14.3 us: tn_dot(): lax.dot_general(left, right, (((0,), (0,)), ((), ())), preferred_element_...]
    pallas_call x0 -> x10, Pallas kernels: none -> 394 us  [the longest x1 76.6 us: expert_weight_grads(): pl.pallas_call(functools.partial(expert_weight_kernel, parts, groups, col...]
    eq x16 -> x1, other arithmetic: 190 us -> 0.52 us  [shards(): bucket_ids == 31]
    all_gather x7 -> x0, waiting for transfers between devices: 157 us -> none  [the longest x1 67.9 us: shards(): lax.all_gather(values_own, 'expert', axis=0, tiled=True)]
    sub x8 -> x0, matrix products: 143 us -> none  [one_group(): grad_scores = attention * (grad_weights - inner)]
    reduce_sum x21 -> x4, other arithmetic: 140 us -> 0.64 us  [the longest x1 0.34 us: pair_slots(): slot_index = jnp.sum(earlier.astype(jnp.int32), axis=1)]
    all_to_all x4 -> x0, waiting for transfers between devices: 99.4 us -> none  [the longest x2 63.8 us: to_experts(): lax.all_to_all(slot_rows, 'expert', split_axis=0, concat_axis=1, tiled=True)]
  transfers between devices with their start and end apart: 18 -> 0, of which waited for: 12 -> 0; matrix products, arithmetic and copies ran while one was open for 21% -> 0% of each run, Pallas kernels for 0% -> 0%
where the time goes in v1:
time: 521 us; the launch traced here: 512 us
  Pallas kernels  394 us (76%)
  local copies, waits for them, and re-layouts  65.4 us (13%)
  matrix products  34.4 us (7%)
  other arithmetic  15 us (3%)
    pallas_call x1, Pallas kernels, expert_weight_grads(): pl.pallas_call(functools.partial(expert_weight_kernel, parts, groups, col...  76.6 us
    pallas_call x1, Pallas kernels, entry_gather(): pl.pallas_call(functools.partial(entry_kernel, groups, columns, count), o...  55.3 us
    pallas_call x1, Pallas kernels, attend_backward(): pl.pallas_call(functools.partial(attend_backward_kernel, heads_here, grou...  53.8 us
    unnamed x80, local copies, waits for them, and re-layouts  50.4 us
    pallas_call x1, Pallas kernels, collect(): pl.pallas_call(functools.partial(collect_kernel, groups, columns), out_sh...  48.7 us
    pallas_call x1, Pallas kernels, dispatch(): pl.pallas_call(functools.partial(dispatch_kernel, groups, columns), out_s...  40.3 us
    pallas_call x1, Pallas kernels, attend_forward(): pl.pallas_call(functools.partial(attend_forward_kernel, heads_here, group...  40.2 us
    pallas_call x1, Pallas kernels, expert_act(): pl.pallas_call(functools.partial(expert_act_kernel, experts_here), grid=(...  36.7 us

profile of v1, /device:TPU:0, one launch (start us, length us, event | category | flops | bytes accessed | tf_op | source)
XLA Modules:
  0.0 512.3 jit_solution(2181800750700243597)
XLA Ops:
  1.3 0.8 reshape.483
  2.1 0.7 broadcast_add_fusion
  2.8 1.3 fusion.56
  4.7 0.5 iota_compare_fusion.12
  5.2 0.8 slice_bitcast_fusion.3
  6.0 0.7 pad_add_fusion
  6.7 0.3 convert_reduce_fusion
  7.1 0.6 fusion.47
  7.8 1.4 broadcast_in_dim.127
  9.2 1.4 broadcast_in_dim.128
  10.6 0.8 copy.133
  11.6 2.5 convolution_convert_fusion.3
  14.2 1.8 copy.131
  16.2 1.1 concatenate.57.refs_1_
  17.3 55.3 %entry_gather.1 = (bf16[8,256,1024]{2,1,0:T(8,128)(2,1)S(1)}, bf16[4,256,512]{2,1,0:T(8,128)(2,1)S(1)}, bf16[4,256,1024]{2,1,0:T(8,128)(2,1)S(1)}) custom-call(bf16[256,1024]{1,0:T(8,128)(2,1)S(1)} %bitcast.119, bf16[256,512]{1,0:T(8,128)(2,1)S(1)} %concatenate.57.refs_1_, bf16[256,1024]{1,0:T(8,128)(2,1)S(1)} %copy-done.8), custom_call_target="tpu_custom_call" | custom-call | tf_op jit(solution)/shard_map/entry_gather/pallas_call | solution.py:278
  72.6 2.0 copy-done
  74.6 1.0 copy-done.4
  75.9 3.2 multiply_reduce_fusion
  79.2 1.4 convert_reduce_fusion.2
  80.6 2.6 fusion.1
  83.2 0.4 convolution_multiply_fusion
  84.0 4.8 convolution_convert_fusion.1.qkv_ref
  88.9 40.2 %attend_forward.1 = (bf16[2048,128]{1,0:T(8,128)(2,1)S(1)}, f32[8,2,256]{2,1,0:T(2,128)S(1)}, bf16[4,8,72,1024]{3,2,1,0:T(8,128)(2,1)S(1)}) custom-call(s32[1]{0:T(128)S(6)} %copy.158.prefix_ref, f32[2,2]{1,0:T(2,128)S(1)} %maximum_multiply_fusion.far_ref, f32[6,512]{1,0:T(8,128)S(1)} %reshape.486.base_ref, ...), custom_call_target="tpu_custom_call" | custom-call | flops 21474836480 | bytes 2097152 | tf_op jit(solution)/shard_map/attend_forward/pallas_call | solution.py:949
  129.2 0.6 copy-done.16
  129.8 14.4 %exchange_mixed.1 = bf16[256,1024]{1,0:T(8,128)(2,1)S(1)} custom-call(bf16[8,256,128]{2,1,0:T(8,128)(2,1)S(1)} %bitcast.129), custom_call_target="tpu_custom_call" | custom-call | tf_op jit(solution)/shard_map/exchange_mixed/pallas_call | solution.py:617
  144.2 0.8 multiply_reduce_fusion.4
  145.1 0.9 copy-done.17
  146.2 0.8 copy-done.22
  147.0 1.2 fusion.57
  148.6 1.2 broadcast_in_dim.110
  149.9 0.9 convolution_convert_fusion
  150.9 40.3 %dispatch_rows.1.row_main.row_tail = bf16[4,8,72,1152]{3,2,1,0:T(8,128)(2,1)S(1)} custom-call(bf16[8,72,1152]{2,1,0:T(8,128)(2,1)S(1)} %bitcast.127), custom_call_target="tpu_custom_call" | custom-call | tf_op jit(solution)/shard_map/dispatch_rows/pallas_call | solution.py:390
  191.1 2.4 copy-done.2
  193.5 36.7 %expert_act.1 = (bf16[4,576,704]{2,1,0:T(8,128)(2,1)}, bf16[4,576,704]{2,1,0:T(8,128)(2,1)}, bf16[4,576,704]{2,1,0:T(8,128)(2,1)}, bf16[4,8,72,1024]{3,2,1,0:T(8,128)(2,1)}, bf16[4,8,72,1152]{3,2,1,0:T(8,128)(2,1)}) custom-call(bf16[4,8,72,1152]{3,2,1,0:T(8,128)(2,1)} %copy-done.2, bf16[4,8,72,1152]{3,2,1,0:T(8,128)(2,1)} %copy-done.2, ...), custom_call_target="tpu_custom_call" | custom-call | flops 19931332608 | bytes 36175872 | tf_op jit(solution)/shard_map/expert_act/pallas_call | solution.py:1381
  230.2 48.7 %collect_rows.1 = bf16[8,72,1152]{2,1,0:T(8,128)(2,1)} custom-call(bf16[4,8,72,1152]{3,2,1,0:T(8,128)(2,1)} %get-tuple-element.41.part), custom_call_target="tpu_custom_call" | custom-call | tf_op jit(solution)/shard_map/collect_rows/pallas_call | solution.py:583
  278.9 1.2 fusion.9
  280.1 2.9 fusion.4
  283.3 0.8 negate_add_fusion
  284.1 1.3 convolution_convert_fusion.5
  285.4 2.2 multiply_reduce_fusion.2
  287.6 0.3 fusion.13
  288.0 1.0 copy-done.20
  288.9 1.6 convolution_convert_fusion.4.grads
  291.0 2.0 convolution_convert_fusion.2
  292.9 24.6 %exchange_grad_mixed.1 = (bf16[8,256,128]{2,1,0:T(8,128)(2,1)S(1)}, bf16[8,32,1024]{2,1,0:T(8,128)(2,1)S(1)}) custom-call(bf16[256,1024]{1,0:T(8,128)(2,1)S(1)} %copy-done.6, bf16[4,8,32,1024]{3,2,1,0:T(8,128)(2,1)S(1)} %bitcast.118), custom_call_target="tpu_custom_call" | custom-call | tf_op jit(solution)/shard_map/exchange_grad_mixed/pallas_call | solution.py:666
  317.5 0.8 copy-done.12
  318.3 0.9 copy-done.13
  319.2 53.8 %attend_backward.1 = (bf16[2048,384]{1,0:T(8,128)(2,1)}, f32[6,512]{1,0:T(8,128)}, f32[2,2,8,256]{3,2,1,0:T(8,128)}, bf16[8,72,1024]{2,1,0:T(8,128)(2,1)}, bf16[32,1024]{1,0:T(8,128)(2,1)}) custom-call(s32[1]{0:T(128)S(6)} %copy.158.prefix_ref, f32[2,2]{1,0:T(2,128)} %copy-done.11, f32[6,512]{1,0:T(8,128)} %copy-done.10, bf16[2048,384]{1,0:T(8,128)(2,1)} %copy-done.15, ...), custom_call_target="tpu_custom_call" | custom-call | flops 37580963840 | bytes 4194304 | tf_op jit(solution)/shard_map/attend_backward/pallas_call | solution.py:1172
  373.1 5.9 %multiply_reduce_fusion.1 = (f32[1024]{0:T(1024)S(1)}, bf16[1024,384]{1,0:T(8,128)(2,1)}) fusion(bf16[1024,512]{1,0:T(8,128)(2,1)S(1)} %bitcast.125, bf16[2048,1024]{1,0:T(8,128)(2,1)} %fusion.1, bf16[2048,384]{1,0:T(8,128)(2,1)} %get-tuple-element.50), kind=kOutput, calls=%fused_computation.15 | convolution fusion | flops 1612184576 | bytes 7344128 | tf_op jit(solution)/shard_map/dot_general | solution.py:793
  380.4 3.7 concatenate.70.grads_own
  384.1 1.0 fusion.6
  385.4 1.0 fusion.26
  386.4 76.6 %expert_weight_grads.1 = (f32[4,704,1024]{2,1,0:T(8,128)}, f32[4,704,1024]{2,1,0:T(8,128)}, f32[4,704,1024]{2,1,0:T(8,128)}, bf16[256,3072]{1,0:T(8,128)(2,1)}, ...) custom-call(bf16[4,8,72,1152]{3,2,1,0:T(8,128)(2,1)} %copy-done.2, ...), custom_call_target="tpu_custom_call" | custom-call | flops 9965666304 | bytes 58195968 | tf_op jit(solution)/shard_map/expert_weight_grads/pallas_call | solution.py:1499
  463.0 5.3 %fusion.16 = (f32[256]{0:T(256)S(1)}, f32[256]{0:T(256)S(1)}, f32[256,1024]{1,0:T(8,128)S(1)}) fusion(bf16[256,1,1024]{2,0,1:T(8,128)(2,1)S(1)} %copy-done.3, f32[1024]{0:T(1024)S(1)} %get-tuple-element.130, bf16[256,3072]{1,0:T(8,128)(2,1)} %get-tuple-element.54, bf16[1024,3072]{1,0:T(8,128)(2,1)} %bitcast.165), kind=kOutput, calls=%fused_computation.38 | convolution fusion | flops 1612185088 | bytes 9443328 | tf_op jit(solution)/shard_map/dot_general | solution.py:789
  468.3 0.3 fusion.15
  468.6 2.0 copy.148
  470.7 0.8 slice_reduce_fusion.1
  471.6 0.7 copy.150
  472.7 0.7 copy.149
  473.4 3.8 unpack_columns.1
  477.2 1.1 bitcast_convert_fusion
  478.3 11.2 %copy.159 = f32[4,1024,704]{1,2,0:T(8,128)} copy(f32[4,1024,704]{1,2,0:T(8,128)} %bitcast.133) | data formatting | bytes 23068672
  489.5 11.2 %copy.160 = f32[4,1024,704]{1,2,0:T(8,128)} copy(f32[4,1024,704]{1,2,0:T(8,128)} %bitcast.132) | data formatting | bytes 23068672
  500.7 11.2 %copy.161 = f32[4,1024,704]{1,2,0:T(8,128)} copy(f32[4,1024,704]{1,2,0:T(8,128)} %bitcast.131) | data formatting | bytes 23068672
  (126 shorter events, 4.8 us)
Async XLA Ops:
  14.2 3.1 copy-start.3
  14.2 3.1 copy-start.8
  72.6 2.0 copy-start
  74.6 1.0 copy-start.4
  75.9 4.7 copy-start.1
  80.6 2.6 copy-start.32
  83.7 5.2 %copy-start.10 = (f32[6,512]{1,0:T(8,128)}, f32[6,512]{1,0:T(8,128)S(1)}, u32[]{:S(2)}) copy-start(f32[6,512]{1,0:T(8,128)S(1)} %reshape.486.base_ref) | copy-start | bytes 36868
  84.0 4.9 copy-start.11
  84.0 4.9 copy-start.7
  88.9 40.3 %copy-start.15 = (bf16[2048,384]{1,0:T(8,128)(2,1)}, bf16[2048,384]{1,0:T(8,128)(2,1)S(1)}, u32[]{:S(2)}) copy-start(bf16[2048,384]{1,0:T(8,128)(2,1)S(1)} %convolution_convert_fusion.1.qkv_ref) | copy-start | bytes 4718596
  129.2 0.6 copy-start.16
  129.8 15.3 %copy-start.9 = (bf16[2048,128]{1,0:T(8,128)(2,1)}, bf16[2048,128]{1,0:T(8,128)(2,1)S(1)}, u32[]{:S(2)}) copy-start(bf16[2048,128]{1,0:T(8,128)(2,1)S(1)} %get-tuple-element.38.mixed_ref) | copy-start | bytes 1572868
  129.8 15.3 %copy-start.14 = (bf16[4,8,72,1024]{3,2,1,0:T(8,128)(2,1)}, bf16[4,8,72,1024]{3,2,1,0:T(8,128)(2,1)S(1)}, u32[]{:S(2)}) copy-start(bf16[4,8,72,1024]{3,2,1,0:T(8,128)(2,1)S(1)} %get-tuple-element.40.grad_main.grad_tail) | copy-start | bytes 14155780
  145.1 1.0 copy-start.17
  145.1 3.3 copy-start.27
  146.2 0.8 copy-start.22
  148.3 1.6 copy-start.29
  191.1 2.4 copy-start.2
  283.3 4.3 copy-start.18
  283.3 4.3 copy-start.24
  287.9 1.0 copy-start.20
  290.6 2.4 copy-start.6
  317.5 0.8 copy-start.12
  318.3 0.9 copy-start.13
  319.2 53.8 %copy-start.5 = (bf16[4,256,512]{2,1,0:T(8,128)(2,1)S(1)}, bf16[4,256,512]{2,1,0:T(8,128)(2,1)}, u32[]{:S(2)}) copy-start(bf16[4,256,512]{2,1,0:T(8,128)(2,1)} %copy-done.4) | copy-start | bytes 3145732
  373.0 6.0 %copy-start.26 = (f32[2,2,8,256]{3,2,1,0:T(8,128)S(1)}, f32[2,2,8,256]{3,2,1,0:T(8,128)}, u32[]{:S(2)}) copy-start(f32[2,2,8,256]{3,2,1,0:T(8,128)} %get-tuple-element.52) | copy-start | bytes 98308
  373.0 6.2 %copy-start.28 = (f32[6,512]{1,0:T(8,128)S(1)}, f32[6,512]{1,0:T(8,128)}, u32[]{:S(2)}) copy-start(f32[6,512]{1,0:T(8,128)} %get-tuple-element.51) | copy-start | bytes 36868
  373.0 6.3 %copy-start.31 = (s32[3,512]{1,0:T(4,128)S(1)}, s32[3,512]{1,0:T(4,128)}, u32[]{:S(2)}) copy-start(s32[3,512]{1,0:T(4,128)} %constant.114) | copy-start | bytes 18436
  373.0 6.3 %copy-start.33 = (pred[32]{0:T(512)(128)(4,1)S(1)}, pred[32]{0:T(512)(128)(4,1)}, u32[]{:S(2)}) copy-start(pred[32]{0:T(512)(128)(4,1)} %get-tuple-element.170) | copy-start | bytes 100
  373.1 6.3 %copy-start.34 = (pred[32]{0:T(512)(128)(4,1)S(1)}, pred[32]{0:T(512)(128)(4,1)}, u32[]{:S(2)}) copy-start(pred[32]{0:T(512)(128)(4,1)} %get-tuple-element.171) | copy-start | bytes 100
  380.4 3.8 copy-start.30
  384.1 1.2 copy-start.19
  463.0 5.3 %copy-start.21 = (f32[256,1024]{1,0:T(8,128)S(1)}, f32[256,1024]{1,0:T(8,128)}, u32[]{:S(2)}) copy-start(f32[256,1024]{1,0:T(8,128)} %copy-done.20) | copy-start | bytes 3145732
  468.3 2.3 copy-start.23
  473.4 3.8 copy-start.25

commit v2 on v1

--- a/solution.py
+++ b/solution.py
@@ -628,57 +628,6 @@
     return out
 
 
-def grad_mixed_kernel(groups, columns, chunks, grads, part, out, part_out, *scratch):
-    spot = Spot(groups, columns)
-    width = out.shape[2]
-
-    def blocks(at, third):
-        if width % 128:
-            return grads.at[at], out.at[spot.place]
-        return grads.at[:, lanes_at(at, width)], out.at[spot.place]
-
-    sums = ColumnSum(spot, chunks, lambda k: k, part, scratch[:4], scratch[4:9])
-    total, total_sem = scratch[9:11]
-    job = Exchange(spot, blocks, 1, *scratch[11:])
-    spot.meet()
-    job.begin()
-    sums.begin()
-    for k in range(chunks):
-        sums.middle(k)
-    stores = [pltpu.make_async_copy(total.at[k], part_out.at[k], total_sem.at[k]) for k in range(chunks)]
-    for k in range(chunks):
-        total[k] = sums.last(k)
-        stores[k].start()
-    job.arrive()
-    job.finish()
-    sums.finish()
-    for store in stores:
-        store.wait()
-
-
-def exchange_grad_mixed(grads, part, groups, which):
-    rows = grads.shape[0]
-    width = grads.shape[1] // groups
-    if width % 128:
-        grads = jnp.transpose(grads.reshape(rows, groups, width), (1, 0, 2))
-    columns, chunks = part.shape[:2]
-    block = part.shape[2:]
-    return pl.pallas_call(
-        functools.partial(grad_mixed_kernel, groups, columns, chunks),
-        out_shape=(
-            jax.ShapeDtypeStruct((groups, rows, width), grads.dtype),
-            jax.ShapeDtypeStruct((chunks,) + block, part.dtype),
-        ),
-        in_specs=[anywhere, anywhere],
-        out_specs=(anywhere, anywhere),
-        scratch_shapes=ColumnSum.scratch(columns, chunks, block)
-        + [pltpu.VMEM((chunks,) + block, part.dtype), pltpu.SemaphoreType.DMA((chunks,))]
-        + Exchange.sems(groups, 1),
-        compiler_params=comm_params(which, 32),
-        name="exchange_grad_mixed",
-    )(grads, part)
-
-
 class Tail:
     def __init__(self, spot, chunks, refs, scratch):
         grads, part, piece, weight, grads_out, sum_all, piece_all, weight_all = refs
@@ -710,33 +659,104 @@
             + ColumnGather.sems(columns)
         )
 
-    def begin(self):
-        self.sums.begin()
-        self.side.begin()
-        self.swap.begin()
-        for k in range(self.chunks):
-            self.sums.middle(k)
-        self.column.begin()
-
-    def gather(self):
-        for k in range(self.chunks):
-            self.own_sum[k] = self.sums.last(k)
-        self.line.begin()
-        self.side.hop(1)
-
-    def hop(self, k):
-        self.line.hop(k)
-        if k + 1 < 4:
-            self.side.hop(k + 1)
-
-    def finish(self):
-        self.column.forward()
-        self.swap.arrive()
-        self.side.finish()
-        self.line.finish()
-        self.column.finish()
-        self.swap.finish()
-        self.sums.finish()
+
+def tail_kernel(
+    groups,
+    columns,
+    chunks,
+    grads,
+    normed,
+    own_weight,
+    gains,
+    extra,
+    piece,
+    weight,
+    grads_out,
+    sum_all,
+    piece_all,
+    weight_all,
+    grads_sc,
+    normed_sc,
+    load_sems,
+    part,
+    *scratch,
+):
+    spot = Spot(groups, columns)
+    refs = (grads, part, piece, weight, grads_out, sum_all, piece_all, weight_all)
+    tail = Tail(spot, chunks, refs, scratch)
+    wide = grads.shape[2]
+    block_rows = D // (columns * chunks)
+    loads = [
+        pltpu.make_async_copy(grads, grads_sc, load_sems.at[0]),
+        pltpu.make_async_copy(normed, normed_sc, load_sems.at[1]),
+    ]
+    for load in loads:
+        load.start()
+    spot.meet()
+    tail.side.begin()
+    tail.swap.begin()
+    for load in loads:
+        load.wait()
+    all_grads = grads_sc[...].reshape(-1, wide)
+
+    for at in range(columns * chunks):
+        rows = pl.ds(at * block_rows, block_rows)
+        grad = tn_dot(normed_sc[:, rows], all_grads)
+        gain = jnp.sum(grad * own_weight[rows, :].astype(jnp.float32), axis=1, keepdims=True)
+        gain = gain / gains[rows, :]
+        lanes = lax.broadcasted_iota(jnp.int32, (block_rows, spare), 1)
+        side = jnp.where(lanes == 0, gain, extra[rows, :].astype(jnp.float32))
+        part[at // chunks, at % chunks] = jnp.concatenate([grad, side], axis=1).astype(jnp.bfloat16)
+    tail.sums.begin()
+    for k in range(chunks):
+        tail.sums.middle(k)
+    tail.column.begin()
+    tail.side.hop(1)
+    for k in range(chunks):
+        tail.own_sum[k] = tail.sums.last(k)
+    tail.line.begin()
+    tail.side.hop(2)
+    tail.line.hop(1)
+    tail.side.hop(3)
+    tail.line.hop(2)
+    tail.column.forward()
+    tail.line.hop(3)
+    tail.side.finish()
+    tail.swap.arrive()
+    tail.line.finish()
+    tail.column.finish()
+    tail.swap.finish()
+    tail.sums.finish()
+
+
+def tail_exchange(grads, normed, own_weight, gains, extra, piece, weight, columns, which):
+    groups, row_count, wide = grads.shape
+    apart = wide // 3 % 128 != 0
+    grads_shape = grads.shape if apart else (row_count, wide * groups)
+    chunks = 2
+    block = (D // columns // chunks, wide + spare)
+    shape_of = lambda shape: jax.ShapeDtypeStruct(shape, jnp.bfloat16)
+    inside = pl.BlockSpec(memory_space=pltpu.VMEM)
+    return pl.pallas_call(
+        functools.partial(tail_kernel, groups, columns, chunks),
+        out_shape=(
+            shape_of(grads_shape),
+            shape_of((groups, chunks) + block),
+            shape_of((groups,) + piece.shape),
+            shape_of((columns,) + weight.shape),
+        ),
+        in_specs=[anywhere, anywhere, inside, inside, inside, anywhere, anywhere],
+        out_specs=(anywhere,) * 4,
+        scratch_shapes=[
+            pltpu.VMEM(grads.shape, jnp.bfloat16),
+            pltpu.VMEM(normed.shape, jnp.bfloat16),
+            pltpu.SemaphoreType.DMA((2,)),
+            pltpu.VMEM((columns, chunks) + block, jnp.bfloat16),
+        ]
+        + Tail.scratch(columns, groups, chunks, block, 1 if apart else 3),
+        compiler_params=comm_params(which, 56),
+        name="tail_exchange",
+    )(grads, normed, own_weight, gains, extra, piece, weight)
 
 
 def unpack_kernel(width, packed, out):
@@ -1263,6 +1283,23 @@
         tail_sc[...] += spread
 
 
+def expert_math(wide_rows, grads, gate_weight, up_weight, down_weight):
+    rows, gates = wide_rows[:, :D], gates_of(wide_rows)
+    gate_act = nt_dot(rows, gate_weight)
+    up_act = nt_dot(rows, up_weight)
+    gelu, slope = gelu_parts(gate_act)
+    hidden = (gelu * up_act).astype(jnp.bfloat16)
+    raw_hidden = nt_dot(grads, down_weight)
+    grad_gates = jnp.sum(raw_hidden * hidden.astype(jnp.float32), axis=1, keepdims=True)
+    grad_hidden = raw_hidden * gates
+    grad_gate = (grad_hidden * up_act * slope).astype(jnp.bfloat16)
+    grad_up = (grad_hidden * gelu).astype(jnp.bfloat16)
+    back = nn_dot(grad_gate, gate_weight) + nn_dot(grad_up, up_weight)
+    lanes = lax.broadcasted_iota(jnp.int32, (back.shape[0], spare), 1)
+    back = jnp.concatenate([back, jnp.where(lanes == 0, grad_gates, 0.0)], axis=1)
+    return hidden, grad_gate, grad_up, back, nn_dot(hidden, down_weight)
+
+
 def expert_act_kernel(
     experts_here,
     row_main,
@@ -1290,24 +1327,13 @@
     sources_at = pl.ds(part * shards_part, shards_part)
     select = tail_select(expert, sources, tail_height)
     wide_rows = expert_input(row_main, row_tail, select)
-    rows, gates = wide_rows[:, :D], gates_of(wide_rows)
     grads = expert_input(grad_main, grad_tail, select)
-    gate_act = nt_dot(rows, gate_weight[0])
-    up_act = nt_dot(rows, up_weight[0])
-    gelu, slope = gelu_parts(gate_act)
-    hidden = (gelu * up_act).astype(jnp.bfloat16)
+    hidden, grad_gate, grad_up, back, result = expert_math(
+        wide_rows, grads, gate_weight[0], up_weight[0], down_weight[0]
+    )
     hidden_ref[0] = hidden
-    raw_hidden = nt_dot(grads, down_weight[0])
-    grad_gates = jnp.sum(raw_hidden * hidden.astype(jnp.float32), axis=1, keepdims=True)
-    grad_hidden = raw_hidden * gates
-    grad_gate = (grad_hidden * up_act * slope).astype(jnp.bfloat16)
-    grad_up = (grad_hidden * gelu).astype(jnp.bfloat16)
     grad_gate_ref[0] = grad_gate
     grad_up_ref[0] = grad_up
-    back = nn_dot(grad_gate, gate_weight[0]) + nn_dot(grad_up, up_weight[0])
-    lanes = lax.broadcasted_iota(jnp.int32, (back.shape[0], spare), 1)
-    back = jnp.concatenate([back, jnp.where(lanes == 0, grad_gates, 0.0)], axis=1)
-    result = nn_dot(hidden, down_weight[0])
 
     def main_copies(at):
         place = pl.ds(pl.multiple_of(at * main_slots, main_slots), main_slots)
@@ -1403,11 +1429,358 @@
     )(rows, rows, grads, grads, gate_weight, up_weight, down_weight)
 
 
+class RowChunk:
+    def __init__(self, spot, number, place_rows, rows_in, rows_all, back_out, bufs, sems):
+        self.spot, self.number, self.place_rows = spot, number, place_rows
+        self.rows_in, self.rows_all, self.back_out = rows_in, rows_all, back_out
+        self.rows, self.back, self.pair_in, self.across_out, self.across_in, self.total = bufs
+        (
+            self.local,
+            self.send,
+            self.recv,
+            self.across_send,
+            self.across_recv,
+            self.core_send,
+            self.core_recv,
+            self.pair_send,
+            self.pair_recv,
+            self.sum_send,
+            self.sum_recv,
+            self.back_send,
+            self.back_recv,
+        ) = sems
+
+    @staticmethod
+    def sems(groups, columns, chunks):
+        half = columns // 2
+        dma = pltpu.SemaphoreType.DMA
+        return (
+            [dma((chunks, 3))]
+            + [dma((chunks, groups))] * 2
+            + [dma((chunks, groups, half))] * 4
+            + [dma((chunks, half))] * 4
+            + [dma((chunks, groups))] * 2
+        )
+
+    def own(self):
+        spot = self.spot
+        return pltpu.make_async_copy(
+            self.rows_in.at[spot.place, self.place_rows],
+            self.rows.at[spot.lane, spot.place],
+            self.local.at[self.number, 0],
+        )
+
+    def keep(self):
+        return pltpu.make_async_copy(
+            self.rows, self.rows_all.at[:, :, self.place_rows], self.local.at[self.number, 1]
+        )
+
+    def swap(self, key):
+        spot, at = self.spot, self.number
+        peer = flip(spot.place, key)
+        return remote(
+            self.rows_in.at[peer, self.place_rows],
+            self.rows.at[spot.lane, spot.place],
+            self.send.at[at, key],
+            self.recv.at[at, key],
+            (peer, spot.lane),
+        )
+
+    def across(self, key, step):
+        spot, at = self.spot, self.number
+        block = self.rows.at[spot.lane, flip(spot.place, key)]
+        return remote(
+            block,
+            block,
+            self.across_send.at[at, key, step],
+            self.across_recv.at[at, key, step],
+            (spot.place, spot.across(step)),
+        )
+
+    def core(self, key, step):
+        spot, at = self.spot, self.number
+        block = self.rows.at[spot.behind(step), flip(spot.place, key)]
+        return remote(
+            block,
+            block,
+            self.core_send.at[at, key, step],
+            self.core_recv.at[at, key, step],
+            (spot.place, spot.partner),
+        )
+
+    def begin(self):
+        self.own().start()
+        for key in range(1, self.spot.groups):
+            self.swap(key).start()
+
+    def advance(self):
+        for key in range(self.spot.groups):
+            if key == 0:
+                self.own().wait()
+            else:
+                self.swap(key).wait_recv()
+            for step in range(1, self.spot.half):
+                self.across(key, step).start()
+            self.core(key, 0).start()
+
+    def complete(self):
+        groups, half = self.spot.groups, self.spot.half
+        for key in range(groups):
+            for step in range(1, half):
+                self.across(key, step).wait_recv()
+                self.core(key, step).start()
+        for key in range(groups):
+            for step in range(half):
+                self.core(key, step).wait_recv()
+        self.keep().start()
+
+    def pair_copy(self, step):
+        spot, at = self.spot, self.number
+        return remote(
+            self.back.at[spot.lane_at(step, True)],
+            self.pair_in.at[step],
+            self.pair_send.at[at, step],
+            self.pair_recv.at[at, step],
+            (spot.place, spot.partner),
+        )
+
+    def sum_copy(self, step):
+        spot, at = self.spot, self.number
+        return remote(
+            self.across_out.at[step],
+            self.across_in.at[step],
+            self.sum_send.at[at, step],
+            self.sum_recv.at[at, step],
+            (spot.place, spot.across(step)),
+        )
+
+    def back_copy(self, key):
+        spot, at = self.spot, self.number
+        peer = flip(spot.place, key)
+        target = self.back_out.at[spot.place, self.place_rows]
+        if key == 0:
+            return pltpu.make_async_copy(self.total.at[peer], target, self.local.at[at, 2])
+        return remote(
+            self.total.at[peer],
+            target,
+            self.back_send.at[at, key],
+            self.back_recv.at[at, key],
+            (peer, spot.lane),
+        )
+
+    def pair(self):
+        for step in list(range(1, self.spot.half)) + [0]:
+            self.pair_copy(step).start()
+
+    def pair_sum(self, step):
+        self.pair_copy(step).wait_recv()
+        mine = self.back[self.spot.lane_at(step, False)].astype(jnp.float32)
+        return mine + self.pair_in[step].astype(jnp.float32)
+
+    def middle(self):
+        for step in range(1, self.spot.half):
+            self.across_out[step] = self.pair_sum(step).astype(jnp.bfloat16)
+            self.sum_copy(step).start()
+
+    def last(self):
+        total = self.pair_sum(0)
+        for step in range(1, self.spot.half):
+            self.sum_copy(step).wait_recv()
+            total = total + self.across_in[step].astype(jnp.float32)
+        self.total[...] = total.astype(jnp.bfloat16)
+        for key in range(self.spot.groups):
+            self.back_copy(key).start()
+
+    def finish(self):
+        groups, half = self.spot.groups, self.spot.half
+        for key in range(1, groups):
+            self.back_copy(key).wait_recv()
+        self.back_copy(0).wait()
+        self.keep().wait()
+        for key in range(groups):
+            if key:
+                self.swap(key).wait_send()
+                self.back_copy(key).wait_send()
+            for step in range(half):
+                self.core(key, step).wait_send()
+                if step:
+                    self.across(key, step).wait_send()
+        for step in range(half):
+            self.pair_copy(step).wait_send()
+            if step:
+                self.sum_copy(step).wait_send()
+
+
+def experts_kernel(
+    experts_here,
+    groups,
+    columns,
+    rows_in,
+    grad_main,
+    grad_tail,
+    gate_weight,
+    up_weight,
+    down_weight,
+    hidden_ref,
+    grad_gate_ref,
+    grad_up_ref,
+    result_ref,
+    rows_all,
+    back_out,
+    result_main,
+    result_tail,
+    result_sems,
+    *scratch,
+):
+    expert = pl.program_id(0)
+    tail_height = result_tail.shape[2]
+    spot = Spot(groups, columns)
+    mains, tails, sems = scratch[:6], scratch[6:12], scratch[12:]
+    chunks = [
+        RowChunk(
+            spot,
+            at,
+            pl.ds(at * main_slots, main_slots),
+            rows_in,
+            rows_all,
+            back_out,
+            [buf.at[at] for buf in mains],
+            sems,
+        )
+        for at in range(experts_here)
+    ]
+    tail = RowChunk(
+        spot,
+        experts_here,
+        pl.ds(experts_here * main_slots, tail_height),
+        rows_in,
+        rows_all,
+        back_out,
+        tails,
+        sems,
+    )
+
+    @pl.when(expert == 0)
+    def _():
+        spot.meet()
+        for chunk in [tail] + chunks:
+            chunk.begin()
+        tail.advance()
+        chunks[0].advance()
+
+    for at in range(experts_here):
+
+        @pl.when(expert == at)
+        def _():
+            if at + 1 < experts_here:
+                chunks[at + 1].advance()
+            if at == 0:
+                tail.complete()
+            chunks[at].complete()
+            if at:
+                chunks[at - 1].middle()
+
+    select = tail_select(expert, groups * columns, tail_height)
+    main_rows, tail_rows, main_back, tail_back = mains[0], tails[0], mains[1], tails[1]
+    wide_rows = expert_input(main_rows.at[expert], tail_rows, select)
+    grads = expert_input(grad_main, grad_tail, select)
+    hidden, grad_gate, grad_up, back, result = expert_math(
+        wide_rows, grads, gate_weight[0], up_weight[0], down_weight[0]
+    )
+    hidden_ref[0] = hidden
+    grad_gate_ref[0] = grad_gate
+    grad_up_ref[0] = grad_up
+    expert_output(back, select, expert, main_back.at[expert], tail_back)
+
+    for at in range(experts_here):
+
+        @pl.when(expert == at)
+        def _():
+            chunks[at].pair()
+            if at == experts_here - 1:
+                tail.pair()
+                chunks[at].middle()
+                tail.middle()
+            if at:
+                chunks[at - 1].last()
+
+    def result_copy(at):
+        place = pl.ds(pl.multiple_of(at * main_slots, main_slots), main_slots)
+        return pltpu.make_async_copy(result_main, result_ref.at[:, :, place], result_sems.at[0])
+
+    @pl.when(expert > 0)
+    def _():
+        result_copy(expert - 1).wait()
+
+    expert_output(result, select, expert, result_main, result_tail)
+    result_copy(expert).start()
+
+    @pl.when(expert == experts_here - 1)
+    def _():
+        place = pl.ds(experts_here * main_slots, tail_height)
+        side = pltpu.make_async_copy(result_tail, result_ref.at[:, :, place], result_sems.at[1])
+        side.start()
+        chunks[-1].last()
+        tail.last()
+        for chunk in chunks + [tail]:
+            chunk.finish()
+        result_copy(expert).wait()
+        side.wait()
+
+
+def experts(rows, grads, gate_weight, up_weight, down_weight, columns):
+    experts_here, units, width = gate_weight.shape
+    groups, height, wide = rows.shape
+    half = columns // 2
+    count = columns * groups * CAP
+    tail_height = height - experts_here * main_slots
+    weight_spec = pl.BlockSpec((1, units, width), lambda e: (e, 0, 0))
+    act_spec = pl.BlockSpec((1, count, units), lambda e: (e, 0, 0))
+    act_shape = jax.ShapeDtypeStruct((experts_here, count, units), jnp.bfloat16)
+    low = lambda *shape: pltpu.VMEM(shape, jnp.bfloat16)
+    bufs = lambda lead, rows_of: [
+        low(*lead, columns, groups, rows_of, wide),
+        low(*lead, columns, groups, rows_of, wide),
+        low(*lead, half, groups, rows_of, wide),
+        low(*lead, half, groups, rows_of, wide),
+        low(*lead, half, groups, rows_of, wide),
+        low(*lead, groups, rows_of, wide),
+    ]
+    return pl.pallas_call(
+        functools.partial(experts_kernel, experts_here, groups, columns),
+        grid=(experts_here,),
+        out_shape=(
+            act_shape,
+            act_shape,
+            act_shape,
+            jax.ShapeDtypeStruct((columns, groups, height, width), jnp.bfloat16),
+            jax.ShapeDtypeStruct((columns,) + rows.shape, jnp.bfloat16),
+            jax.ShapeDtypeStruct(rows.shape, jnp.bfloat16),
+        ),
+        in_specs=[anywhere]
+        + row_specs(grads, experts_here, lambda index: lambda e: index(e, 0))
+        + [weight_spec] * 3,
+        out_specs=(act_spec, act_spec, act_spec, anywhere, anywhere, anywhere),
+        scratch_shapes=[
+            low(columns, groups, main_slots, width),
+            low(columns, groups, tail_height, width),
+            pltpu.SemaphoreType.DMA((2,)),
+        ]
+        + bufs((experts_here,), main_slots)
+        + bufs((), tail_height)
+        + RowChunk.sems(groups, columns, experts_here + 1),
+        compiler_params=comm_params(10, 60),
+        cost_estimate=pl.CostEstimate(
+            flops=12 * experts_here * count * width * units,
+            transcendentals=experts_here * count * units,
+            bytes_accessed=6 * experts_here * width * units + 8 * experts_here * count * width,
+        ),
+        name="experts",
+    )(rows, grads, grads, gate_weight, up_weight, down_weight)
+
+
 def expert_weight_kernel(
     parts,
-    groups,
-    columns,
-    chunks,
     row_main,
     row_tail,
     grad_main,
@@ -1415,35 +1788,11 @@
     hidden_ref,
     grad_gate_ref,
     grad_up_ref,
-    grads_qkv,
-    grads_own,
-    piece,
-    qkv_rows,
     gate_out,
     up_out,
     down_out,
-    grads_out,
-    sum_all,
-    piece_all,
-    qkv_all,
-    *scratch,
 ):
     expert, part = pl.program_id(0), pl.program_id(1)
-    steps = EXPERTS // groups * parts
-    now = expert * parts + part
-    spot = Spot(groups, columns)
-    tail = Tail(
-        spot,
-        chunks,
-        (grads_qkv, grads_own, piece, qkv_rows, grads_out, sum_all, piece_all, qkv_all),
-        scratch,
-    )
-
-    @pl.when(now == 0)
-    def _():
-        spot.meet()
-        tail.begin()
-
     sources = row_main.shape[0] * row_main.shape[1]
     select = tail_select(expert, sources, row_tail.shape[2])
     wide_rows = expert_input(row_main, row_tail, select)
@@ -1465,30 +1814,8 @@
             up_out[0] += tn_dot(grad_up_ref[0], rows)
             down_out[0] += tn_dot(hidden_ref[0], grad_low)
 
-    @pl.when(now == 0)
-    def _():
-        tail.gather()
-
-    @pl.when(now == steps // 2)
-    def _():
-        tail.hop(1)
-
-    @pl.when(now == steps - 1)
-    def _():
-        tail.hop(2)
-        tail.hop(3)
-        tail.finish()
-
-
-def expert_weight_grads(
-    rows, grads, hidden, grad_gate, grad_up, grads_qkv, grads_own, piece, qkv_rows
-):
-    groups, row_count, thirds = grads_qkv.shape
-    apart = thirds // 3 % 128 != 0
-    grads_shape = grads_qkv.shape if apart else (row_count, thirds * groups)
-    columns, chunks = grads_own.shape[:2]
-    block = grads_own.shape[2:]
-    shape_of = lambda shape: jax.ShapeDtypeStruct(shape, jnp.bfloat16)
+
+def expert_weight_grads(rows, grads, hidden, grad_gate, grad_up):
     experts_here, count, units = hidden.shape
     width = grads.shape[-1]
     parts = parts_of(rows)
@@ -1497,43 +1824,21 @@
     out_spec = pl.BlockSpec((1, units, width), lambda e, c: (e, 0, 0))
     out_shape = jax.ShapeDtypeStruct((experts_here, units, width), jnp.float32)
     return pl.pallas_call(
-        functools.partial(expert_weight_kernel, parts, groups, columns, chunks),
+        functools.partial(expert_weight_kernel, parts),
         grid=(experts_here, parts),
-        out_shape=(
-            out_shape,
-            out_shape,
-            out_shape,
-            shape_of(grads_shape),
-            shape_of((groups, chunks) + block),
-            shape_of((groups,) + piece.shape),
-            shape_of((columns,) + qkv_rows.shape),
-        ),
+        out_shape=(out_shape, out_shape, out_shape),
         in_specs=row_specs(rows, experts_here, order)
         + row_specs(grads, experts_here, order)
-        + [act_spec] * 3
-        + [anywhere] * 4,
-        out_specs=(out_spec, out_spec, out_spec) + (anywhere,) * 4,
-        scratch_shapes=Tail.scratch(columns, groups, chunks, block, 1 if apart else 3),
-        compiler_params=comm_params(7, 60),
+        + [act_spec] * 3,
+        out_specs=(out_spec, out_spec, out_spec),
+        compiler_params=pltpu.CompilerParams(vmem_limit_bytes=60 * mega),
         cost_estimate=pl.CostEstimate(
             flops=6 * experts_here * count * width * units,
             transcendentals=0,
             bytes_accessed=12 * experts_here * width * units + 10 * experts_here * count * width,
         ),
         name="expert_weight_grads",
-    )(
-        rows,
-        rows,
-        grads,
-        grads,
-        hidden,
-        grad_gate,
-        grad_up,
-        grads_qkv,
-        grads_own,
-        piece,
-        qkv_rows,
-    )
+    )(rows, rows, grads, grads, hidden, grad_gate, grad_up)
 
 
 def pair_slots(token_routes, ranks, experts_here):
@@ -1674,14 +1979,21 @@
         axis=2,
     ).reshape(TOP * row_count, D + spare)
     outgoing = nn_dot(slot_pairs, wide_rows).astype(jnp.bfloat16)
-    rows_received = dispatch(outgoing.reshape(groups, height, D + spare), columns_of, 2)
+    outgoing = outgoing.reshape(groups, height, D + spare)
     gate_across, up_across, down_across = (
         jnp.transpose(weight, (0, 2, 1)) for weight in (gate_weight, up_weight, down_weight)
     )
-    hidden, grad_gate, grad_up, result_part, back_part = expert_act(
-        rows_received, grads_received, gate_across, up_across, down_across
-    )
-    grad_returned = collect(back_part, 3).reshape(groups * height, D + spare)
+    if columns_of * groups <= part_sources:
+        hidden, grad_gate, grad_up, result_part, rows_received, grad_returned = experts(
+            outgoing, grads_received, gate_across, up_across, down_across, columns_of
+        )
+    else:
+        rows_received = dispatch(outgoing, columns_of, 2)
+        hidden, grad_gate, grad_up, result_part, back_part = expert_act(
+            rows_received, grads_received, gate_across, up_across, down_across
+        )
+        grad_returned = collect(back_part, 3)
+    grad_returned = grad_returned.reshape(groups * height, D + spare)
     grad_low_two = tn_dot(slot_any, grad_returned[:, :D])
     grad_gates = jnp.transpose(
         tn_dot(slot_pairs, grad_returned[:, D:])[:, 0].reshape(TOP, row_count)
@@ -1696,12 +2008,16 @@
     low_middle = grad_middle.astype(jnp.bfloat16)
     out_grad = tn_dot(attended, low_middle)
     grad_attended = nt_dot(low_middle, out_full).astype(jnp.bfloat16)
-    grad_mixed, out_sums = exchange_grad_mixed(
-        grad_attended,
-        out_grad.astype(jnp.bfloat16).reshape(columns_of, groups, shard_rows // groups, D),
-        groups,
-        9,
-    )
+    grad_attended = jnp.transpose(grad_attended.reshape(row_count, groups, width), (1, 0, 2))
+    grad_mixed = lax.all_to_all(
+        grad_attended, "expert", split_axis=0, concat_axis=0, tiled=True
+    )
+    gate_grad, up_grad, down_grad = expert_weight_grads(
+        rows_received, grads_received, hidden, grad_gate, grad_up
+    )
+    out_sums = lax.psum_scatter(
+        out_grad.astype(jnp.bfloat16), "shard", scatter_dimension=0, tiled=True
+    ).reshape(groups, shard_rows // groups, D)
     grad_qkv, near_sums, side_sums, returned, out_piece = attend_backward(
         prefix,
         far_bias,
@@ -1735,12 +2051,9 @@
         ((0, 0), (0, shard_rows - table_rows * heads_here)),
     ).reshape(D, 1)
 
-    own_grad = tn_dot(normed_all, grad_qkv)
-    gain_part = jnp.sum(own_grad * own_weight.astype(jnp.float32), axis=1) / gain_attn
-    last_pack = jnp.concatenate(
+    extra = jnp.concatenate(
         [
-            own_grad,
-            gain_part[:, None],
+            jnp.zeros((D, 1), jnp.float32),
             table_column,
             gain_moe_grad[:, None],
             router_grad,
@@ -1748,19 +2061,16 @@
         ],
         axis=1,
     ).astype(jnp.bfloat16)
-    chunks = 2
-    gate_grad, up_grad, down_grad, grad_projected, last_all, out_all, qkv_full = (
-        expert_weight_grads(
-            rows_received,
-            grads_received,
-            hidden,
-            grad_gate,
-            grad_up,
-            grad_qkv.reshape(groups, row_count, 3 * width),
-            last_pack.reshape(columns_of, chunks, shard_rows // chunks, 3 * width + spare),
-            out_piece,
-            qkv_weight,
-        )
+    grad_projected, last_all, out_all, qkv_full = tail_exchange(
+        grad_qkv.reshape(groups, row_count, 3 * width),
+        normed_all,
+        own_weight,
+        gain_attn[:, None],
+        extra,
+        out_piece,
+        qkv_weight,
+        columns_of,
+        7,
     )
     qkv_full = qkv_full.reshape(D, 3 * D)
     out_total = out_all.reshape(shard_rows, D).astype(jnp.float32)

time: 521 us -> 468 us (0.90)
  local copies, waits for them, and re-layouts: 65.4 us -> 30.8 us
  Pallas kernels: 394 us -> 363 us
  between operations: 3.15 us -> 16.6 us
  matrix products: 34.4 us -> 24.3 us
    pallas_call x5 -> x3, Pallas kernels: 227 us -> 194 us  [the longest x1 100 us: experts(): pl.pallas_call(functools.partial(experts_kernel, experts_here, groups, co...]
    unnamed x80 -> x68, local copies, waits for them, and re-layouts: 50.4 us -> 18.2 us
    dot_general x6 -> x5, matrix products: 14.3 us -> 8.84 us  [tn_dot(): lax.dot_general(left, right, (((0,), (0,)), ((), ())), preferred_element_...]
  transfers between devices with their start and end apart: 0 -> 2, of which waited for: 0 -> 0; matrix products, arithmetic and copies ran while one was open for 0% -> 1% of each run, Pallas kernels for 0% -> 5%
where the time goes in v2:
time: 468 us; the launch traced here: 458 us
  Pallas kernels  363 us (78%)
  local copies, waits for them, and re-layouts  30.8 us (7%)
  matrix products  24.3 us (5%)
  other arithmetic  18.5 us (4%)
  between operations  16.6 us (4%)
  starting transfers between devices  4.79 us (1%)
    pallas_call x1, Pallas kernels, experts(): pl.pallas_call(functools.partial(experts_kernel, experts_here, groups, co...  100 us
    pallas_call x1, Pallas kernels, tail_exchange(): pl.pallas_call(functools.partial(tail_kernel, groups, columns, chunks), o...  71 us
    pallas_call x1, Pallas kernels, attend_backward(): pl.pallas_call(functools.partial(attend_backward_kernel, heads_here, grou...  55.9 us
    pallas_call x1, Pallas kernels, entry_gather(): pl.pallas_call(functools.partial(entry_kernel, groups, columns, count), o...  55.2 us
    pallas_call x1, Pallas kernels, attend_forward(): pl.pallas_call(functools.partial(attend_forward_kernel, heads_here, group...  40.4 us
    pallas_call x1, Pallas kernels, expert_weight_grads(): pl.pallas_call(functools.partial(expert_weight_kernel, parts), grid=(expe...  22.3 us
    unnamed x68, local copies, waits for them, and re-layouts  18.2 us
    pallas_call x1, Pallas kernels, exchange_mixed(): pl.pallas_call(functools.partial(mixed_kernel, groups, columns), out_shap...  14.4 us
  transfers between devices with their start and end apart: 2, of which 0 were waited for; matrix products, arithmetic and copies ran while one was open for 1% of the time, Pallas kernels for 5%

profile of v2, /device:TPU:0, one launch (start us, length us, event | category | flops | bytes accessed | tf_op | source)
XLA Modules:
  0.0 458.3 jit_solution(15269208927688052037)
XLA Ops:
  7.2 0.7 broadcast_add_fusion
  7.9 0.8 slice_bitcast_fusion.3
  8.7 0.7 pad_add_fusion
  9.4 0.3 convert_reduce_fusion
  9.7 0.8 reshape.474
  10.6 0.8 broadcast_in_dim.135
  11.4 0.8 broadcast_in_dim.136
  12.2 0.8 copy.154
  13.0 1.7 copy.152
  15.1 1.0 copy-done.1
  16.2 1.0 copy-done.6
  17.2 55.2 %entry_gather.1 = (bf16[8,256,1024]{2,1,0:T(8,128)(2,1)S(1)}, bf16[4,256,512]{2,1,0:T(8,128)(2,1)S(1)}, bf16[4,256,1024]{2,1,0:T(8,128)(2,1)S(1)}) custom-call(bf16[256,1024]{1,0:T(8,128)(2,1)S(1)} %bitcast.128, bf16[256,512]{1,0:T(8,128)(2,1)S(1)} %concatenate.46.refs_1_, bf16[256,1024]{1,0:T(8,128)(2,1)S(1)} %copy-done.6), custom_call_target="tpu_custom_call" | custom-call | tf_op jit(solution)/shard_map/entry_gather/pallas_call | solution.py:278
  72.4 2.0 copy-done
  74.4 0.4 convert_reduce_fusion.1
  74.8 1.0 slice_convert_fusion.1
  76.7 3.1 multiply_reduce_fusion
  80.0 0.4 convolution_multiply_fusion
  80.7 2.8 fusion.1.normed
  83.5 1.9 copy-done.18
  85.5 2.3 convolution_convert_fusion.1.qkv_ref
  87.9 0.5 convolution_convert_fusion.3
  88.4 40.4 %attend_forward.1 = (bf16[2048,128]{1,0:T(8,128)(2,1)S(1)}, f32[8,2,256]{2,1,0:T(2,128)S(1)}, bf16[4,8,72,1024]{3,2,1,0:T(8,128)(2,1)S(1)}) custom-call(s32[1]{0:T(128)S(6)} %copy.181.prefix_ref, f32[2,2]{1,0:T(2,128)S(1)} %maximum_multiply_fusion.far_ref, f32[6,512]{1,0:T(8,128)S(1)} %reshape.477.base_ref, ...), custom_call_target="tpu_custom_call" | custom-call | flops 21474836480 | bytes 2097152 | tf_op jit(solution)/shard_map/attend_forward/pallas_call | solution.py:969
  128.8 2.2 copy-done.10
  131.0 14.4 %exchange_mixed.1 = bf16[256,1024]{1,0:T(8,128)(2,1)S(1)} custom-call(bf16[8,256,128]{2,1,0:T(8,128)(2,1)S(1)} %bitcast.130), custom_call_target="tpu_custom_call" | custom-call | tf_op jit(solution)/shard_map/exchange_mixed/pallas_call | solution.py:617
  145.5 0.8 multiply_reduce_fusion.3
  146.4 1.0 copy-done.13
  147.5 0.8 copy-done.19
  148.3 0.3 fusion.58
  148.9 1.2 broadcast_in_dim.116
  150.2 2.0 convolution_convert_fusion
  152.2 100.4 %experts.1 = (bf16[4,576,704]{2,1,0:T(8,128)(2,1)}, bf16[4,576,704]{2,1,0:T(8,128)(2,1)}, bf16[4,576,704]{2,1,0:T(8,128)(2,1)}, bf16[4,8,72,1024]{3,2,1,0:T(8,12...) custom-call(bf16[8,72,1152]{2,1,0:T(8,128)(2,1)} %bitcast.166, ...), custom_call_target="tpu_custom_call" | custom-call | flops 19931332608 | bytes 36175872 | tf_op jit(solution)/shard_map/experts/pallas_call | solution.py:1749
  252.7 1.2 fusion.10
  253.9 2.9 fusion.5
  256.8 0.6 fusion.57
  258.4 0.7 negate_add_fusion
  259.1 2.1 multiply_reduce_fusion.1
  261.3 0.3 fusion.14
  261.6 1.0 copy-done.16
  262.6 2.1 convolution_convert_fusion.2
  264.7 2.0 fusion.3
  266.7 0.9 copy.180
  267.5 4.7 %all-to-all-start = ((bf16[8,256,128]{2,1,0:T(8,128)(2,1)}), bf16[8,256,128]{2,1,0:T(8,128)(2,1)S(1)}, u32[]{:S(2)}, u32[]{:S(2)}) async-start(bf16[8,256,128]{2,1,0:T(8,128)(2,1)} %bitcast.119), calls=%async_computation | async-start | bytes 1048576 | tf_op jit(solution)/shard_map/all_to_all | solution.py:2012
  272.3 1.0 slice.119.own_weight
  273.3 0.2 convolution_convert_fusion.5
  273.9 22.3 %expert_weight_grads.1 = (f32[4,704,1024]{2,1,0:T(8,128)}, f32[4,704,1024]{2,1,0:T(8,128)}, f32[4,704,1024]{2,1,0:T(8,128)}) custom-call(bf16[4,8,72,1152]{3,2,1,0:T(8,128)(2,1)} %get-tuple-element.52.row_main.row_tail, bf16[4,8,72,1152]{3,2,1,0:T(8,128)(2,1)} %get-tuple-element.52.row_main.row_tail, bf16[4,8,72,1024]{3,2,1,0:T(8,128)(2,1)} %copy-done.10, ...), custom_call_target="tpu_custom_call" | custom-call | flops 9965666304 | bytes 58195968 | tf_op jit(solution)/shard_map/expert_weight_grads/pallas_call | solution.py:1826
  296.2 0.8 copy-done.23
  297.0 55.9 %attend_backward.1 = (bf16[2048,384]{1,0:T(8,128)(2,1)}, f32[6,512]{1,0:T(8,128)}, f32[2,2,8,256]{3,2,1,0:T(8,128)}, bf16[8,72,1024]{2,1,0:T(8,128)(2,1)}, bf16[32,1024]{1,0:T(8,128)(2,1)}) custom-call(s32[1]{0:T(128)S(6)} %copy.181.prefix_ref, f32[2,2]{1,0:T(2,128)} %copy-done.9, f32[6,512]{1,0:T(8,128)} %copy-done.8, bf16[2048,384]{1,0:T(8,128)(2,1)} %copy-done.11, ...), custom_call_target="tpu_custom_call" | custom-call | flops 37580963840 | bytes 4194304 | tf_op jit(solution)/shard_map/attend_backward/pallas_call | solution.py:1192
  352.9 0.9 reduce_sum.195
  353.9 0.7 reshape.493
  355.4 1.5 concatenate.54.extra
  356.9 71.0 %tail_exchange.1 = (bf16[256,3072]{1,0:T(8,128)(2,1)}, bf16[8,2,128,512]{3,2,1,0:T(8,128)(2,1)}, bf16[8,32,1024]{2,1,0:T(8,128)(2,1)}, bf16[4,256,3072]{2,1,0:T(8,128)(2,1)}) custom-call(bf16[8,256,384]{2,1,0:T(8,128)(2,1)} %bitcast.135, bf16[2048,1024]{1,0:T(8,128)(2,1)} %copy-done.18, bf16[1024,384]{1,0:T(8,128)(2,1)} %slice.119.own_weight, ...), custom_call_target="tpu_custom_call" | custom-call | tf_op jit(solution)/shard_map/tail_exchange/pallas_call | solution.py:740
  427.8 1.1 fusion.33
  429.0 0.8 slice_reduce_fusion.1
  429.9 2.1 slice_convert_fusion
  432.0 3.7 unpack_columns.1
  435.7 2.4 fusion.7
  438.2 4.8 %fusion.17 = (f32[256]{0:T(256)S(1)}, f32[256]{0:T(256)S(1)}, f32[256,1024]{1,0:T(8,128)S(1)}) fusion(bf16[256,1,1024]{2,0,1:T(8,128)(2,1)S(1)} %copy-done.3, f32[1024]{0:T(1024)S(1)} %get-tuple-element.139, bf16[256,3072]{1,0:T(8,128)(2,1)S(1)} %copy-done.26, bf16[1024,3072]{1,0:T(8,128)(2,1)} %bitcast.156), kind=kOutput, calls=%fused_computation.38 | convolution fusion | flops 1612185088 | bytes 9443328 | tf_op jit(solution)/shard_map/dot_general | solution.py:809
  443.0 0.3 fusion.16
  443.3 2.0 copy.169
  445.4 0.7 copy.171
  446.0 0.9 slice.133
  447.2 0.7 copy.170
  447.9 2.1 bitcast_convert_fusion
  450.0 1.0 fusion.25
  (115 shorter events, 4.0 us)
Async XLA Ops:
  7.2 289.0 %reduce-scatter.2.cloned.1.call-start = ((), (), s32[]{:S(2)}) async-start(), calls=%async_computation.2 | async-start | bytes 2621440 | tf_op jit(solution)/shard_map/reduce_scatter | solution.py:2018
  15.1 1.0 copy-start.1
  16.2 1.0 copy-start.6
  72.4 2.0 copy-start
  76.7 3.3 copy-start.28
  80.5 7.9 %copy-start.8 = (f32[6,512]{1,0:T(8,128)}, f32[6,512]{1,0:T(8,128)S(1)}, u32[]{:S(2)}) copy-start(f32[6,512]{1,0:T(8,128)S(1)} %reshape.477.base_ref) | copy-start | bytes 36868
  83.5 2.0 copy-start.18
  85.5 2.4 copy-start.21
  87.8 40.9 %copy-start.11 = (bf16[2048,384]{1,0:T(8,128)(2,1)}, bf16[2048,384]{1,0:T(8,128)(2,1)S(1)}, u32[]{:S(2)}) copy-start(bf16[2048,384]{1,0:T(8,128)(2,1)S(1)} %convolution_convert_fusion.1.qkv_ref) | copy-start | bytes 4718596
  88.4 40.4 %copy-start.9 = (f32[2,2]{1,0:T(2,128)}, f32[2,2]{1,0:T(2,128)S(1)}, u32[]{:S(2)}) copy-start(f32[2,2]{1,0:T(2,128)S(1)} %maximum_multiply_fusion.far_ref) | copy-start | bytes 52
  88.4 57.1 %copy-start.2 = (bf16[256,1,1024]{2,0,1:T(8,128)(2,1)S(1)}, bf16[256,1,1024]{2,0,1:T(8,128)(2,1)}, u32[]{:S(2)}) copy-start(bf16[256,1,1024]{2,0,1:T(8,128)(2,1)} %param.16) | copy-start | bytes 1572868
  128.8 2.2 copy-start.10
  131.0 15.3 %copy-start.7 = (bf16[2048,128]{1,0:T(8,128)(2,1)}, bf16[2048,128]{1,0:T(8,128)(2,1)S(1)}, u32[]{:S(2)}) copy-start(bf16[2048,128]{1,0:T(8,128)(2,1)S(1)} %get-tuple-element.37.mixed_ref) | copy-start | bytes 1572868
  131.0 15.3 %copy-start.12 = (f32[8,2,256]{2,1,0:T(2,128)}, f32[8,2,256]{2,1,0:T(2,128)S(1)}, u32[]{:S(2)}) copy-start(f32[8,2,256]{2,1,0:T(2,128)S(1)} %get-tuple-element.41.totals_ref) | copy-start | bytes 49156
  145.5 0.9 copy-start.4
  146.3 1.0 copy-start.13
  146.3 2.3 copy-start.24
  147.5 0.8 copy-start.19
  252.7 4.1 copy-start.25
  257.4 3.9 copy-start.14
  257.4 3.9 copy-start.22
  261.2 1.3 copy-start.5
  261.6 1.0 copy-start.16
  266.6 6.6 %copy-start.20 = (bf16[256,1024]{1,0:T(8,128)(2,1)S(1)}, bf16[256,1024]{1,0:T(8,128)(2,1)}, u32[]{:S(2)}) copy-start(bf16[256,1024]{1,0:T(8,128)(2,1)} %copy-done.19) | copy-start | bytes 1572868
  267.5 28.6 %all-to-all-start = ((bf16[8,256,128]{2,1,0:T(8,128)(2,1)}), bf16[8,256,128]{2,1,0:T(8,128)(2,1)S(1)}, u32[]{:S(2)}, u32[]{:S(2)}) async-start(bf16[8,256,128]{2,1,0:T(8,128)(2,1)} %bitcast.119), calls=%async_computation | async-start | bytes 1048576 | tf_op jit(solution)/shard_map/all_to_all | solution.py:2012
  296.2 0.8 copy-start.23
  297.0 57.7 %copy-start.27 = (s32[3,512]{1,0:T(4,128)S(1)}, s32[3,512]{1,0:T(4,128)}, u32[]{:S(2)}) copy-start(s32[3,512]{1,0:T(4,128)} %constant.115) | copy-start | bytes 18436
  435.7 2.5 copy-start.3
  435.7 2.5 copy-start.26
  438.2 4.8 %copy-start.17 = (f32[256,1024]{1,0:T(8,128)S(1)}, f32[256,1024]{1,0:T(8,128)}, u32[]{:S(2)}) copy-start(f32[256,1024]{1,0:T(8,128)} %copy-done.16) | copy-start | bytes 3145732
  443.3 6.7 %copy-start.15 = (f32[256,1024]{1,0:T(8,128)S(1)}, f32[256,1024]{1,0:T(8,128)}, u32[]{:S(2)}) copy-start(f32[256,1024]{1,0:T(8,128)} %copy-done.13) | copy-start | bytes 3145732
Sparse Core Ops, SparseCore 0:
  264.8 30.6 reduce-scatter.1

commit v3 on v2

--- a/solution.py
+++ b/solution.py
@@ -43,6 +43,18 @@
     return out
 
 
+def near_keys(groups):
+    return list(range(1, groups // 2))
+
+
+def far_keys(groups):
+    return list(range(groups // 2, groups))
+
+
+def early_keys(groups):
+    return [key for key in far_keys(groups) if key % line_shape(groups)[1] == 0]
+
+
 class Spot:
     def __init__(self, groups, columns):
         self.groups, self.columns = groups, columns
@@ -159,10 +171,13 @@
             self.each(job, origin, self.full.at[origin], False, True, lambda copy: copy.start())
 
     def finish(self):
+        for row in range(self.long):
+            for step in range(1, self.wide):
+                self.arrive(row * self.wide + (self.y + step) % self.wide)
+        self.settle()
+
+    def settle(self):
         place, wide = self.spot.place, self.wide
-        for row in range(self.long):
-            for step in range(1, wide):
-                self.arrive(row * wide + (self.y + step) % wide)
         stop = lambda copy: copy.wait_send()
         self.each(0, place, self.own, True, True, stop)
         for k in range(1, self.long):
@@ -235,7 +250,7 @@
         pltpu.make_async_copy(self.own, self.full.at[self.spot.lane], self.local_sem).wait()
 
 
-def comm_params(which, limit=16):
+def comm_params(which, limit=60):
     return pltpu.CompilerParams(
         collective_id=which, has_side_effects=True, vmem_limit_bytes=limit * mega
     )
@@ -244,46 +259,160 @@
 anywhere = pl.BlockSpec(memory_space=pl.ANY)
 
 
-def entry_kernel(groups, columns, count, *refs):
-    tokens, refs = refs[0], refs[1:]
-    owns, refs = refs[:count], refs[count:]
-    tokens_all, refs = refs[0], refs[1:]
-    fulls, sems = refs[:count], refs[count:]
+def entry_kernel(
+    groups,
+    columns,
+    tokens,
+    gain,
+    pack,
+    out_weight,
+    rows,
+    tokens_all,
+    normed_all,
+    qkv_all,
+    pack_all,
+    out_all,
+    far_rows,
+    token_sc,
+    normed_sc,
+    qkv_sc,
+    gain_sc,
+    pack_sc,
+    token_sem,
+    normed_sems,
+    qkv_sems,
+    pack_sem,
+    *sems,
+):
     spot = Spot(groups, columns)
     line = LineGather(spot, tokens, tokens_all, *sems[:3])
-    across = [
-        ColumnGather(spot, owns[i], fulls[i], *sems[3 + 5 * i : 8 + 5 * i]) for i in range(count)
-    ]
+    gains = ColumnGather(spot, gain, gain_sc, *sems[3:8])
+    packs = ColumnGather(spot, pack, pack_sc, *sems[8:13])
+    outs = ColumnGather(spot, out_weight, out_all, *sems[13:18])
+    far_send, far_recv = sems[18:]
+    wide = qkv_sc.shape[2]
+
+    def far_copy(key):
+        peer = flip(spot.place, key)
+        return remote(
+            rows.at[peer],
+            far_rows.at[spot.place],
+            far_send.at[key],
+            far_recv.at[key],
+            (peer, spot.lane),
+        )
+
+    def stores(origin):
+        return (
+            pltpu.make_async_copy(
+                normed_sc.at[origin], normed_all.at[origin], normed_sems.at[origin]
+            ),
+            pltpu.make_async_copy(qkv_sc.at[origin], qkv_all.at[origin], qkv_sems.at[origin]),
+        )
+
+    def project(origin, source):
+        load = pltpu.make_async_copy(source, token_sc, token_sem)
+        load.start()
+        load.wait()
+        features = token_sc[...].astype(jnp.float32)
+        factor = lax.rsqrt(jnp.mean(features * features, axis=-1, keepdims=True) + epsilon)
+        gain_row = jnp.concatenate([gain_sc[at, 0:1, :] for at in range(columns)], axis=1)
+        normed = (features * factor * gain_row).astype(jnp.bfloat16)
+        normed_sc[origin] = normed
+        weight = pack_sc[...].reshape(D, -1)[:, :wide]
+        qkv_sc[origin] = nn_dot(normed, weight).astype(jnp.bfloat16)
+        for store in stores(origin):
+            store.start()
+
     spot.meet()
     line.begin()
-    for gather in across:
-        gather.begin()
-    for k in range(1, 4):
-        line.hop(k)
-        if k <= count:
-            across[k - 1].forward()
-    for gather in across[3:]:
-        gather.forward()
-    for gather in across:
-        gather.finish()
-    line.finish()
-
-
-def entry_gather(tokens, owns, groups, columns):
-    count = len(owns)
-    sems = LineGather.sems(groups) + ColumnGather.sems(columns) * count
-    shapes = [jax.ShapeDtypeStruct((groups,) + tokens.shape, tokens.dtype)] + [
-        jax.ShapeDtypeStruct((columns,) + own.shape, own.dtype) for own in owns
-    ]
+    gains.begin()
+    packs.begin()
+    outs.begin()
+    gains.forward()
+    packs.forward()
+    gains.finish()
+    packs.finish()
+    keep = pltpu.make_async_copy(pack_sc, pack_all, pack_sem)
+    keep.start()
+    project(spot.place, tokens)
+    line.hop(1)
+    outs.forward()
+    line.hop(2)
+    for key in early_keys(groups):
+        far_copy(key).start()
+    line.hop(3)
+
+    def own_column(row, carry):
+        @pl.when(row != line.z)
+        def _():
+            origin = row * line.wide + line.y
+            project(origin, tokens_all.at[origin])
+
+        return carry
+
+    lax.fori_loop(0, line.long, own_column, 0)
+
+    def other_column(at, carry):
+        row = line.z + ((at + 1) // 2) * (1 - 2 * (at % 2))
+
+        @pl.when((row >= 0) & (row < line.long))
+        def _():
+            for step in range(1, line.wide):
+                origin = row * line.wide + (line.y + step) % line.wide
+                line.arrive(origin)
+                project(origin, tokens_all.at[origin])
+
+        return carry
+
+    lax.fori_loop(0, 2 * line.long - 1, other_column, 0)
+    for key in early_keys(groups):
+        far_copy(key).wait_recv()
+    for key in early_keys(groups):
+        far_copy(key).wait_send()
+    line.settle()
+    outs.finish()
+    keep.wait()
+    for origin in range(groups):
+        for store in stores(origin):
+            store.wait()
+
+
+def entry_gather(tokens, gain, pack, out_weight, rows, wide, which):
+    groups = rows.shape[0]
+    columns = D // out_weight.shape[0]
+    count = tokens.shape[0]
+    low = lambda *shape: jax.ShapeDtypeStruct(shape, jnp.bfloat16)
+    dma = pltpu.SemaphoreType.DMA
     return pl.pallas_call(
-        functools.partial(entry_kernel, groups, columns, count),
-        out_shape=shapes,
-        in_specs=[anywhere] * (1 + count),
-        out_specs=[anywhere] * (1 + count),
-        scratch_shapes=sems,
-        compiler_params=comm_params(1),
+        functools.partial(entry_kernel, groups, columns),
+        out_shape=(
+            low(groups, *tokens.shape),
+            low(groups, *tokens.shape),
+            low(groups, count, wide),
+            low(columns, *pack.shape),
+            low(columns, *out_weight.shape),
+            low(*rows.shape),
+        ),
+        in_specs=[anywhere] * 5,
+        out_specs=(anywhere,) * 6,
+        scratch_shapes=[
+            pltpu.VMEM(tokens.shape, jnp.bfloat16),
+            pltpu.VMEM((groups,) + tokens.shape, jnp.bfloat16),
+            pltpu.VMEM((groups, count, wide), jnp.bfloat16),
+            pltpu.VMEM((columns,) + gain.shape, jnp.float32),
+            pltpu.VMEM((columns,) + pack.shape, jnp.bfloat16),
+            dma(()),
+            dma((groups,)),
+            dma((groups,)),
+            dma(()),
+        ]
+        + LineGather.sems(groups)
+        + ColumnGather.sems(columns) * 3
+        + [dma((groups,))] * 2,
+        compiler_params=comm_params(which),
         name="entry_gather",
-    )(tokens, *owns)
+    )(tokens, gain, pack, out_weight, rows)
 
 
 class Dispatch:
@@ -340,14 +469,10 @@
         )
 
     def begin(self):
+        groups = self.spot.groups
         self.own().start()
-        for key in range(1, self.spot.groups):
+        for key in far_keys(groups) + near_keys(groups):
             self.swap(key).start()
-
-    def pass_on(self, key):
-        for step in range(1, self.spot.half):
-            self.across(key, step).wait_recv()
-            self.core(key, step).start()
 
     def advance(self, key):
         if key == 0:
@@ -357,12 +482,14 @@
         for step in range(1, self.spot.half):
             self.across(key, step).start()
         self.core(key, 0).start()
-        if key > 0:
-            self.pass_on(key - 1)
+
+    def pass_on(self, key):
+        for step in range(1, self.spot.half):
+            self.across(key, step).wait_recv()
+            self.core(key, step).start()
 
     def finish(self):
         groups, half = self.spot.groups, self.spot.half
-        self.pass_on(groups - 1)
         for key in range(groups):
             for step in range(half):
                 self.core(key, step).wait_recv()
@@ -382,6 +509,9 @@
     job.begin()
     for key in range(groups):
         job.advance(key)
+        if key:
+            job.pass_on(key - 1)
+    job.pass_on(groups - 1)
     job.finish()
 
 
@@ -428,7 +558,8 @@
             self.copy(key, third).start()
 
     def begin(self):
-        for key in range(self.spot.groups):
+        groups = self.spot.groups
+        for key in far_keys(groups) + near_keys(groups) + [0]:
             self.start(key)
 
     def arrive(self):
@@ -518,8 +649,14 @@
 class Collect:
     def __init__(self, spot, part, out, scratch):
         self.spot, self.total = spot, scratch[9]
+        self.keys = far_keys(spot.groups) + near_keys(spot.groups) + [0]
         self.sums = ColumnSum(
-            spot, spot.groups, lambda k: flip(spot.place, k), part, scratch[:4], scratch[4:9]
+            spot,
+            spot.groups,
+            lambda k: flip(spot.place, self.keys[k]),
+            part,
+            scratch[:4],
+            scratch[4:9],
         )
         self.out = out
         self.local, self.send, self.recv = scratch[10:]
@@ -533,14 +670,14 @@
             + [pltpu.SemaphoreType.DMA((groups,))] * 2
         )
 
-    def copy(self, key):
-        spot = self.spot
+    def copy(self, k):
+        spot, key = self.spot, self.keys[k]
         target = self.out.at[spot.place]
         if key == 0:
-            return pltpu.make_async_copy(self.total.at[0], target, self.local)
+            return pltpu.make_async_copy(self.total.at[k], target, self.local)
         peer = flip(spot.place, key)
         return remote(
-            self.total.at[key], target, self.send.at[key], self.recv.at[key], (peer, spot.lane)
+            self.total.at[k], target, self.send.at[k], self.recv.at[k], (peer, spot.lane)
         )
 
     def begin(self):
@@ -554,11 +691,12 @@
         self.copy(key).start()
 
     def finish(self):
-        for key in range(1, self.spot.groups):
-            self.copy(key).wait_recv()
-        for key in range(1, self.spot.groups):
-            self.copy(key).wait_send()
-        self.copy(0).wait()
+        last = self.spot.groups - 1
+        for k in range(last):
+            self.copy(k).wait_recv()
+        for k in range(last):
+            self.copy(k).wait_send()
+        self.copy(last).wait()
         self.sums.finish()
 
 
@@ -586,7 +724,7 @@
         in_specs=[anywhere],
         out_specs=anywhere,
         scratch_shapes=Collect.scratch(columns, groups, block),
-        compiler_params=comm_params(which, 56),
+        compiler_params=comm_params(which),
         name="collect_rows",
     )(part)
 
@@ -692,9 +830,12 @@
     ]
     for load in loads:
         load.start()
+    far = far_keys(groups)
+    early, late = far[: len(far) // 2], far[len(far) // 2 :]
     spot.meet()
     tail.side.begin()
-    tail.swap.begin()
+    for key in early + near_keys(groups) + [0]:
+        tail.swap.start(key)
     for load in loads:
         load.wait()
     all_grads = grads_sc[...].reshape(-1, wide)
@@ -719,8 +860,10 @@
     tail.line.hop(1)
     tail.side.hop(3)
     tail.line.hop(2)
+    for key in late:
+        tail.swap.start(key)
+    tail.line.hop(3)
     tail.column.forward()
-    tail.line.hop(3)
     tail.side.finish()
     tail.swap.arrive()
     tail.line.finish()
@@ -754,29 +897,87 @@
             pltpu.VMEM((columns, chunks) + block, jnp.bfloat16),
         ]
         + Tail.scratch(columns, groups, chunks, block, 1 if apart else 3),
-        compiler_params=comm_params(which, 56),
+        compiler_params=comm_params(which),
         name="tail_exchange",
     )(grads, normed, own_weight, gains, extra, piece, weight)
 
 
-def unpack_kernel(width, packed, out):
+def finish_kernel(
+    width,
+    grads,
+    weight,
+    packed,
+    packed_extra,
+    tokens,
+    gain,
+    grad_middle,
+    out_low,
+    input_grad,
+    qkv_grad,
+    out_grad,
+    extra,
+    total_sc,
+):
+    third = pl.program_id(0)
     for group in range(packed.shape[0]):
-        out[:, group * width : (group + 1) * width] = packed[group].astype(jnp.float32)
-
-
-def unpack_columns(packed, width):
-    groups, rows = packed.shape[:2]
-    if width % 128:
-        blocks = packed[:, :, : 3 * width].reshape(groups, rows, 3, width).astype(jnp.float32)
-        return jnp.transpose(blocks, (1, 2, 0, 3)).reshape(rows, 3 * groups * width)
+        qkv_grad[:, group * width : (group + 1) * width] = packed[group].astype(jnp.float32)
+    part = nt_dot(grads[...], weight[...].reshape(D, -1))
+
+    @pl.when(third == 0)
+    def _():
+        total_sc[...] = part
+
+    @pl.when(third > 0)
+    def _():
+        total_sc[...] += part
+
+    @pl.when(third == 2)
+    def _():
+        features = tokens[...].astype(jnp.float32)
+        factor = lax.rsqrt(jnp.mean(features * features, axis=-1, keepdims=True) + epsilon)
+        unit = features * factor
+        scaled = total_sc[...] * gain[...]
+        inner = jnp.mean(scaled * unit, axis=-1, keepdims=True)
+        input_grad[...] = grad_middle[...] + factor * (scaled - unit * inner)
+        out_grad[...] = out_low[...].astype(jnp.float32)
+        extra[...] = jnp.sum(packed_extra[...].astype(jnp.float32), axis=0)
+
+
+def finish(grads, weight, packed, tokens, gain, grad_middle, out_low, width):
+    groups, shard_rows = packed.shape[:2]
+    columns = weight.shape[0]
+    rows = grads.shape[0]
+    whole = lambda t: (0, 0)
+    full = jax.ShapeDtypeStruct((rows, D), jnp.float32)
     return pl.pallas_call(
-        functools.partial(unpack_kernel, width),
+        functools.partial(finish_kernel, width),
         grid=(3,),
-        out_shape=jax.ShapeDtypeStruct((rows, 3 * groups * width), jnp.float32),
-        in_specs=[pl.BlockSpec((groups, rows, width), lambda t: (0, 0, t))],
-        out_specs=pl.BlockSpec((rows, groups * width), lambda t: (0, t)),
-        name="unpack_columns",
-    )(packed)
+        out_shape=(
+            full,
+            jax.ShapeDtypeStruct((shard_rows, 3 * D), jnp.float32),
+            jax.ShapeDtypeStruct((shard_rows, D), jnp.float32),
+            jax.ShapeDtypeStruct((shard_rows, spare), jnp.float32),
+        ),
+        in_specs=[
+            pl.BlockSpec((rows, D), lambda t: (0, t)),
+            pl.BlockSpec((columns, shard_rows, D), lambda t: (0, 0, t)),
+            pl.BlockSpec((groups, shard_rows, width), lambda t: (0, 0, t)),
+            pl.BlockSpec((groups, shard_rows, spare), lambda t: (0, 0, 3 * width // spare)),
+            pl.BlockSpec((rows, D), whole),
+            pl.BlockSpec((1, D), whole),
+            pl.BlockSpec((rows, D), whole),
+            pl.BlockSpec((shard_rows, D), whole),
+        ],
+        out_specs=(
+            pl.BlockSpec((rows, D), whole),
+            pl.BlockSpec((shard_rows, D), lambda t: (0, t)),
+            pl.BlockSpec((shard_rows, D), whole),
+            pl.BlockSpec((shard_rows, spare), whole),
+        ),
+        scratch_shapes=[pltpu.VMEM((rows, D), jnp.float32)],
+        compiler_params=pltpu.CompilerParams(vmem_limit_bytes=60 * mega),
+        name="finish",
+    )(grads, weight, packed, packed, tokens, gain, grad_middle, out_low)
 
 
 def rms_norm(features, scales):
@@ -849,6 +1050,104 @@
     return (key_pos <= query_pos) | (key_pos < prefix_length)
 
 
+class Spread:
+    def __init__(self, spot, rows, far_rows, full, sems):
+        self.spot, self.rows, self.far_rows, self.full = spot, rows, far_rows, full
+        self.local, self.send, self.recv = sems[:3]
+        self.across_send, self.across_recv, self.core_send, self.core_recv = sems[3:]
+        self.early = early_keys(spot.groups)
+        self.rest = [key for key in far_keys(spot.groups) if key not in self.early]
+        self.near = near_keys(spot.groups)
+
+    @staticmethod
+    def sems(groups, columns):
+        return [pltpu.SemaphoreType.DMA((groups,))] * 3 + [
+            pltpu.SemaphoreType.DMA((groups, columns // 2))
+        ] * 4
+
+    def source(self, key):
+        spot = self.spot
+        if key == 0:
+            return self.rows.at[spot.place]
+        at = flip(spot.place, key)
+        return self.far_rows.at[at] if key in self.early else self.full.at[spot.lane, at]
+
+    def local_copy(self, key):
+        spot = self.spot
+        target = self.full.at[spot.lane, flip(spot.place, key)]
+        return pltpu.make_async_copy(self.source(key), target, self.local.at[key])
+
+    def swap(self, key):
+        spot = self.spot
+        peer = flip(spot.place, key)
+        return remote(
+            self.rows.at[peer],
+            self.full.at[spot.lane, spot.place],
+            self.send.at[key],
+            self.recv.at[key],
+            (peer, spot.lane),
+        )
+
+    def across(self, key, step):
+        spot = self.spot
+        return remote(
+            self.source(key),
+            self.full.at[spot.lane, flip(spot.place, key)],
+            self.across_send.at[key, step],
+            self.across_recv.at[key, step],
+            (spot.place, spot.across(step)),
+        )
+
+    def core(self, key, step):
+        spot = self.spot
+        lane = spot.behind(step)
+        target = self.full.at[lane, flip(spot.place, key)]
+        return remote(
+            target if step else self.source(key),
+            target,
+            self.core_send.at[key, step],
+            self.core_recv.at[key, step],
+            (spot.place, spot.partner),
+        )
+
+    def send_on(self, key):
+        for step in range(1, self.spot.half):
+            self.across(key, step).start()
+        self.core(key, 0).start()
+
+    def begin(self):
+        for key in self.rest + self.near:
+            self.swap(key).start()
+        for key in [0] + self.early:
+            self.send_on(key)
+            self.local_copy(key).start()
+
+    def advance(self, key):
+        self.swap(key).wait_recv()
+        self.send_on(key)
+
+    def pass_on(self, key):
+        for step in range(1, self.spot.half):
+            self.across(key, step).wait_recv()
+            self.core(key, step).start()
+
+    def finish(self):
+        half = self.spot.half
+        keys = range(self.spot.groups)
+        for key in keys:
+            for step in range(half):
+                self.core(key, step).wait_recv()
+        for key in keys:
+            if key in self.near + self.rest:
+                self.swap(key).wait_send()
+            else:
+                self.local_copy(key).wait()
+            for step in range(half):
+                self.core(key, step).wait_send()
+                if step:
+                    self.across(key, step).wait_send()
+
+
 def attend_forward_kernel(
     heads_here,
     groups,
@@ -858,6 +1157,7 @@
     base_ref,
     qkv_ref,
     rows_ref,
+    far_rows_ref,
     mixed_ref,
     totals_ref,
     full_ref,
@@ -870,7 +1170,7 @@
     query_tile = pl.program_id(0)
     tiles = qkv_ref.shape[0] // tile
     spot = Spot(groups, columns)
-    job = Dispatch(spot, rows_ref, full_ref, sems)
+    job = Spread(spot, rows_ref, far_rows_ref, full_ref, sems)
 
     @pl.when(query_tile == 0)
     def _():
@@ -949,18 +1249,30 @@
         totals_ref[0, pl.ds(head, 1), :] = tops[head] + jnp.log2(total)
     mixed_ref[...] = jnp.transpose(jnp.concatenate(parts, axis=0)).astype(jnp.bfloat16)
 
-    for key in range(groups):
-
-        @pl.when(query_tile == key * tiles // groups)
-        def _():
+    @pl.when(query_tile == tiles // 4)
+    def _():
+        for key in job.near:
+            job.advance(key)
+
+    @pl.when(query_tile == tiles // 2)
+    def _():
+        job.pass_on(0)
+        for key in job.early:
+            job.pass_on(key)
+
+    @pl.when(query_tile == tiles - 3)
+    def _():
+        for key in job.rest:
             job.advance(key)
 
     @pl.when(query_tile == tiles - 1)
     def _():
+        for key in job.near + job.rest:
+            job.pass_on(key)
         job.finish()
 
 
-def attend_forward(prefix, far_bias, base_bias, qkv, rows, columns):
+def attend_forward(prefix, far_bias, base_bias, qkv, rows, far_rows, columns):
     length = qkv.shape[0]
     groups = rows.shape[0]
     width = qkv.shape[1] // 3
@@ -980,6 +1292,7 @@
             pl.BlockSpec(base_bias.shape, lambda i: (0, 0)),
             pl.BlockSpec(qkv.shape, lambda i: (0, 0)),
             anywhere,
+            anywhere,
         ],
         out_specs=(
             pl.BlockSpec((tile, width), lambda i: (i, 0)),
@@ -991,14 +1304,14 @@
             pltpu.VMEM((heads_here, length, tile), jnp.float32),
             pltpu.VMEM((width, length), jnp.bfloat16),
         ]
-        + Dispatch.sems(groups, columns),
-        compiler_params=comm_params(5, 40),
+        + Spread.sems(groups, columns),
+        compiler_params=comm_params(5),
         cost_estimate=pl.CostEstimate(
             flops=40 * length * length * width, transcendentals=length * length * heads_here,
             bytes_accessed=8 * length * width,
         ),
         name="attend_forward",
-    )(prefix, far_bias, base_bias, qkv, rows)
+    )(prefix, far_bias, base_bias, qkv, rows, far_rows)
 
 
 def attend_backward_kernel(
@@ -1283,13 +1596,12 @@
         tail_sc[...] += spread
 
 
-def expert_math(wide_rows, grads, gate_weight, up_weight, down_weight):
+def expert_math(wide_rows, raw_hidden, gate_weight, up_weight, down_weight):
     rows, gates = wide_rows[:, :D], gates_of(wide_rows)
     gate_act = nt_dot(rows, gate_weight)
     up_act = nt_dot(rows, up_weight)
     gelu, slope = gelu_parts(gate_act)
     hidden = (gelu * up_act).astype(jnp.bfloat16)
-    raw_hidden = nt_dot(grads, down_weight)
     grad_gates = jnp.sum(raw_hidden * hidden.astype(jnp.float32), axis=1, keepdims=True)
     grad_hidden = raw_hidden * gates
     grad_gate = (grad_hidden * up_act * slope).astype(jnp.bfloat16)
@@ -1329,7 +1641,11 @@
     wide_rows = expert_input(row_main, row_tail, select)
     grads = expert_input(grad_main, grad_tail, select)
     hidden, grad_gate, grad_up, back, result = expert_math(
-        wide_rows, grads, gate_weight[0], up_weight[0], down_weight[0]
+        wide_rows,
+        nt_dot(grads, down_weight[0]),
+        gate_weight[0],
+        up_weight[0],
+        down_weight[0],
     )
     hidden_ref[0] = hidden
     grad_gate_ref[0] = grad_gate
@@ -1458,7 +1774,8 @@
             [dma((chunks, 3))]
             + [dma((chunks, groups))] * 2
             + [dma((chunks, groups, half))] * 4
-            + [dma((chunks, half))] * 4
+            + [dma((chunks, half))] * 2
+            + [dma((chunks, half, 2))] * 2
             + [dma((chunks, groups))] * 2
         )
 
@@ -1509,8 +1826,9 @@
         )
 
     def begin(self):
+        groups = self.spot.groups
         self.own().start()
-        for key in range(1, self.spot.groups):
+        for key in far_keys(groups) + near_keys(groups):
             self.swap(key).start()
 
     def advance(self):
@@ -1544,13 +1862,19 @@
             (spot.place, spot.partner),
         )
 
-    def sum_copy(self, step):
+    def side(self, near):
+        half = self.spot.groups // 2
+        here = self.spot.place // half
+        return pl.ds((here if near else 1 - here) * half, half)
+
+    def sum_copy(self, step, near):
         spot, at = self.spot, self.number
+        groups = self.side(near)
         return remote(
-            self.across_out.at[step],
-            self.across_in.at[step],
-            self.sum_send.at[at, step],
-            self.sum_recv.at[at, step],
+            self.across_out.at[step, groups],
+            self.across_in.at[step, groups],
+            self.sum_send.at[at, step, near],
+            self.sum_recv.at[at, step, near],
             (spot.place, spot.across(step)),
         )
 
@@ -1572,23 +1896,29 @@
         for step in list(range(1, self.spot.half)) + [0]:
             self.pair_copy(step).start()
 
-    def pair_sum(self, step):
-        self.pair_copy(step).wait_recv()
-        mine = self.back[self.spot.lane_at(step, False)].astype(jnp.float32)
-        return mine + self.pair_in[step].astype(jnp.float32)
+    def pair_sum(self, step, near):
+        groups = self.side(near)
+        mine = self.back[self.spot.lane_at(step, False), groups].astype(jnp.float32)
+        return mine + self.pair_in[step, groups].astype(jnp.float32)
 
     def middle(self):
         for step in range(1, self.spot.half):
-            self.across_out[step] = self.pair_sum(step).astype(jnp.bfloat16)
-            self.sum_copy(step).start()
-
-    def last(self):
-        total = self.pair_sum(0)
+            self.pair_copy(step).wait_recv()
+        for near in range(2):
+            for step in range(1, self.spot.half):
+                total = self.pair_sum(step, near)
+                self.across_out[step, self.side(near)] = total.astype(jnp.bfloat16)
+                self.sum_copy(step, near).start()
+        self.pair_copy(0).wait_recv()
+
+    def last(self, near):
+        total = self.pair_sum(0, near)
         for step in range(1, self.spot.half):
-            self.sum_copy(step).wait_recv()
-            total = total + self.across_in[step].astype(jnp.float32)
-        self.total[...] = total.astype(jnp.bfloat16)
-        for key in range(self.spot.groups):
+            self.sum_copy(step, near).wait_recv()
+            total = total + self.across_in[step, self.side(near)].astype(jnp.float32)
+        self.total[self.side(near)] = total.astype(jnp.bfloat16)
+        groups = self.spot.groups
+        for key in near_keys(groups) + [0] if near else far_keys(groups):
             self.back_copy(key).start()
 
     def finish(self):
@@ -1608,7 +1938,8 @@
         for step in range(half):
             self.pair_copy(step).wait_send()
             if step:
-                self.sum_copy(step).wait_send()
+                self.sum_copy(step, 0).wait_send()
+                self.sum_copy(step, 1).wait_send()
 
 
 def experts_kernel(
@@ -1663,10 +1994,16 @@
     @pl.when(expert == 0)
     def _():
         spot.meet()
-        for chunk in [tail] + chunks:
-            chunk.begin()
+        tail.begin()
+        chunks[0].begin()
+    select = tail_select(expert, groups * columns, tail_height)
+    raw_hidden = nt_dot(expert_input(grad_main, grad_tail, select), down_weight[0])
+
+    @pl.when(expert == 0)
+    def _():
         tail.advance()
         chunks[0].advance()
+        chunks[1].begin()
 
     for at in range(experts_here):
 
@@ -1674,18 +2011,18 @@
         def _():
             if at + 1 < experts_here:
                 chunks[at + 1].advance()
+            if at + 2 < experts_here:
+                chunks[at + 2].begin()
             if at == 0:
                 tail.complete()
             chunks[at].complete()
             if at:
                 chunks[at - 1].middle()
 
-    select = tail_select(expert, groups * columns, tail_height)
     main_rows, tail_rows, main_back, tail_back = mains[0], tails[0], mains[1], tails[1]
     wide_rows = expert_input(main_rows.at[expert], tail_rows, select)
-    grads = expert_input(grad_main, grad_tail, select)
     hidden, grad_gate, grad_up, back, result = expert_math(
-        wide_rows, grads, gate_weight[0], up_weight[0], down_weight[0]
+        wide_rows, raw_hidden, gate_weight[0], up_weight[0], down_weight[0]
     )
     hidden_ref[0] = hidden
     grad_gate_ref[0] = grad_gate
@@ -1702,7 +2039,8 @@
                 chunks[at].middle()
                 tail.middle()
             if at:
-                chunks[at - 1].last()
+                chunks[at - 1].last(0)
+                chunks[at - 1].last(1)
 
     def result_copy(at):
         place = pl.ds(pl.multiple_of(at * main_slots, main_slots), main_slots)
@@ -1720,8 +2058,9 @@
         place = pl.ds(experts_here * main_slots, tail_height)
         side = pltpu.make_async_copy(result_tail, result_ref.at[:, :, place], result_sems.at[1])
         side.start()
-        chunks[-1].last()
-        tail.last()
+        for near in range(2):
+            chunks[-1].last(near)
+            tail.last(near)
         for chunk in chunks + [tail]:
             chunk.finish()
         result_copy(expert).wait()
@@ -1769,7 +2108,7 @@
         + bufs((experts_here,), main_slots)
         + bufs((), tail_height)
         + RowChunk.sems(groups, columns, experts_here + 1),
-        compiler_params=comm_params(10, 60),
+        compiler_params=comm_params(10),
         cost_estimate=pl.CostEstimate(
             flops=12 * experts_here * count * width * units,
             transcendentals=experts_here * count * units,
@@ -1916,10 +2255,26 @@
         ],
         axis=1,
     )
-    tokens_all, small_full, out_full = entry_gather(
-        inputs.reshape(row_count, D), [packed_small, out_weight], groups, columns_of
-    )
-    tokens_all = tokens_all.reshape(length, D)
+    token_routes = routes.reshape(row_count, TOP)
+    slots = pair_slots(token_routes, priority.reshape(row_count), experts_here)
+    slot_map = (
+        jnp.arange(groups * height, dtype=jnp.int32)[:, None] == slots[None, :]
+    ).reshape(groups * height, TOP, row_count)
+    slot_any = jnp.any(slot_map, axis=1).astype(jnp.bfloat16)
+    slot_pairs = slot_map.astype(jnp.bfloat16).reshape(groups * height, TOP * row_count)
+    grad_low = grad_out.reshape(row_count, D)
+    grad_slots = nn_dot(slot_any, grad_low).astype(jnp.bfloat16).reshape(groups, height, D)
+    _, normed_all, qkv_own, small_full, out_full, far_slots = entry_gather(
+        inputs.reshape(row_count, D),
+        jnp.broadcast_to(norm_attn.astype(jnp.float32)[None], (8, shard_rows)),
+        packed_small,
+        out_weight,
+        grad_slots,
+        3 * width,
+        1,
+    )
+    normed_all = normed_all.reshape(length, D)
+    qkv_own = qkv_own.reshape(length, 3 * width)
     small_full = small_full.reshape(D, 3 * width + spare)
     out_full = out_full.reshape(D, D)
     own_weight = small_full[:, : 3 * width]
@@ -1943,20 +2298,8 @@
     base_bias = jnp.transpose(base_bias, (2, 0, 1)).reshape(heads_here * 3, 2 * tile)
     far_bias = jnp.stack([table_own[15], table_own[31]], axis=1) * log2e
 
-    token_routes = routes.reshape(row_count, TOP)
-    slots = pair_slots(token_routes, priority.reshape(row_count), experts_here)
-    slot_map = (
-        jnp.arange(groups * height, dtype=jnp.int32)[:, None] == slots[None, :]
-    ).reshape(groups * height, TOP, row_count)
-    slot_any = jnp.any(slot_map, axis=1).astype(jnp.bfloat16)
-    slot_pairs = slot_map.astype(jnp.bfloat16).reshape(groups * height, TOP * row_count)
-
-    grad_low = grad_out.reshape(row_count, D)
-    grad_slots = nn_dot(slot_any, grad_low).astype(jnp.bfloat16).reshape(groups, height, D)
-    normed_all = rms_norm(tokens_all.astype(jnp.float32), gain_attn).astype(jnp.bfloat16)
-    qkv_own = nn_dot(normed_all, own_weight).astype(jnp.bfloat16)
     mixed_own, totals, grads_received = attend_forward(
-        prefix, far_bias, base_bias, qkv_own, grad_slots, columns_of
+        prefix, far_bias, base_bias, qkv_own, grad_slots, far_slots, columns_of
     )
     attended = exchange_mixed(mixed_own.reshape(groups, row_count, width), columns_of, 8)
 
@@ -2030,10 +2373,13 @@
         out_sums,
         columns_of,
     )
-    pair_out = tn_dot(slot_pairs, returned.reshape(groups * height, D)).reshape(
-        TOP, row_count, D
-    )
-    mixture = gate_values[:, 0:1] * pair_out[0] + gate_values[:, 1:2] * pair_out[1]
+    slot_gates = jnp.sum(
+        slot_map.astype(jnp.float32) * jnp.transpose(gate_values)[None], axis=1
+    )
+    slot_high = lax.reduce_precision(slot_gates, 8, 7)
+    slot_parts = jnp.concatenate([slot_high, slot_gates - slot_high], axis=1).astype(jnp.bfloat16)
+    mixture = tn_dot(slot_parts, returned.reshape(groups * height, D))
+    mixture = mixture[:row_count] + mixture[row_count:]
     output = (middle + mixture).astype(jnp.bfloat16)
 
     table_grad = jnp.einsum(
@@ -2072,24 +2418,35 @@
         columns_of,
         7,
     )
-    qkv_full = qkv_full.reshape(D, 3 * D)
-    out_total = out_all.reshape(shard_rows, D).astype(jnp.float32)
     last_all = last_all.reshape(groups, shard_rows, 3 * width + spare)
-    qkv_total = unpack_columns(last_all, width)
-    last_extra = last_all[:, :, 3 * width :].astype(jnp.float32)
-    extra_total = jnp.sum(last_extra, axis=0)
-    table_total = jnp.transpose(
-        last_extra[:, : table_rows * heads_here, 1].reshape(groups, table_rows, heads_here),
-        (1, 0, 2),
-    ).reshape(table_rows, HEADS)
-
-    if width % 128:
+    out_all = out_all.reshape(shard_rows, D)
+    if width % 128 == 0:
+        input_grad, qkv_total, out_total, extra_total = finish(
+            grad_projected,
+            qkv_full,
+            last_all,
+            inputs.reshape(row_count, D),
+            gain_attn[None],
+            grad_middle,
+            out_all,
+            width,
+        )
+    else:
         grad_projected = jnp.transpose(
             grad_projected.reshape(groups, row_count, 3, width), (1, 2, 0, 3)
         ).reshape(row_count, 3 * D)
-    grad_low_one = nt_dot(grad_projected, qkv_full)
-    _, norm_one_back = jax.vjp(lambda features: rms_norm(features, gain_attn), tokens_in)
-    input_grad = grad_middle + norm_one_back(grad_low_one)[0]
+        grad_low_one = nt_dot(grad_projected, qkv_full.reshape(D, 3 * D))
+        _, norm_one_back = jax.vjp(lambda features: rms_norm(features, gain_attn), tokens_in)
+        input_grad = grad_middle + norm_one_back(grad_low_one)[0]
+        qkv_total = jnp.transpose(
+            last_all[:, :, : 3 * width].reshape(groups, shard_rows, 3, width), (1, 2, 0, 3)
+        ).reshape(shard_rows, 3 * D).astype(jnp.float32)
+        out_total = out_all.astype(jnp.float32)
+        extra_total = jnp.sum(last_all[:, :, 3 * width :].astype(jnp.float32), axis=0)
+    table_part = last_all[:, : table_rows * heads_here, 3 * width + 1].astype(jnp.float32)
+    table_total = jnp.transpose(
+        table_part.reshape(groups, table_rows, heads_here), (1, 0, 2)
+    ).reshape(table_rows, HEADS)
     return (
         output.reshape(row_count, 1, D),
         input_grad.reshape(row_count, 1, D),

time: 468 us -> 445 us (0.951)
  local copies, waits for them, and re-layouts: 30.8 us -> 23.5 us
  other arithmetic: 18.5 us -> 11.4 us
  matrix products: 24.3 us -> 19.2 us
    pallas_call x2, Pallas kernels: 58.9 us -> 76.1 us  [the longest x1 66.1 us: entry_gather(): pl.pallas_call(functools.partial(entry_kernel, groups, columns), out_shap...]
    pallas_call x1, Pallas kernels: 71 us -> 60.4 us  [tail_exchange(): pl.pallas_call(functools.partial(tail_kernel, groups, columns, chunks), o...]
    unnamed x68 -> x39, local copies, waits for them, and re-layouts: 18.2 us -> 9.01 us
    convert_element_type x4 -> x0, other arithmetic: 7.41 us -> none  [the longest x1 2.79 us: shards(): rms_norm(tokens_all.astype(jnp.float32), gain_attn).astype(jnp.bfloat16)]
    pallas_call x1, Pallas kernels: 55.9 us -> 50.4 us  [attend_backward(): pl.pallas_call(functools.partial(attend_backward_kernel, heads_here, grou...]
    pallas_call x1, Pallas kernels: 40.4 us -> 35 us  [attend_forward(): pl.pallas_call(functools.partial(attend_forward_kernel, heads_here, group...]
    dot_general x3 -> x2, matrix products: 8.92 us -> 4.23 us  [nt_dot(): lax.dot_general(left, right, (((1,), (1,)), ((), ())), preferred_element_...]
where the time goes in v3:
time: 445 us; the launch traced here: 436 us
  Pallas kernels  362 us (81%)
  local copies, waits for them, and re-layouts  23.5 us (5%)
  matrix products  19.2 us (4%)
  between operations  16.3 us (4%)
  other arithmetic  11.4 us (3%)
    pallas_call x1, Pallas kernels, experts(): pl.pallas_call(functools.partial(experts_kernel, experts_here, groups, co...  102 us
    pallas_call x1, Pallas kernels, entry_gather(): pl.pallas_call(functools.partial(entry_kernel, groups, columns), out_shap...  66.1 us
    pallas_call x1, Pallas kernels, tail_exchange(): pl.pallas_call(functools.partial(tail_kernel, groups, columns, chunks), o...  60.4 us
    pallas_call x1, Pallas kernels, attend_backward(): pl.pallas_call(functools.partial(attend_backward_kernel, heads_here, grou...  50.4 us
    pallas_call x1, Pallas kernels, attend_forward(): pl.pallas_call(functools.partial(attend_forward_kernel, heads_here, group...  35 us
    pallas_call x1, Pallas kernels, expert_weight_grads(): pl.pallas_call(functools.partial(expert_weight_kernel, parts), grid=(expe...  22.2 us
    pallas_call x1, Pallas kernels, exchange_mixed(): pl.pallas_call(functools.partial(mixed_kernel, groups, columns), out_shap...  15.9 us
    pallas_call x1, Pallas kernels, finish(): pl.pallas_call(functools.partial(finish_kernel, width), grid=(3,), out_sh...  10.1 us
  transfers between devices with their start and end apart: 2, of which 0 were waited for; matrix products, arithmetic and copies ran while one was open for 1% of the time, Pallas kernels for 5%

profile of v3, /device:TPU:0, one launch (start us, length us, event | category | flops | bytes accessed | tf_op | source)
XLA Modules:
  0.0 436.3 jit_solution(1241627340087909214)
XLA Ops:
  7.2 0.7 broadcast_add_fusion
  7.9 0.8 slice_bitcast_fusion.3
  8.7 0.7 pad_add_fusion
  9.4 0.3 convert_reduce_fusion
  9.7 0.8 reshape.451
  10.7 0.8 broadcast_in_dim.137
  11.4 0.8 copy.157
  12.3 0.8 broadcast_in_dim.136
  13.0 0.2 fusion.6
  13.3 1.8 copy.155
  15.1 0.2 copy.156
  15.3 1.5 convolution_convert_fusion.2
  16.8 0.9 concatenate.50.pack
  17.7 0.6 broadcast_in_dim.113.gain
  18.3 66.1 %entry_gather.1 = (bf16[8,256,1024]{2,1,0:T(8,128)(2,1)}, bf16[8,256,1024]{2,1,0:T(8,128)(2,1)}, bf16[8,256,384]{2,1,0:T(8,128)(2,1)}, bf16[4,256,512]{2,1,0:T(8...) custom-call(bf16[256,1024]{1,0:T(8,128)(2,1)} %bitcast.116, f32[8,256]{1,0:T(8,128)} %broadcast_in_dim.113.gain, ...), custom_call_target="tpu_custom_call" | custom-call | tf_op jit(solution)/shard_map/entry_gather/pallas_call | solution.py:387
  84.3 2.0 fusion.32
  86.3 2.0 slice_convert_fusion
  89.2 0.4 convolution_multiply_fusion
  89.7 0.6 reshape.458.base_ref
  90.5 0.6 maximum_multiply_fusion.far_ref
  91.1 35.0 %attend_forward.1 = (bf16[2048,128]{1,0:T(8,128)(2,1)}, f32[8,2,256]{2,1,0:T(2,128)}, bf16[4,8,72,1024]{3,2,1,0:T(8,128)(2,1)}) custom-call(s32[1]{0:T(128)S(6)} %copy.183.prefix_ref, f32[2,2]{1,0:T(2,128)} %maximum_multiply_fusion.far_ref, f32[6,512]{1,0:T(8,128)} %reshape.458.base_ref, bf16[2048,384]{1,0:T(8,128)(2,1)} %bitcast.145, ...), custom_call_target="tpu_custom_call" | custom-call | flops 21474836480 | bytes 2097152 | tf_op jit(solution)/shard_map/attend_forward/pallas_call | solution.py:1281
  126.2 15.9 %exchange_mixed.1 = bf16[256,1024]{1,0:T(8,128)(2,1)} custom-call(bf16[8,256,128]{2,1,0:T(8,128)(2,1)} %bitcast.125), custom_call_target="tpu_custom_call" | custom-call | tf_op jit(solution)/shard_map/exchange_mixed/pallas_call | solution.py:755
  142.1 1.9 multiply_reduce_fusion.2
  144.1 1.0 copy-done.2
  145.1 0.3 fusion.51
  145.6 0.2 copy.175
  146.0 2.0 convolution_convert_fusion
  148.0 102.0 %experts.1 = (bf16[4,576,704]{2,1,0:T(8,128)(2,1)}, bf16[4,576,704]{2,1,0:T(8,128)(2,1)}, bf16[4,576,704]{2,1,0:T(8,128)(2,1)}, bf16[4,8,72,1024]{3,2,1,0:T(8,12...) custom-call(bf16[8,72,1152]{2,1,0:T(8,128)(2,1)} %bitcast.153, ...), custom_call_target="tpu_custom_call" | custom-call | flops 19931332608 | bytes 36175872 | tf_op jit(solution)/shard_map/experts/pallas_call | solution.py:2088
  250.1 1.2 fusion.7
  251.3 2.9 fusion.3
  254.2 0.6 fusion.50
  255.7 0.7 negate_add_fusion
  256.4 1.9 multiply_reduce_fusion
  258.3 0.3 fusion.11.grad_middle
  258.6 0.7 copy-done.4
  259.3 2.1 convolution_convert_fusion.1
  261.5 2.3 fusion.1
  263.8 0.9 copy.182
  264.7 3.7 all-to-all-start
  268.5 1.0 slice.112.own_weight
  269.4 0.2 convolution_convert_fusion.4
  269.6 0.2 copy.169
  269.8 0.2 broadcast_in_dim.139
  270.1 0.2 select_reduce_fusion
  270.4 22.2 %expert_weight_grads.1 = (f32[4,704,1024]{2,1,0:T(8,128)}, f32[4,704,1024]{2,1,0:T(8,128)}, f32[4,704,1024]{2,1,0:T(8,128)}) custom-call(bf16[4,8,72,1152]{3,2,1,0:T(8,128)(2,1)} %get-tuple-element.64.row_main.row_tail, bf16[4,8,72,1152]{3,2,1,0:T(8,128)(2,1)} %get-tuple-element.64.row_main.row_tail, ...), custom_call_target="tpu_custom_call" | custom-call | flops 9965666304 | bytes 58195968 | tf_op jit(solution)/shard_map/expert_weight_grads/pallas_call | solution.py:2165
  292.7 0.8 copy-done.9
  293.5 50.4 %attend_backward.1 = (bf16[2048,384]{1,0:T(8,128)(2,1)}, f32[6,512]{1,0:T(8,128)}, f32[2,2,8,256]{3,2,1,0:T(8,128)}, bf16[8,72,1024]{2,1,0:T(8,128)(2,1)}, bf16[32,1024]{1,0:T(8,128)(2,1)}) custom-call(s32[1]{0:T(128)S(6)} %copy.183.prefix_ref, f32[2,2]{1,0:T(2,128)} %maximum_multiply_fusion.far_ref, f32[6,512]{1,0:T(8,128)} %reshape.458.base_ref, ...), custom_call_target="tpu_custom_call" | custom-call | flops 37580963840 | bytes 4194304 | tf_op jit(solution)/shard_map/attend_backward/pallas_call | solution.py:1505
  343.9 0.9 reduce_sum.164
  344.7 0.2 slice_reduce_fusion.4
  344.9 0.7 reshape.472
  345.6 0.2 fusion.10
  346.1 0.2 copy.178
  346.4 1.5 concatenate.59.extra
  347.9 60.4 %tail_exchange.1 = (bf16[256,3072]{1,0:T(8,128)(2,1)}, bf16[8,2,128,512]{3,2,1,0:T(8,128)(2,1)}, bf16[8,32,1024]{2,1,0:T(8,128)(2,1)}, bf16[4,256,3072]{2,1,0:T(8,128)(2,1)}) custom-call(bf16[8,256,384]{2,1,0:T(8,128)(2,1)} %bitcast.120, bf16[2048,1024]{1,0:T(8,128)(2,1)} %bitcast.118, bf16[1024,384]{1,0:T(8,128)(2,1)} %slice.112.own_weight, ...), custom_call_target="tpu_custom_call" | custom-call | tf_op jit(solution)/shard_map/tail_exchange/pallas_call | solution.py:883
  408.3 0.8 slice_convert_fusion.1
  409.2 10.1 %finish.1 = (f32[256,1024]{1,0:T(8,128)}, f32[256,3072]{1,0:T(8,128)}, f32[256,1024]{1,0:T(8,128)}, f32[256,128]{1,0:T(8,128)}) custom-call(bf16[256,3072]{1,0:T(8,128)(2,1)} %get-tuple-element.56.grads, bf16[4,256,3072]{2,1,0:T(8,128)(2,1)} %get-tuple-element.57.weight, bf16[8,256,512]{2,1,0:T(8,128)(2,1)} %bitcast.105, bf16[8,256,512]{2,1,0:T(8,128)(2,1)} %bitcast.106, ...), custom_call_target="tpu_custom_call" | custom-call | tf_op jit(solution)/shard_map/finish/pallas_call | solution.py:952
  419.2 1.8 slice_reduce_fusion.1
  421.0 1.0 slice.96
  422.0 2.3 fusion.15
  424.3 1.1 fusion.21
  425.4 0.2 copy.170
  425.6 0.7 copy.173
  426.3 2.0 copy.172
  428.3 0.7 copy.174
  (78 shorter events, 2.0 us)
Async XLA Ops:
  7.2 285.5 %reduce-scatter.2.cloned.1.call-start = ((), (), s32[]{:S(2)}) async-start(), calls=%async_computation.2 | async-start | bytes 2621440 | tf_op jit(solution)/shard_map/reduce_scatter | solution.py:2361
  13.3 2.0 copy-start.6
  15.1 2.6 copy-start.11
  18.3 71.0 %copy-start.14 = (s32[1536]{0:T(1024)S(1)}, s32[1536]{0:T(1024)}, u32[]{:S(2)}) copy-start(s32[1536]{0:T(1024)} %constant.96.clone) | copy-start | bytes 18436
  91.1 50.9 %copy-start.1 = (bf16[4,256,1024]{2,1,0:T(8,128)(2,1)S(1)}, bf16[4,256,1024]{2,1,0:T(8,128)(2,1)}, u32[]{:S(2)}) copy-start(bf16[4,256,1024]{2,1,0:T(8,128)(2,1)} %get-tuple-element.45) | copy-start | bytes 6291460
  91.1 50.9 %copy-start.5 = (bf16[256,1,1024]{2,0,1:T(8,128)(2,1)S(1)}, bf16[256,1,1024]{2,0,1:T(8,128)(2,1)}, u32[]{:S(2)}) copy-start(bf16[256,1,1024]{2,0,1:T(8,128)(2,1)} %param.16) | copy-start | bytes 1572868
  143.9 1.2 copy-start.2
  143.9 1.6 copy-start.10
  250.1 4.1 copy-start.12
  256.4 1.9 copy-start.7
  258.3 1.0 copy-start.4
  259.3 2.1 copy-start
  263.8 4.6 %copy-start.3 = (bf16[4,256,512]{2,1,0:T(8,128)(2,1)S(1)}, bf16[4,256,512]{2,1,0:T(8,128)(2,1)}, u32[]{:S(2)}) copy-start(bf16[4,256,512]{2,1,0:T(8,128)(2,1)} %get-tuple-element.41) | copy-start | bytes 3145732
  264.7 27.9 %all-to-all-start = ((bf16[8,256,128]{2,1,0:T(8,128)(2,1)}), bf16[8,256,128]{2,1,0:T(8,128)(2,1)S(1)}, u32[]{:S(2)}, u32[]{:S(2)}) async-start(bf16[8,256,128]{2,1,0:T(8,128)(2,1)} %bitcast.103), calls=%async_computation | async-start | bytes 1048576 | tf_op jit(solution)/shard_map/all_to_all | solution.py:2355
  292.6 0.8 copy-start.9
  293.4 52.2 %copy-start.13 = (s32[3,512]{1,0:T(4,128)S(1)}, s32[3,512]{1,0:T(4,128)}, u32[]{:S(2)}) copy-start(s32[3,512]{1,0:T(4,128)} %constant.111) | copy-start | bytes 18436
  424.3 2.0 copy-start.8
Sparse Core Ops, SparseCore 0:
  261.6 29.7 reduce-scatter.1

commit v4 on v3

--- a/solution.py
+++ b/solution.py
@@ -273,6 +273,8 @@
     pack_all,
     out_all,
     far_rows,
+    side_rows,
+    gain_all,
     token_sc,
     normed_sc,
     qkv_sc,
@@ -282,6 +284,7 @@
     normed_sems,
     qkv_sems,
     pack_sem,
+    gain_sem,
     *sems,
 ):
     spot = Spot(groups, columns)
@@ -289,7 +292,7 @@
     gains = ColumnGather(spot, gain, gain_sc, *sems[3:8])
     packs = ColumnGather(spot, pack, pack_sc, *sems[8:13])
     outs = ColumnGather(spot, out_weight, out_all, *sems[13:18])
-    far_send, far_recv = sems[18:]
+    far_send, far_recv, side_send, side_recv = sems[18:]
     wide = qkv_sc.shape[2]
 
     def far_copy(key):
@@ -300,6 +303,16 @@
             far_send.at[key],
             far_recv.at[key],
             (peer, spot.lane),
+        )
+
+    def side_copy(key, step):
+        at = flip(spot.place, key)
+        return remote(
+            far_rows.at[at] if key else rows.at[at],
+            side_rows.at[step - 1, at],
+            side_send.at[key, step],
+            side_recv.at[key, step],
+            (spot.place, spot.across(step)),
         )
 
     def stores(origin):
@@ -335,9 +348,13 @@
     packs.finish()
     keep = pltpu.make_async_copy(pack_sc, pack_all, pack_sem)
     keep.start()
+    keep_gain = pltpu.make_async_copy(gain_sc, gain_all, gain_sem)
+    keep_gain.start()
     project(spot.place, tokens)
     line.hop(1)
     outs.forward()
+    for step in range(1, spot.half):
+        side_copy(0, step).start()
     line.hop(2)
     for key in early_keys(groups):
         far_copy(key).start()
@@ -352,6 +369,11 @@
         return carry
 
     lax.fori_loop(0, line.long, own_column, 0)
+
+    for key in early_keys(groups):
+        far_copy(key).wait_recv()
+        for step in range(1, spot.half):
+            side_copy(key, step).start()
 
     def other_column(at, carry):
         row = line.z + ((at + 1) // 2) * (1 - 2 * (at % 2))
@@ -366,13 +388,16 @@
         return carry
 
     lax.fori_loop(0, 2 * line.long - 1, other_column, 0)
-    for key in early_keys(groups):
-        far_copy(key).wait_recv()
+    line.settle()
     for key in early_keys(groups):
         far_copy(key).wait_send()
-    line.settle()
+    for key in [0] + early_keys(groups):
+        for step in range(1, spot.half):
+            side_copy(key, step).wait_recv()
+            side_copy(key, step).wait_send()
     outs.finish()
     keep.wait()
+    keep_gain.wait()
     for origin in range(groups):
         for store in stores(origin):
             store.wait()
@@ -393,9 +418,11 @@
             low(columns, *pack.shape),
             low(columns, *out_weight.shape),
             low(*rows.shape),
+            low(columns // 2 - 1, *rows.shape),
+            jax.ShapeDtypeStruct((columns,) + gain.shape, jnp.float32),
         ),
         in_specs=[anywhere] * 5,
-        out_specs=(anywhere,) * 6,
+        out_specs=(anywhere,) * 8,
         scratch_shapes=[
             pltpu.VMEM(tokens.shape, jnp.bfloat16),
             pltpu.VMEM((groups,) + tokens.shape, jnp.bfloat16),
@@ -406,10 +433,12 @@
             dma((groups,)),
             dma((groups,)),
             dma(()),
+            dma(()),
         ]
         + LineGather.sems(groups)
         + ColumnGather.sems(columns) * 3
-        + [dma((groups,))] * 2,
+        + [dma((groups,))] * 2
+        + [dma((groups, columns // 2))] * 2,
         compiler_params=comm_params(which),
         name="entry_gather",
     )(tokens, gain, pack, out_weight, rows)
@@ -805,7 +834,6 @@
     grads,
     normed,
     own_weight,
-    gains,
     extra,
     piece,
     weight,
@@ -843,8 +871,8 @@
     for at in range(columns * chunks):
         rows = pl.ds(at * block_rows, block_rows)
         grad = tn_dot(normed_sc[:, rows], all_grads)
-        gain = jnp.sum(grad * own_weight[rows, :].astype(jnp.float32), axis=1, keepdims=True)
-        gain = gain / gains[rows, :]
+        weights = own_weight[rows, :][:, :wide].astype(jnp.float32)
+        gain = jnp.sum(grad * weights, axis=1, keepdims=True)
         lanes = lax.broadcasted_iota(jnp.int32, (block_rows, spare), 1)
         side = jnp.where(lanes == 0, gain, extra[rows, :].astype(jnp.float32))
         part[at // chunks, at % chunks] = jnp.concatenate([grad, side], axis=1).astype(jnp.bfloat16)
@@ -872,7 +900,7 @@
     tail.sums.finish()
 
 
-def tail_exchange(grads, normed, own_weight, gains, extra, piece, weight, columns, which):
+def tail_exchange(grads, normed, own_weight, extra, piece, weight, columns, which):
     groups, row_count, wide = grads.shape
     apart = wide // 3 % 128 != 0
     grads_shape = grads.shape if apart else (row_count, wide * groups)
@@ -888,7 +916,7 @@
             shape_of((groups,) + piece.shape),
             shape_of((columns,) + weight.shape),
         ),
-        in_specs=[anywhere, anywhere, inside, inside, inside, anywhere, anywhere],
+        in_specs=[anywhere, anywhere, inside, inside, anywhere, anywhere],
         out_specs=(anywhere,) * 4,
         scratch_shapes=[
             pltpu.VMEM(grads.shape, jnp.bfloat16),
@@ -899,7 +927,7 @@
         + Tail.scratch(columns, groups, chunks, block, 1 if apart else 3),
         compiler_params=comm_params(which),
         name="tail_exchange",
-    )(grads, normed, own_weight, gains, extra, piece, weight)
+    )(grads, normed, own_weight, extra, piece, weight)
 
 
 def finish_kernel(
@@ -940,7 +968,7 @@
         inner = jnp.mean(scaled * unit, axis=-1, keepdims=True)
         input_grad[...] = grad_middle[...] + factor * (scaled - unit * inner)
         out_grad[...] = out_low[...].astype(jnp.float32)
-        extra[...] = jnp.sum(packed_extra[...].astype(jnp.float32), axis=0)
+        extra[...] = jnp.transpose(jnp.sum(packed_extra[...].astype(jnp.float32), axis=0))
 
 
 def finish(grads, weight, packed, tokens, gain, grad_middle, out_low, width):
@@ -956,7 +984,7 @@
             full,
             jax.ShapeDtypeStruct((shard_rows, 3 * D), jnp.float32),
             jax.ShapeDtypeStruct((shard_rows, D), jnp.float32),
-            jax.ShapeDtypeStruct((shard_rows, spare), jnp.float32),
+            jax.ShapeDtypeStruct((spare, shard_rows), jnp.float32),
         ),
         in_specs=[
             pl.BlockSpec((rows, D), lambda t: (0, t)),
@@ -972,7 +1000,7 @@
             pl.BlockSpec((rows, D), whole),
             pl.BlockSpec((shard_rows, D), lambda t: (0, t)),
             pl.BlockSpec((shard_rows, D), whole),
-            pl.BlockSpec((shard_rows, spare), whole),
+            pl.BlockSpec((spare, shard_rows), whole),
         ),
         scratch_shapes=[pltpu.VMEM((rows, D), jnp.float32)],
         compiler_params=pltpu.CompilerParams(vmem_limit_bytes=60 * mega),
@@ -1051,9 +1079,10 @@
 
 
 class Spread:
-    def __init__(self, spot, rows, far_rows, full, sems):
-        self.spot, self.rows, self.far_rows, self.full = spot, rows, far_rows, full
-        self.local, self.send, self.recv = sems[:3]
+    def __init__(self, spot, rows, far_rows, side_rows, full, sems):
+        self.spot, self.rows, self.full = spot, rows, full
+        self.far_rows, self.side_rows = far_rows, side_rows
+        self.send, self.recv, self.local = sems[:3]
         self.across_send, self.across_recv, self.core_send, self.core_recv = sems[3:]
         self.early = early_keys(spot.groups)
         self.rest = [key for key in far_keys(spot.groups) if key not in self.early]
@@ -1061,21 +1090,24 @@
 
     @staticmethod
     def sems(groups, columns):
-        return [pltpu.SemaphoreType.DMA((groups,))] * 3 + [
-            pltpu.SemaphoreType.DMA((groups, columns // 2))
-        ] * 4
-
-    def source(self, key):
+        half = columns // 2
+        return [pltpu.SemaphoreType.DMA((groups,))] * 2 + [
+            pltpu.SemaphoreType.DMA((groups, half))
+        ] * 5
+
+    def source(self, key, step):
         spot = self.spot
-        if key == 0:
-            return self.rows.at[spot.place]
         at = flip(spot.place, key)
-        return self.far_rows.at[at] if key in self.early else self.full.at[spot.lane, at]
-
-    def local_copy(self, key):
+        if key and key not in self.early:
+            return self.full.at[spot.behind(step), at]
+        if step:
+            return self.side_rows.at[step - 1, at]
+        return self.far_rows.at[at] if key else self.rows.at[at]
+
+    def local_copy(self, key, step):
         spot = self.spot
-        target = self.full.at[spot.lane, flip(spot.place, key)]
-        return pltpu.make_async_copy(self.source(key), target, self.local.at[key])
+        target = self.full.at[spot.behind(step), flip(spot.place, key)]
+        return pltpu.make_async_copy(self.source(key, step), target, self.local.at[key, step])
 
     def swap(self, key):
         spot = self.spot
@@ -1090,9 +1122,10 @@
 
     def across(self, key, step):
         spot = self.spot
+        block = self.full.at[spot.lane, flip(spot.place, key)]
         return remote(
-            self.source(key),
-            self.full.at[spot.lane, flip(spot.place, key)],
+            block,
+            block,
             self.across_send.at[key, step],
             self.across_recv.at[key, step],
             (spot.place, spot.across(step)),
@@ -1100,31 +1133,27 @@
 
     def core(self, key, step):
         spot = self.spot
-        lane = spot.behind(step)
-        target = self.full.at[lane, flip(spot.place, key)]
         return remote(
-            target if step else self.source(key),
-            target,
+            self.source(key, step),
+            self.full.at[spot.behind(step), flip(spot.place, key)],
             self.core_send.at[key, step],
             self.core_recv.at[key, step],
             (spot.place, spot.partner),
         )
-
-    def send_on(self, key):
-        for step in range(1, self.spot.half):
-            self.across(key, step).start()
-        self.core(key, 0).start()
 
     def begin(self):
         for key in self.rest + self.near:
             self.swap(key).start()
         for key in [0] + self.early:
-            self.send_on(key)
-            self.local_copy(key).start()
+            for step in range(self.spot.half):
+                self.core(key, step).start()
+                self.local_copy(key, step).start()
 
     def advance(self, key):
         self.swap(key).wait_recv()
-        self.send_on(key)
+        for step in range(1, self.spot.half):
+            self.across(key, step).start()
+        self.core(key, 0).start()
 
     def pass_on(self, key):
         for step in range(1, self.spot.half):
@@ -1138,13 +1167,14 @@
             for step in range(half):
                 self.core(key, step).wait_recv()
         for key in keys:
-            if key in self.near + self.rest:
+            moved = key in self.near + self.rest
+            if moved:
                 self.swap(key).wait_send()
-            else:
-                self.local_copy(key).wait()
             for step in range(half):
                 self.core(key, step).wait_send()
-                if step:
+                if not moved:
+                    self.local_copy(key, step).wait()
+                elif step:
                     self.across(key, step).wait_send()
 
 
@@ -1158,6 +1188,7 @@
     qkv_ref,
     rows_ref,
     far_rows_ref,
+    side_rows_ref,
     mixed_ref,
     totals_ref,
     full_ref,
@@ -1170,7 +1201,7 @@
     query_tile = pl.program_id(0)
     tiles = qkv_ref.shape[0] // tile
     spot = Spot(groups, columns)
-    job = Spread(spot, rows_ref, far_rows_ref, full_ref, sems)
+    job = Spread(spot, rows_ref, far_rows_ref, side_rows_ref, full_ref, sems)
 
     @pl.when(query_tile == 0)
     def _():
@@ -1256,8 +1287,7 @@
 
     @pl.when(query_tile == tiles // 2)
     def _():
-        job.pass_on(0)
-        for key in job.early:
+        for key in job.near[:1]:
             job.pass_on(key)
 
     @pl.when(query_tile == tiles - 3)
@@ -1267,12 +1297,12 @@
 
     @pl.when(query_tile == tiles - 1)
     def _():
-        for key in job.near + job.rest:
+        for key in job.near[1:] + job.rest:
             job.pass_on(key)
         job.finish()
 
 
-def attend_forward(prefix, far_bias, base_bias, qkv, rows, far_rows, columns):
+def attend_forward(prefix, far_bias, base_bias, qkv, rows, far_rows, side_rows, columns):
     length = qkv.shape[0]
     groups = rows.shape[0]
     width = qkv.shape[1] // 3
@@ -1293,6 +1323,7 @@
             pl.BlockSpec(qkv.shape, lambda i: (0, 0)),
             anywhere,
             anywhere,
+            anywhere,
         ],
         out_specs=(
             pl.BlockSpec((tile, width), lambda i: (i, 0)),
@@ -1311,7 +1342,7 @@
             bytes_accessed=8 * length * width,
         ),
         name="attend_forward",
-    )(prefix, far_bias, base_bias, qkv, rows, far_rows)
+    )(prefix, far_bias, base_bias, qkv, rows, far_rows, side_rows)
 
 
 def attend_backward_kernel(
@@ -1596,20 +1627,39 @@
         tail_sc[...] += spread
 
 
-def expert_math(wide_rows, raw_hidden, gate_weight, up_weight, down_weight):
-    rows, gates = wide_rows[:, :D], gates_of(wide_rows)
+def expert_math(rows, gates, raw_hidden, gate_weight, up_weight, down_weight):
     gate_act = nt_dot(rows, gate_weight)
     up_act = nt_dot(rows, up_weight)
     gelu, slope = gelu_parts(gate_act)
-    hidden = (gelu * up_act).astype(jnp.bfloat16)
-    grad_gates = jnp.sum(raw_hidden * hidden.astype(jnp.float32), axis=1, keepdims=True)
+    hidden = gelu * up_act
+    low_hidden = hidden.astype(jnp.bfloat16)
+    grad_gates = jnp.sum(raw_hidden * low_hidden.astype(jnp.float32), axis=1, keepdims=True)
     grad_hidden = raw_hidden * gates
     grad_gate = (grad_hidden * up_act * slope).astype(jnp.bfloat16)
     grad_up = (grad_hidden * gelu).astype(jnp.bfloat16)
     back = nn_dot(grad_gate, gate_weight) + nn_dot(grad_up, up_weight)
-    lanes = lax.broadcasted_iota(jnp.int32, (back.shape[0], spare), 1)
-    back = jnp.concatenate([back, jnp.where(lanes == 0, grad_gates, 0.0)], axis=1)
-    return hidden, grad_gate, grad_up, back, nn_dot(hidden, down_weight)
+    gated = (hidden * gates).astype(jnp.bfloat16)
+    return gated, grad_gate, grad_up, back, grad_gates, nn_dot(low_hidden, down_weight)
+
+
+def slot_lanes(expert, experts_here, sources):
+    main = sources * main_slots
+    count = sources * CAP
+    rows = lax.broadcasted_iota(jnp.int32, (count, sources), 0)
+    source = jnp.where(rows < main, rows // main_slots, (rows - main) // tail_slots)
+    hot = jnp.where(lax.broadcasted_iota(jnp.int32, (count, sources), 1) == source, 1.0, 0.0)
+    rows = lax.broadcasted_iota(jnp.int32, (count, spare), 0)
+    lane = jnp.where(
+        rows < main,
+        expert * main_slots + rows % main_slots,
+        experts_here * main_slots + expert * tail_slots + (rows - main) % tail_slots,
+    )
+    return hot.astype(jnp.bfloat16), lax.broadcasted_iota(jnp.int32, (count, spare), 1) == lane
+
+
+def split_low(values):
+    high = values.astype(jnp.bfloat16)
+    return high, (values - high.astype(jnp.float32)).astype(jnp.bfloat16)
 
 
 def expert_act_kernel(
@@ -1640,13 +1690,16 @@
     select = tail_select(expert, sources, tail_height)
     wide_rows = expert_input(row_main, row_tail, select)
     grads = expert_input(grad_main, grad_tail, select)
-    hidden, grad_gate, grad_up, back, result = expert_math(
-        wide_rows,
+    hidden, grad_gate, grad_up, back, grad_gates, result = expert_math(
+        wide_rows[:, :D],
+        gates_of(wide_rows),
         nt_dot(grads, down_weight[0]),
         gate_weight[0],
         up_weight[0],
         down_weight[0],
     )
+    lanes = lax.broadcasted_iota(jnp.int32, (back.shape[0], spare), 1)
+    back = jnp.concatenate([back, jnp.where(lanes == 0, grad_gates, 0.0)], axis=1)
     hidden_ref[0] = hidden
     grad_gate_ref[0] = grad_gate
     grad_up_ref[0] = grad_up
@@ -1771,108 +1824,100 @@
         half = columns // 2
         dma = pltpu.SemaphoreType.DMA
         return (
-            [dma((chunks, 3))]
+            [dma((chunks, 4))]
             + [dma((chunks, groups))] * 2
-            + [dma((chunks, groups, half))] * 4
-            + [dma((chunks, half))] * 2
-            + [dma((chunks, half, 2))] * 2
+            + [dma((chunks, half, 2))] * 8
             + [dma((chunks, groups))] * 2
         )
 
-    def own(self):
-        spot = self.spot
-        return pltpu.make_async_copy(
-            self.rows_in.at[spot.place, self.place_rows],
-            self.rows.at[spot.lane, spot.place],
-            self.local.at[self.number, 0],
-        )
-
-    def keep(self):
-        return pltpu.make_async_copy(
-            self.rows, self.rows_all.at[:, :, self.place_rows], self.local.at[self.number, 1]
-        )
-
-    def swap(self, key):
-        spot, at = self.spot, self.number
-        peer = flip(spot.place, key)
-        return remote(
-            self.rows_in.at[peer, self.place_rows],
-            self.rows.at[spot.lane, spot.place],
-            self.send.at[at, key],
-            self.recv.at[at, key],
-            (peer, spot.lane),
-        )
-
-    def across(self, key, step):
-        spot, at = self.spot, self.number
-        block = self.rows.at[spot.lane, flip(spot.place, key)]
-        return remote(
-            block,
-            block,
-            self.across_send.at[at, key, step],
-            self.across_recv.at[at, key, step],
-            (spot.place, spot.across(step)),
-        )
-
-    def core(self, key, step):
-        spot, at = self.spot, self.number
-        block = self.rows.at[spot.behind(step), flip(spot.place, key)]
-        return remote(
-            block,
-            block,
-            self.core_send.at[at, key, step],
-            self.core_recv.at[at, key, step],
-            (spot.place, spot.partner),
-        )
-
-    def begin(self):
+    def keys(self, near):
         groups = self.spot.groups
-        self.own().start()
-        for key in far_keys(groups) + near_keys(groups):
-            self.swap(key).start()
-
-    def advance(self):
-        for key in range(self.spot.groups):
-            if key == 0:
-                self.own().wait()
-            else:
-                self.swap(key).wait_recv()
-            for step in range(1, self.spot.half):
-                self.across(key, step).start()
-            self.core(key, 0).start()
-
-    def complete(self):
-        groups, half = self.spot.groups, self.spot.half
-        for key in range(groups):
-            for step in range(1, half):
-                self.across(key, step).wait_recv()
-                self.core(key, step).start()
-        for key in range(groups):
-            for step in range(half):
-                self.core(key, step).wait_recv()
-        self.keep().start()
-
-    def pair_copy(self, step):
-        spot, at = self.spot, self.number
-        return remote(
-            self.back.at[spot.lane_at(step, True)],
-            self.pair_in.at[step],
-            self.pair_send.at[at, step],
-            self.pair_recv.at[at, step],
-            (spot.place, spot.partner),
-        )
+        return [0] + near_keys(groups) if near else far_keys(groups)
 
     def side(self, near):
         half = self.spot.groups // 2
         here = self.spot.place // half
         return pl.ds((here if near else 1 - here) * half, half)
 
+    def swap(self, key):
+        spot, at = self.spot, self.number
+        peer = flip(spot.place, key)
+        source = self.rows_in.at[peer, self.place_rows]
+        target = self.rows.at[spot.lane, spot.place]
+        if key == 0:
+            return pltpu.make_async_copy(source, target, self.local.at[at, 0])
+        return remote(
+            source, target, self.send.at[at, key], self.recv.at[at, key], (peer, spot.lane)
+        )
+
+    def keep(self, near):
+        side = self.side(near)
+        return pltpu.make_async_copy(
+            self.rows.at[:, side],
+            self.rows_all.at[:, side, self.place_rows],
+            self.local.at[self.number, 1 + near],
+        )
+
+    def across(self, near, step):
+        spot, at = self.spot, self.number
+        block = self.rows.at[spot.lane, self.side(near)]
+        return remote(
+            block,
+            block,
+            self.across_send.at[at, step, near],
+            self.across_recv.at[at, step, near],
+            (spot.place, spot.across(step)),
+        )
+
+    def core(self, near, step):
+        spot, at = self.spot, self.number
+        block = self.rows.at[spot.behind(step), self.side(near)]
+        return remote(
+            block,
+            block,
+            self.core_send.at[at, step, near],
+            self.core_recv.at[at, step, near],
+            (spot.place, spot.partner),
+        )
+
+    def begin(self, near):
+        for key in self.keys(near):
+            self.swap(key).start()
+
+    def advance(self, near):
+        for key in self.keys(near):
+            self.swap(key).wait_recv() if key else self.swap(key).wait()
+        for step in range(1, self.spot.half):
+            self.across(near, step).start()
+        self.core(near, 0).start()
+
+    def complete(self, near):
+        half = self.spot.half
+        for step in range(1, half):
+            self.across(near, step).wait_recv()
+            self.core(near, step).start()
+        for step in range(half):
+            self.core(near, step).wait_recv()
+        if self.rows_all is not None:
+            self.keep(near).start()
+
+    def pair_copy(self, step, near):
+        spot, at = self.spot, self.number
+        side = self.side(near)
+        return remote(
+            self.back.at[spot.lane_at(step, True), side],
+            self.pair_in.at[step, side],
+            self.pair_send.at[at, step, near],
+            self.pair_recv.at[at, step, near],
+            (spot.place, spot.partner),
+        )
+
     def sum_copy(self, step, near):
         spot, at = self.spot, self.number
-        groups = self.side(near)
+        side = self.side(near)
         return remote(
-            self.across_out.at[step, groups],
-            self.across_in.at[step, groups],
+            self.across_out.at[step, side],
+            self.across_in.at[step, side],
             self.sum_send.at[at, step, near],
             self.sum_recv.at[at, step, near],
             (spot.place, spot.across(step)),
@@ -1883,7 +1928,7 @@
         peer = flip(spot.place, key)
         target = self.back_out.at[spot.place, self.place_rows]
         if key == 0:
-            return pltpu.make_async_copy(self.total.at[peer], target, self.local.at[at, 2])
+            return pltpu.make_async_copy(self.total.at[peer], target, self.local.at[at, 3])
         return remote(
             self.total.at[peer],
             target,
@@ -1892,33 +1937,30 @@
             (peer, spot.lane),
         )
 
-    def pair(self):
+    def pair(self, near):
         for step in list(range(1, self.spot.half)) + [0]:
-            self.pair_copy(step).start()
+            self.pair_copy(step, near).start()
 
     def pair_sum(self, step, near):
-        groups = self.side(near)
-        mine = self.back[self.spot.lane_at(step, False), groups].astype(jnp.float32)
-        return mine + self.pair_in[step, groups].astype(jnp.float32)
-
-    def middle(self):
+        side = self.side(near)
+        mine = self.back[self.spot.lane_at(step, False), side].astype(jnp.float32)
+        return mine + self.pair_in[step, side].astype(jnp.float32)
+
+    def middle(self, near):
         for step in range(1, self.spot.half):
-            self.pair_copy(step).wait_recv()
-        for near in range(2):
-            for step in range(1, self.spot.half):
-                total = self.pair_sum(step, near)
-                self.across_out[step, self.side(near)] = total.astype(jnp.bfloat16)
-                self.sum_copy(step, near).start()
-        self.pair_copy(0).wait_recv()
+            self.pair_copy(step, near).wait_recv()
+            total = self.pair_sum(step, near)
+            self.across_out[step, self.side(near)] = total.astype(self.total.dtype)
+            self.sum_copy(step, near).start()
+        self.pair_copy(0, near).wait_recv()
 
     def last(self, near):
         total = self.pair_sum(0, near)
         for step in range(1, self.spot.half):
             self.sum_copy(step, near).wait_recv()
             total = total + self.across_in[step, self.side(near)].astype(jnp.float32)
-        self.total[self.side(near)] = total.astype(jnp.bfloat16)
-        groups = self.spot.groups
-        for key in near_keys(groups) + [0] if near else far_keys(groups):
+        self.total[self.side(near)] = total.astype(self.total.dtype)
+        for key in self.keys(near):
             self.back_copy(key).start()
 
     def finish(self):
@@ -1926,20 +1968,30 @@
         for key in range(1, groups):
             self.back_copy(key).wait_recv()
         self.back_copy(0).wait()
-        self.keep().wait()
+        for near in range(2):
+            if self.rows_all is not None:
+                self.keep(near).wait()
+            for step in range(half):
+                self.core(near, step).wait_send()
+                self.pair_copy(step, near).wait_send()
+                if step:
+                    self.across(near, step).wait_send()
+                    self.sum_copy(step, near).wait_send()
         for key in range(groups):
             if key:
                 self.swap(key).wait_send()
                 self.back_copy(key).wait_send()
-            for step in range(half):
-                self.core(key, step).wait_send()
-                if step:
-                    self.across(key, step).wait_send()
-        for step in range(half):
-            self.pair_copy(step).wait_send()
-            if step:
-                self.sum_copy(step, 0).wait_send()
-                self.sum_copy(step, 1).wait_send()
+
+
+half_chunks = ((1, 0), (1, 1), (0, 0), (0, 1), (0, 2), (0, 3), (1, 2), (1, 3))
+
+
+def half_expert(step):
+    return step - 2 * ((step // 2 + 1) // 2)
+
+
+def half_far(step):
+    return (step // 2 + 1) // 2 % 2
 
 
 def experts_kernel(
@@ -1947,6 +1999,7 @@
     groups,
     columns,
     rows_in,
+    gates_in,
     grad_main,
     grad_tail,
     gate_weight,
@@ -1958,15 +2011,25 @@
     result_ref,
     rows_all,
     back_out,
+    gates_out,
+    act_sc,
+    act_sems,
     result_main,
     result_tail,
     result_sems,
     *scratch,
 ):
-    expert = pl.program_id(0)
+    now = pl.program_id(0)
+    expert = half_expert(now)
     tail_height = result_tail.shape[2]
+    half_groups = groups // 2
+    sources = half_groups * columns
+    main_count, count = sources * main_slots, sources * CAP
     spot = Spot(groups, columns)
-    mains, tails, sems = scratch[:6], scratch[6:12], scratch[12:]
+    here = spot.place // half_groups
+    side_at = here + half_far(now) * (1 - 2 * here)
+    side = pl.ds(side_at * half_groups, half_groups)
+    mains, tails, sides, sems = scratch[:6], scratch[6:12], scratch[12:18], scratch[18:]
     chunks = [
         RowChunk(
             spot,
@@ -1990,104 +2053,195 @@
         tails,
         sems,
     )
-
-    @pl.when(expert == 0)
+    scalars = RowChunk(
+        spot, experts_here + 1, pl.ds(0, 8), gates_in, None, gates_out, sides, sems
+    )
+
+    @pl.when(now == 0)
     def _():
         spot.meet()
-        tail.begin()
-        chunks[0].begin()
-    select = tail_select(expert, groups * columns, tail_height)
-    raw_hidden = nt_dot(expert_input(grad_main, grad_tail, select), down_weight[0])
-
-    @pl.when(expert == 0)
+        scalars.begin(1)
+        tail.begin(1)
+        chunks[0].begin(1)
+        chunks[1].begin(1)
+        scalars.begin(0)
+        tail.begin(0)
+        chunks[0].begin(0)
+        sides[1][...] = jnp.zeros_like(sides[1])
+
+    select = tail_select(expert, sources, tail_height)
+
+    def joined(main, low):
+        width = main.shape[-1]
+        low = nn_dot(select, low.reshape(-1, width)).astype(jnp.bfloat16)
+        return jnp.concatenate([main.reshape(-1, width), low], axis=0)
+
+    raw_hidden = nt_dot(joined(grad_main[:, side], grad_tail[:, side]), down_weight[0])
+
+    def before(step):
+        if step == 0:
+            scalars.advance(1)
+            tail.advance(1)
+            chunks[0].advance(1)
+            chunks[1].begin(0)
+            chunks[1].advance(1)
+            scalars.complete(1)
+            tail.complete(1)
+        elif step == 1:
+            scalars.advance(0)
+            tail.advance(0)
+            chunks[0].advance(0)
+            chunks[2].begin(0)
+        elif step == 2:
+            chunks[1].advance(0)
+            chunks[3].begin(0)
+            scalars.complete(0)
+            tail.complete(0)
+        elif step == 3:
+            chunks[2].advance(0)
+            chunks[2].begin(1)
+            chunks[3].begin(1)
+        elif step == 4:
+            chunks[3].advance(0)
+        elif step == 5:
+            chunks[2].advance(1)
+        elif step == 6:
+            chunks[3].advance(1)
+        near, at = half_chunks[step]
+        chunks[at].complete(near)
+        if step:
+            near, at = half_chunks[step - 1]
+            chunks[at].middle(near)
+        if step == 6:
+            tail.middle(0)
+            scalars.middle(0)
+
+    for step in range(len(half_chunks)):
+
+        @pl.when(now == step)
+        def _():
+            before(step)
+
+    rows = joined(mains[0][expert, :, side], tails[0][:, side])
+    hot, of_slot = slot_lanes(expert, experts_here, sources)
+    gate_high, gate_rest = split_low(sides[0][:, side, 0, :].reshape(sources, spare))
+    gates = nn_dot(hot, gate_high) + nn_dot(hot, gate_rest)
+    gates = jnp.sum(jnp.where(of_slot, gates, 0.0), axis=1, keepdims=True)
+    hidden, grad_gate, grad_up, back, grad_gates, result = expert_math(
+        rows, gates, raw_hidden, gate_weight[0], up_weight[0], down_weight[0]
+    )
+
+    def spread(value, main_target, tail_target):
+        low = value.astype(jnp.bfloat16)
+        main_target(low[:main_count].reshape(columns, half_groups, main_slots, -1))
+        part = tn_dot(select, low[main_count:]).astype(jnp.bfloat16)
+        part = part.reshape(columns, half_groups, tail_height, -1)
+
+        @pl.when(expert == 0)
+        def _():
+            tail_target[:, side] = part
+
+        @pl.when(expert > 0)
+        def _():
+            tail_target[:, side] += part
+
+    def store_back(value):
+        mains[1][expert, :, side] = value
+
+    spread(back, store_back, tails[1])
+    side_high, side_rest = split_low(jnp.where(of_slot, grad_gates, 0.0))
+    lanes = (tn_dot(hot, side_high) + tn_dot(hot, side_rest)).reshape(columns, half_groups, spare)
+    sides[1][:, side, 0, :] += lanes
+
+    def after(step):
+        near, at = half_chunks[step]
+        chunks[at].pair(near)
+        if step == 5:
+            tail.pair(0)
+            scalars.pair(0)
+        if step == 7:
+            tail.pair(1)
+            scalars.pair(1)
+            chunks[at].middle(1)
+            tail.middle(1)
+            scalars.middle(1)
+        if step:
+            near, at = half_chunks[step - 1]
+            chunks[at].last(near)
+        if step == 6:
+            tail.last(0)
+            scalars.last(0)
+
+    for step in range(len(half_chunks)):
+
+        @pl.when(now == step)
+        def _():
+            after(step)
+
+    act_rows = pl.ds(pl.multiple_of(side_at * count, 32), count)
+
+    def act_copies():
+        outs = (hidden_ref, grad_gate_ref, grad_up_ref)
+        return [
+            pltpu.make_async_copy(act_sc.at[k], out.at[expert, act_rows], act_sems.at[k])
+            for k, out in enumerate(outs)
+        ]
+
+    def result_copy():
+        place = pl.ds(pl.multiple_of(expert * main_slots, main_slots), main_slots)
+        return pltpu.make_async_copy(
+            result_main, result_ref.at[:, side, place], result_sems.at[0]
+        )
+
+    @pl.when(now > 0)
     def _():
-        tail.advance()
-        chunks[0].advance()
-        chunks[1].begin()
-
-    for at in range(experts_here):
-
-        @pl.when(expert == at)
-        def _():
-            if at + 1 < experts_here:
-                chunks[at + 1].advance()
-            if at + 2 < experts_here:
-                chunks[at + 2].begin()
-            if at == 0:
-                tail.complete()
-            chunks[at].complete()
-            if at:
-                chunks[at - 1].middle()
-
-    main_rows, tail_rows, main_back, tail_back = mains[0], tails[0], mains[1], tails[1]
-    wide_rows = expert_input(main_rows.at[expert], tail_rows, select)
-    hidden, grad_gate, grad_up, back, result = expert_math(
-        wide_rows, raw_hidden, gate_weight[0], up_weight[0], down_weight[0]
-    )
-    hidden_ref[0] = hidden
-    grad_gate_ref[0] = grad_gate
-    grad_up_ref[0] = grad_up
-    expert_output(back, select, expert, main_back.at[expert], tail_back)
-
-    for at in range(experts_here):
-
-        @pl.when(expert == at)
-        def _():
-            chunks[at].pair()
-            if at == experts_here - 1:
-                tail.pair()
-                chunks[at].middle()
-                tail.middle()
-            if at:
-                chunks[at - 1].last(0)
-                chunks[at - 1].last(1)
-
-    def result_copy(at):
-        place = pl.ds(pl.multiple_of(at * main_slots, main_slots), main_slots)
-        return pltpu.make_async_copy(result_main, result_ref.at[:, :, place], result_sems.at[0])
-
-    @pl.when(expert > 0)
-    def _():
-        result_copy(expert - 1).wait()
-
-    expert_output(result, select, expert, result_main, result_tail)
-    result_copy(expert).start()
-
-    @pl.when(expert == experts_here - 1)
+        result_copy().wait()
+        for copy in act_copies():
+            copy.wait()
+
+    def store_result(value):
+        result_main[...] = value
+
+    spread(result, store_result, result_tail)
+    act_sc[0] = hidden
+    act_sc[1] = grad_gate
+    act_sc[2] = grad_up
+    result_copy().start()
+    for copy in act_copies():
+        copy.start()
+
+    @pl.when(now == len(half_chunks) - 1)
     def _():
         place = pl.ds(experts_here * main_slots, tail_height)
-        side = pltpu.make_async_copy(result_tail, result_ref.at[:, :, place], result_sems.at[1])
-        side.start()
-        for near in range(2):
-            chunks[-1].last(near)
-            tail.last(near)
-        for chunk in chunks + [tail]:
+        low = pltpu.make_async_copy(result_tail, result_ref.at[:, :, place], result_sems.at[1])
+        low.start()
+        chunks[-1].last(1)
+        tail.last(1)
+        scalars.last(1)
+        for chunk in chunks + [tail, scalars]:
             chunk.finish()
-        result_copy(expert).wait()
-        side.wait()
-
-
-def experts(rows, grads, gate_weight, up_weight, down_weight, columns):
+        result_copy().wait()
+        for copy in act_copies():
+            copy.wait()
+        low.wait()
+
+
+def experts(rows, gates, grads, gate_weight, up_weight, down_weight, columns):
     experts_here, units, width = gate_weight.shape
     groups, height, wide = rows.shape
     half = columns // 2
     count = columns * groups * CAP
     tail_height = height - experts_here * main_slots
-    weight_spec = pl.BlockSpec((1, units, width), lambda e: (e, 0, 0))
-    act_spec = pl.BlockSpec((1, count, units), lambda e: (e, 0, 0))
+    weight_spec = pl.BlockSpec((1, units, width), lambda t: (half_expert(t), 0, 0))
     act_shape = jax.ShapeDtypeStruct((experts_here, count, units), jnp.bfloat16)
     low = lambda *shape: pltpu.VMEM(shape, jnp.bfloat16)
-    bufs = lambda lead, rows_of: [
-        low(*lead, columns, groups, rows_of, wide),
-        low(*lead, columns, groups, rows_of, wide),
-        low(*lead, half, groups, rows_of, wide),
-        low(*lead, half, groups, rows_of, wide),
-        low(*lead, half, groups, rows_of, wide),
-        low(*lead, groups, rows_of, wide),
+    bufs = lambda lead, *block, kind=jnp.bfloat16: [
+        pltpu.VMEM((*lead, *first, groups, *block), kind)
+        for first in ((columns,), (columns,), (half,), (half,), (half,), ())
     ]
     return pl.pallas_call(
         functools.partial(experts_kernel, experts_here, groups, columns),
-        grid=(experts_here,),
+        grid=(len(half_chunks),),
         out_shape=(
             act_shape,
             act_shape,
@@ -2095,19 +2249,23 @@
             jax.ShapeDtypeStruct((columns, groups, height, width), jnp.bfloat16),
             jax.ShapeDtypeStruct((columns,) + rows.shape, jnp.bfloat16),
             jax.ShapeDtypeStruct(rows.shape, jnp.bfloat16),
+            jax.ShapeDtypeStruct(gates.shape, jnp.float32),
         ),
-        in_specs=[anywhere]
-        + row_specs(grads, experts_here, lambda index: lambda e: index(e, 0))
+        in_specs=[anywhere, anywhere]
+        + row_specs(grads, experts_here, lambda index: lambda t: index(half_expert(t), 0))
         + [weight_spec] * 3,
-        out_specs=(act_spec, act_spec, act_spec, anywhere, anywhere, anywhere),
+        out_specs=(anywhere,) * 7,
         scratch_shapes=[
-            low(columns, groups, main_slots, width),
+            low(3, count // 2, units),
+            pltpu.SemaphoreType.DMA((3,)),
+            low(columns, groups // 2, main_slots, width),
             low(columns, groups, tail_height, width),
             pltpu.SemaphoreType.DMA((2,)),
         ]
-        + bufs((experts_here,), main_slots)
-        + bufs((), tail_height)
-        + RowChunk.sems(groups, columns, experts_here + 1),
+        + bufs((experts_here,), main_slots, wide)
+        + bufs((), tail_height, wide)
+        + bufs((), 8, spare, kind=jnp.float32)
+        + RowChunk.sems(groups, columns, experts_here + 2),
         compiler_params=comm_params(10),
         cost_estimate=pl.CostEstimate(
             flops=12 * experts_here * count * width * units,
@@ -2115,11 +2273,12 @@
             bytes_accessed=6 * experts_here * width * units + 8 * experts_here * count * width,
         ),
         name="experts",
-    )(rows, grads, grads, gate_weight, up_weight, down_weight)
+    )(rows, gates, grads, grads, gate_weight, up_weight, down_weight)
 
 
 def expert_weight_kernel(
     parts,
+    halves,
     row_main,
     row_tail,
     grad_main,
@@ -2134,16 +2293,23 @@
     expert, part = pl.program_id(0), pl.program_id(1)
     sources = row_main.shape[0] * row_main.shape[1]
     select = tail_select(expert, sources, row_tail.shape[2])
-    wide_rows = expert_input(row_main, row_tail, select)
-    rows = wide_rows[:, :D]
-    grads = expert_input(grad_main, grad_tail, select)
-    grad_low = (grads.astype(jnp.float32) * gates_of(wide_rows)).astype(jnp.bfloat16)
+    if halves == 1:
+        rows = expert_input(row_main, row_tail, select)[:, :D]
+        grads = expert_input(grad_main, grad_tail, select)
+    else:
+        groups = row_main.shape[1] // halves
+        select = tail_select(expert, sources // halves, row_tail.shape[2])
+        sides = [slice(at * groups, (at + 1) * groups) for at in range(halves)]
+        both = lambda main, low: jnp.concatenate(
+            [expert_input(main[:, side], low[:, side], select) for side in sides], axis=0
+        )
+        rows, grads = both(row_main, row_tail), both(grad_main, grad_tail)
 
     @pl.when(part == 0)
     def _():
         gate_out[0] = tn_dot(grad_gate_ref[0], rows)
         up_out[0] = tn_dot(grad_up_ref[0], rows)
-        down_out[0] = tn_dot(hidden_ref[0], grad_low)
+        down_out[0] = tn_dot(hidden_ref[0], grads)
 
     if parts > 1:
 
@@ -2151,10 +2317,10 @@
         def _():
             gate_out[0] += tn_dot(grad_gate_ref[0], rows)
             up_out[0] += tn_dot(grad_up_ref[0], rows)
-            down_out[0] += tn_dot(hidden_ref[0], grad_low)
-
-
-def expert_weight_grads(rows, grads, hidden, grad_gate, grad_up):
+            down_out[0] += tn_dot(hidden_ref[0], grads)
+
+
+def expert_weight_grads(rows, grads, hidden, grad_gate, grad_up, halves):
     experts_here, count, units = hidden.shape
     width = grads.shape[-1]
     parts = parts_of(rows)
@@ -2163,7 +2329,7 @@
     out_spec = pl.BlockSpec((1, units, width), lambda e, c: (e, 0, 0))
     out_shape = jax.ShapeDtypeStruct((experts_here, units, width), jnp.float32)
     return pl.pallas_call(
-        functools.partial(expert_weight_kernel, parts),
+        functools.partial(expert_weight_kernel, parts, halves),
         grid=(experts_here, parts),
         out_shape=(out_shape, out_shape, out_shape),
         in_specs=row_specs(rows, experts_here, order)
@@ -2241,19 +2407,26 @@
     shard_rows = D // columns_of
     height = slot_rows(experts_here)
 
-    own_columns = lax.dynamic_slice_in_dim(
-        qkv_weight.reshape(shard_rows, 3, groups, width), place, 1, 2
-    ).reshape(shard_rows, 3 * width)
     packed_small = jnp.concatenate(
         [
-            own_columns,
-            router_weight,
-            norm_attn[:, None],
-            norm_moe[:, None],
-            column(bias_table.reshape(-1), shard_rows),
-            jnp.zeros((shard_rows, spare - EXPERTS - 3), jnp.bfloat16),
+            lax.dynamic_slice(
+                qkv_weight, (0, third * D + place * width), (shard_rows, width)
+            )
+            for third in range(3)
+        ]
+        + [jnp.pad(router_weight, ((0, 0), (0, spare - EXPERTS)))],
+        axis=1,
+    )
+    table_rows = BUCKETS // columns_of
+    table_low = bias_table.astype(jnp.float32).reshape(1, table_rows * HEADS)
+    gain_rows = jnp.concatenate(
+        [
+            norm_attn.astype(jnp.float32)[None],
+            norm_moe.astype(jnp.float32)[None],
+            jnp.pad(table_low, ((0, 0), (0, shard_rows - table_rows * HEADS))),
+            jnp.zeros((5, shard_rows), jnp.float32),
         ],
-        axis=1,
+        axis=0,
     )
     token_routes = routes.reshape(row_count, TOP)
     slots = pair_slots(token_routes, priority.reshape(row_count), experts_here)
@@ -2264,9 +2437,9 @@
     slot_pairs = slot_map.astype(jnp.bfloat16).reshape(groups * height, TOP * row_count)
     grad_low = grad_out.reshape(row_count, D)
     grad_slots = nn_dot(slot_any, grad_low).astype(jnp.bfloat16).reshape(groups, height, D)
-    _, normed_all, qkv_own, small_full, out_full, far_slots = entry_gather(
+    _, normed_all, qkv_own, small_full, out_full, far_slots, side_slots, gains = entry_gather(
         inputs.reshape(row_count, D),
-        jnp.broadcast_to(norm_attn.astype(jnp.float32)[None], (8, shard_rows)),
+        gain_rows,
         packed_small,
         out_weight,
         grad_slots,
@@ -2277,17 +2450,12 @@
     qkv_own = qkv_own.reshape(length, 3 * width)
     small_full = small_full.reshape(D, 3 * width + spare)
     out_full = out_full.reshape(D, D)
-    own_weight = small_full[:, : 3 * width]
-    extra = small_full[:, 3 * width :]
-    router_full = extra[:, :EXPERTS]
-    gain_attn = extra[:, EXPERTS].astype(jnp.float32)
-    gain_moe = extra[:, EXPERTS + 1].astype(jnp.float32)
-    table_rows = BUCKETS // columns_of
-    table_full = (
-        extra[:, EXPERTS + 2].reshape(columns_of, shard_rows)[:, : table_rows * HEADS]
-    ).reshape(BUCKETS, HEADS)
+    router_full = small_full[:, 3 * width : 3 * width + EXPERTS]
+    gain_attn = gains[:, 0].reshape(D)
+    gain_moe = gains[:, 1].reshape(D)
+    table_full = gains[:, 2, : table_rows * HEADS].reshape(BUCKETS, HEADS)
     table_own = lax.dynamic_slice_in_dim(
-        table_full.astype(jnp.float32), place * heads_here, heads_here, 1
+        table_full, place * heads_here, heads_here, 1
     )
     near_ids = jnp.asarray(skew_buckets(), jnp.int32)
     near_hot = (near_ids[:, None] == jnp.arange(BUCKETS, dtype=jnp.int32)).astype(jnp.float32)
@@ -2299,7 +2467,7 @@
     far_bias = jnp.stack([table_own[15], table_own[31]], axis=1) * log2e
 
     mixed_own, totals, grads_received = attend_forward(
-        prefix, far_bias, base_bias, qkv_own, grad_slots, far_slots, columns_of
+        prefix, far_bias, base_bias, qkv_own, grad_slots, far_slots, side_slots, columns_of
     )
     attended = exchange_mixed(mixed_own.reshape(groups, row_count, width), columns_of, 8)
 
@@ -2312,35 +2480,59 @@
         lambda logit_in: router_head(logit_in, token_routes, loss_weights), logits
     )
     gate_values = router_out[0]
-    gate_high = lax.reduce_precision(gate_values, 8, 7)
-    gate_parts = jnp.stack([gate_high, gate_values - gate_high], axis=-1).astype(jnp.bfloat16)
-    wide_rows = jnp.concatenate(
-        [
-            jnp.broadcast_to(low_two[None], (TOP, row_count, D)),
-            jnp.pad(jnp.transpose(gate_parts, (1, 0, 2)), ((0, 0), (0, 0), (0, spare - 2))),
-        ],
-        axis=2,
-    ).reshape(TOP * row_count, D + spare)
-    outgoing = nn_dot(slot_pairs, wide_rows).astype(jnp.bfloat16)
-    outgoing = outgoing.reshape(groups, height, D + spare)
+    slot_gates = jnp.sum(
+        slot_map.astype(jnp.float32) * jnp.transpose(gate_values)[None], axis=1
+    )
+    fused = columns_of * groups <= part_sources and experts_here == 4
+    if fused:
+        outgoing = nn_dot(slot_any, low_two).astype(jnp.bfloat16).reshape(groups, height, D)
+        gate_block = jnp.pad(
+            jnp.sum(slot_gates, axis=1).reshape(groups, 1, height),
+            ((0, 0), (0, 7), (0, spare - height)),
+        )
+    else:
+        gate_high = lax.reduce_precision(gate_values, 8, 7)
+        gate_parts = jnp.stack([gate_high, gate_values - gate_high], axis=-1).astype(jnp.bfloat16)
+        wide_rows = jnp.concatenate(
+            [
+                jnp.broadcast_to(low_two[None], (TOP, row_count, D)),
+                jnp.pad(jnp.transpose(gate_parts, (1, 0, 2)), ((0, 0), (0, 0), (0, spare - 2))),
+            ],
+            axis=2,
+        ).reshape(TOP * row_count, D + spare)
+        outgoing = nn_dot(slot_pairs, wide_rows).astype(jnp.bfloat16)
+        outgoing = outgoing.reshape(groups, height, D + spare)
     gate_across, up_across, down_across = (
         jnp.transpose(weight, (0, 2, 1)) for weight in (gate_weight, up_weight, down_weight)
     )
-    if columns_of * groups <= part_sources:
-        hidden, grad_gate, grad_up, result_part, rows_received, grad_returned = experts(
-            outgoing, grads_received, gate_across, up_across, down_across, columns_of
-        )
+    if fused:
+        (
+            hidden,
+            grad_gate,
+            grad_up,
+            result_part,
+            rows_received,
+            grad_returned,
+            side_returned,
+        ) = experts(
+            outgoing, gate_block, grads_received, gate_across, up_across, down_across, columns_of
+        )
+        slot_grads = side_returned[:, 0, :height].reshape(groups * height)
+        grad_gates = jnp.sum(
+            jnp.where(slot_map, slot_grads[:, None, None], 0.0), axis=0
+        )
+        grad_gates = jnp.transpose(grad_gates)
+        grad_returned = grad_returned.reshape(groups * height, D)
     else:
         rows_received = dispatch(outgoing, columns_of, 2)
         hidden, grad_gate, grad_up, result_part, back_part = expert_act(
             rows_received, grads_received, gate_across, up_across, down_across
         )
-        grad_returned = collect(back_part, 3)
-    grad_returned = grad_returned.reshape(groups * height, D + spare)
+        grad_returned = collect(back_part, 3).reshape(groups * height, D + spare)
+        grad_gates = jnp.transpose(
+            tn_dot(slot_pairs, grad_returned[:, D:])[:, 0].reshape(TOP, row_count)
+        )
     grad_low_two = tn_dot(slot_any, grad_returned[:, :D])
-    grad_gates = jnp.transpose(
-        tn_dot(slot_pairs, grad_returned[:, D:])[:, 0].reshape(TOP, row_count)
-    )
     grad_top = grad_low.astype(jnp.float32)
     grad_logits = router_back((grad_gates, jnp.ones((), jnp.float32)))[0]
     low_logits = grad_logits.astype(jnp.bfloat16)
@@ -2356,7 +2548,7 @@
         grad_attended, "expert", split_axis=0, concat_axis=0, tiled=True
     )
     gate_grad, up_grad, down_grad = expert_weight_grads(
-        rows_received, grads_received, hidden, grad_gate, grad_up
+        rows_received, grads_received, hidden, grad_gate, grad_up, 2 if fused else 1
     )
     out_sums = lax.psum_scatter(
         out_grad.astype(jnp.bfloat16), "shard", scatter_dimension=0, tiled=True
@@ -2373,9 +2565,6 @@
         out_sums,
         columns_of,
     )
-    slot_gates = jnp.sum(
-        slot_map.astype(jnp.float32) * jnp.transpose(gate_values)[None], axis=1
-    )
     slot_high = lax.reduce_precision(slot_gates, 8, 7)
     slot_parts = jnp.concatenate([slot_high, slot_gates - slot_high], axis=1).astype(jnp.bfloat16)
     mixture = tn_dot(slot_parts, returned.reshape(groups * height, D))
@@ -2410,8 +2599,7 @@
     grad_projected, last_all, out_all, qkv_full = tail_exchange(
         grad_qkv.reshape(groups, row_count, 3 * width),
         normed_all,
-        own_weight,
-        gain_attn[:, None],
+        small_full,
         extra,
         out_piece,
         qkv_weight,
@@ -2442,7 +2630,7 @@
             last_all[:, :, : 3 * width].reshape(groups, shard_rows, 3, width), (1, 2, 0, 3)
         ).reshape(shard_rows, 3 * D).astype(jnp.float32)
         out_total = out_all.astype(jnp.float32)
-        extra_total = jnp.sum(last_all[:, :, 3 * width :].astype(jnp.float32), axis=0)
+        extra_total = jnp.sum(last_all[:, :, 3 * width :].astype(jnp.float32), axis=0).T
     table_part = last_all[:, : table_rows * heads_here, 3 * width + 1].astype(jnp.float32)
     table_total = jnp.transpose(
         table_part.reshape(groups, table_rows, heads_here), (1, 0, 2)
@@ -2450,12 +2638,12 @@
     return (
         output.reshape(row_count, 1, D),
         input_grad.reshape(row_count, 1, D),
-        extra_total[:, 0],
-        extra_total[:, 2],
+        extra_total[0] / norm_attn.astype(jnp.float32),
+        extra_total[2],
         qkv_total,
         out_total,
         table_total,
-        extra_total[:, 3 : 3 + EXPERTS],
+        extra_total[3 : 3 + EXPERTS].T,
         jnp.transpose(gate_grad, (0, 2, 1)),
         jnp.transpose(up_grad, (0, 2, 1)),
         jnp.transpose(down_grad, (0, 2, 1)),

time: 445 us -> 427 us (0.960); the launches traced: 436 us -> 425 us
  Pallas kernels: 362 us -> 357 us
    pallas_call x1, Pallas kernels: 102 us -> 97.2 us  [experts(): pl.pallas_call(functools.partial(experts_kernel, experts_here, groups, co...]
    unnamed x39 -> x32, local copies, waits for them, and re-layouts: 9.01 us -> 4.56 us
  transfers between devices with their start and end apart: 2 -> 2, of which waited for: 0 -> 1; matrix products, arithmetic and copies ran while one was open for 1% -> 1% of each run, Pallas kernels for 5% -> 5%
where the time goes in v4:
time: 427 us; the launch traced here: 425 us
  Pallas kernels  357 us (84%)
  local copies, waits for them, and re-layouts  19.1 us (4%)
  matrix products  17.1 us (4%)
  between operations  15.7 us (4%)
  other arithmetic  10.7 us (3%)
    pallas_call x1, Pallas kernels, experts(): pl.pallas_call(functools.partial(experts_kernel, experts_here, groups, co...  97.2 us
    pallas_call x1, Pallas kernels, entry_gather(): pl.pallas_call(functools.partial(entry_kernel, groups, columns), out_shap...  66.4 us
    pallas_call x1, Pallas kernels, tail_exchange(): pl.pallas_call(functools.partial(tail_kernel, groups, columns, chunks), o...  59.8 us
    pallas_call x1, Pallas kernels, attend_backward(): pl.pallas_call(functools.partial(attend_backward_kernel, heads_here, grou...  51.1 us
    pallas_call x1, Pallas kernels, attend_forward(): pl.pallas_call(functools.partial(attend_forward_kernel, heads_here, group...  34.8 us
    pallas_call x1, Pallas kernels, expert_weight_grads(): pl.pallas_call(functools.partial(expert_weight_kernel, parts, halves), gr...  22.2 us
    pallas_call x1, Pallas kernels, exchange_mixed(): pl.pallas_call(functools.partial(mixed_kernel, groups, columns), out_shap...  15.9 us
    pallas_call x1, Pallas kernels, finish(): pl.pallas_call(functools.partial(finish_kernel, width), grid=(3,), out_sh...  10.1 us
  transfers between devices with their start and end apart: 2, of which 1 were waited for; matrix products, arithmetic and copies ran while one was open for 1% of the time, Pallas kernels for 5%

profile of v4, /device:TPU:0, one launch (start us, length us, event | category | flops | bytes accessed | tf_op | source)
XLA Modules:
  0.0 425.0 jit_solution(1647680877988663485)
XLA Ops:
  7.2 0.8 reshape.335
  8.0 0.7 broadcast_add_fusion
  8.7 0.7 broadcast_in_dim.133
  9.3 0.7 convert_element_type.61
  10.0 0.8 slice_bitcast_fusion.2
  10.8 0.7 pad_add_fusion
  11.5 0.3 convert_reduce_fusion
  11.8 0.8 copy.102
  12.7 0.2 fusion.1
  13.0 2.5 convolution_convert_fusion.2
  15.5 0.7 maximum_maximum_fusion.gain
  16.2 0.9 constant_dynamic-slice_fusion.2
  17.1 0.7 fusion.17.pack
  17.9 66.4 %entry_gather.1 = (bf16[8,256,1024]{2,1,0:T(8,128)(2,1)}, bf16[8,256,1024]{2,1,0:T(8,128)(2,1)}, bf16[8,256,384]{2,1,0:T(8,128)(2,1)}, bf16[4,256,512]{2,1,0:T(8...) custom-call(bf16[256,1024]{1,0:T(8,128)(2,1)} %bitcast.109, ...), custom_call_target="tpu_custom_call" | custom-call | tf_op jit(solution)/shard_map/entry_gather/pallas_call | solution.py:412
  84.2 0.7 slice_reduce_fusion.1
  85.0 1.4 fusion.37
  87.1 0.6 convolution_multiply_fusion
  88.0 0.6 reshape.340.base_ref
  88.7 0.6 maximum_multiply_fusion.far_ref
  89.3 34.8 %attend_forward.1 = (bf16[2048,128]{1,0:T(8,128)(2,1)}, f32[8,2,256]{2,1,0:T(2,128)}, bf16[4,8,72,1024]{3,2,1,0:T(8,128)(2,1)}) custom-call(s32[1]{0:T(128)S(6)} %copy.122.prefix_ref, f32[2,2]{1,0:T(2,128)} %maximum_multiply_fusion.far_ref, f32[6,512]{1,0:T(8,128)} %reshape.340.base_ref, bf16[2048,384]{1,0:T(8,128)(2,1)} %bitcast.145, ...), custom_call_target="tpu_custom_call" | custom-call | flops 21474836480 | bytes 2097152 | tf_op jit(solution)/shard_map/attend_forward/pallas_call | solution.py:1311
  124.1 15.9 %exchange_mixed.1 = bf16[256,1024]{1,0:T(8,128)(2,1)} custom-call(bf16[8,256,128]{2,1,0:T(8,128)(2,1)} %bitcast.120), custom_call_target="tpu_custom_call" | custom-call | tf_op jit(solution)/shard_map/exchange_mixed/pallas_call | solution.py:784
  140.1 1.9 multiply_reduce_fusion.2
  141.9 0.2 multiply_convert_fusion
  142.1 1.2 fusion.39
  143.4 1.5 convolution_convert_fusion.1
  144.9 0.6 fusion.38
  145.5 0.1 select_reduce_fusion.3
  145.7 0.2 select_reduce_fusion.1
  146.0 0.6 pad.23.gates_in
  146.6 97.2 %experts.1 = (bf16[4,576,704]{2,1,0:T(8,128)(2,1)}, bf16[4,576,704]{2,1,0:T(8,128)(2,1)}, bf16[4,576,704]{2,1,0:T(8,128)(2,1)}, bf16[4,8,72,1024]{3,2,1,0:T(8,12...) custom-call(bf16[8,72,1024]{2,1,0:T(8,128)(2,1)} %bitcast.116, ...), custom_call_target="tpu_custom_call" | custom-call | flops 19931332608 | bytes 36175872 | tf_op jit(solution)/shard_map/experts/pallas_call | solution.py:2242
  243.8 1.9 fusion.40
  245.7 0.8 slice_reduce_fusion
  246.5 0.2 select_reduce_fusion.2
  247.6 0.7 negate_add_fusion
  248.3 1.6 multiply_reduce_fusion
  249.9 0.3 fusion.5.grad_middle
  250.2 0.7 copy-done.2
  251.0 2.1 convolution_convert_fusion
  253.1 2.3 fusion
  255.4 0.9 copy.121
  256.3 3.9 all-to-all-start
  260.2 0.2 convolution_convert_fusion.4
  260.5 0.2 copy.110
  260.7 0.2 broadcast_in_dim.134
  261.0 22.2 %expert_weight_grads.1 = (f32[4,704,1024]{2,1,0:T(8,128)}, f32[4,704,1024]{2,1,0:T(8,128)}, f32[4,704,1024]{2,1,0:T(8,128)}) custom-call(bf16[4,8,72,1024]{3,2,1,0:T(8,128)(2,1)} %get-tuple-element.70.row_main.row_tail, bf16[4,8,72,1024]{3,2,1,0:T(8,128)(2,1)} %get-tuple-element.70.row_main.row_tail, ...), custom_call_target="tpu_custom_call" | custom-call | flops 9965666304 | bytes 58195968 | tf_op jit(solution)/shard_map/expert_weight_grads/pallas_call | solution.py:2331
  283.1 1.0 reduce-scatter.2.cloned.1.call-done
  284.1 51.1 %attend_backward.1 = (bf16[2048,384]{1,0:T(8,128)(2,1)}, f32[6,512]{1,0:T(8,128)}, f32[2,2,8,256]{3,2,1,0:T(8,128)}, bf16[8,72,1024]{2,1,0:T(8,128)(2,1)}, bf16[32,1024]{1,0:T(8,128)(2,1)}) custom-call(s32[1]{0:T(128)S(6)} %copy.122.prefix_ref, f32[2,2]{1,0:T(2,128)} %maximum_multiply_fusion.far_ref, f32[6,512]{1,0:T(8,128)} %reshape.340.base_ref, ...), custom_call_target="tpu_custom_call" | custom-call | flops 37580963840 | bytes 4194304 | tf_op jit(solution)/shard_map/attend_backward/pallas_call | solution.py:1536
  335.2 0.9 reduce_sum.181
  336.0 0.2 slice_reduce_fusion.3
  336.2 0.7 reshape.355
  337.0 0.2 fusion.4
  337.4 0.2 copy.117
  337.7 1.3 concatenate.52.extra
  339.0 59.8 %tail_exchange.1 = (bf16[256,3072]{1,0:T(8,128)(2,1)}, bf16[8,2,128,512]{3,2,1,0:T(8,128)(2,1)}, bf16[8,32,1024]{2,1,0:T(8,128)(2,1)}, bf16[4,256,3072]{2,1,0:T(8,128)(2,1)}) custom-call(bf16[8,256,384]{2,1,0:T(8,128)(2,1)} %bitcast.115, bf16[2048,1024]{1,0:T(8,128)(2,1)} %bitcast.111, bf16[1024,512]{1,0:T(8,128)(2,1)} %bitcast.114, ...), custom_call_target="tpu_custom_call" | custom-call | tf_op jit(solution)/shard_map/tail_exchange/pallas_call | solution.py:911
  398.8 0.8 slice_convert_fusion
  399.7 10.1 %finish.1 = (f32[256,1024]{1,0:T(8,128)}, f32[256,3072]{1,0:T(8,128)}, f32[256,1024]{1,0:T(8,128)}, f32[128,256]{1,0:T(8,128)}) custom-call(bf16[256,3072]{1,0:T(8,128)(2,1)} %get-tuple-element.62.grads, bf16[4,256,3072]{2,1,0:T(8,128)(2,1)} %get-tuple-element.63.weight, bf16[8,256,512]{2,1,0:T(8,128)(2,1)} %bitcast.103, bf16[8,256,512]{2,1,0:T(8,128)(2,1)} %bitcast.104, ...), custom_call_target="tpu_custom_call" | custom-call | tf_op jit(solution)/shard_map/finish/pallas_call | solution.py:980
  409.8 1.3 fusion.36
  411.1 1.4 slice_bitcast_fusion
  412.5 1.0 fusion.9
  413.5 1.1 fusion.13
  414.6 0.2 copy.111
  414.8 0.7 copy.114
  415.5 2.0 copy.113
  417.6 0.6 convert_divide_fusion
  (66 shorter events, 1.5 us)
Async XLA Ops:
  7.2 276.9 %reduce-scatter.2.cloned.1.call-start = ((), (), s32[]{:S(2)}) async-start(), calls=%async_computation.2 | async-start | bytes 2621440 | tf_op jit(solution)/shard_map/reduce_scatter | solution.py:2553
  17.1 70.0 %copy-start.12 = (s32[1536]{0:T(1024)S(1)}, s32[1536]{0:T(1024)}, u32[]{:S(2)}) copy-start(s32[1536]{0:T(1024)} %constant.106.clone) | copy-start | bytes 18436
  89.3 50.7 %copy-start.1 = (bf16[4,256,1024]{2,1,0:T(8,128)(2,1)S(1)}, bf16[4,256,1024]{2,1,0:T(8,128)(2,1)}, u32[]{:S(2)}) copy-start(bf16[4,256,1024]{2,1,0:T(8,128)(2,1)} %get-tuple-element.49) | copy-start | bytes 6291460
  89.3 50.8 %copy-start.3 = (bf16[256,1,1024]{2,0,1:T(8,128)(2,1)S(1)}, bf16[256,1,1024]{2,0,1:T(8,128)(2,1)}, u32[]{:S(2)}) copy-start(bf16[256,1,1024]{2,0,1:T(8,128)(2,1)} %param.16) | copy-start | bytes 1572868
  142.1 2.8 copy-start.8
  142.1 3.4 copy-start.7
  248.3 1.6 copy-start.4
  249.9 1.0 copy-start.2
  251.0 2.1 copy-start
  256.3 26.8 %all-to-all-start = ((bf16[8,256,128]{2,1,0:T(8,128)(2,1)}), bf16[8,256,128]{2,1,0:T(8,128)(2,1)S(1)}, u32[]{:S(2)}, u32[]{:S(2)}) async-start(bf16[8,256,128]{2,1,0:T(8,128)(2,1)} %bitcast.101), calls=%async_computation | async-start | bytes 1048576 | tf_op jit(solution)/shard_map/all_to_all | solution.py:2547
  283.1 1.0 copy-start.6
  284.1 52.8 %copy-start.11 = (s32[3,512]{1,0:T(4,128)S(1)}, s32[3,512]{1,0:T(4,128)}, u32[]{:S(2)}) copy-start(s32[3,512]{1,0:T(4,128)} %constant.123) | copy-start | bytes 18436
  399.7 12.9 %copy-start.10 = (bf16[8,72,1024]{2,1,0:T(8,128)(2,1)S(1)}, bf16[8,72,1024]{2,1,0:T(8,128)(2,1)}, u32[]{:S(2)}) copy-start(bf16[8,72,1024]{2,1,0:T(8,128)(2,1)} %get-tuple-element.56) | copy-start | bytes 3538948
  413.5 2.0 copy-start.5
  414.6 3.0 copy-start.9
Sparse Core Ops, SparseCore 0:
  253.2 30.8 reduce-scatter.1

commit v5 on v4

--- a/solution.py
+++ b/solution.py
@@ -103,8 +103,8 @@
 
 
 class LineGather:
-    def __init__(self, spot, own, full, local_sem, send_sems, recv_sems):
-        self.spot, self.own, self.full = spot, own, full
+    def __init__(self, spot, own, full, local_sem, send_sems, recv_sems, rows=None):
+        self.spot, self.own, self.full, self.rows = spot, own, full, rows
         self.local_sem, self.send_sems, self.recv_sems = local_sem, send_sems, recv_sems
         self.long, self.wide = line_shape(spot.groups)
         self.z = spot.place // self.wide
@@ -119,10 +119,13 @@
             pltpu.SemaphoreType.DMA((groups,)),
         ]
 
+    def block(self, origin):
+        return self.full.at[origin] if self.rows is None else self.full.at[origin, self.rows]
+
     def copy(self, job, way, origin, source, target):
         return remote(
             source,
-            self.full.at[origin],
+            self.block(origin),
             self.send_sems.at[job, way],
             self.recv_sems.at[origin],
             (target, self.spot.lane),
@@ -149,7 +152,7 @@
     def begin(self):
         place = self.spot.place
         self.each(0, place, self.own, True, True, lambda copy: copy.start())
-        pltpu.make_async_copy(self.own, self.full.at[place], self.local_sem).start()
+        pltpu.make_async_copy(self.own, self.block(place), self.local_sem).start()
 
     def arrive(self, origin):
         self.copy(0, 0, origin, self.own, self.spot.place).wait_recv()
@@ -161,14 +164,14 @@
         def _():
             origin = place - k * wide
             self.arrive(origin)
-            self.each(k, origin, self.full.at[origin], True, False, lambda copy: copy.start())
+            self.each(k, origin, self.block(origin), True, False, lambda copy: copy.start())
 
         @pl.when(self.z + k < self.long)
         def _():
             origin = place + k * wide
             self.arrive(origin)
             job = self.long - 1 + k
-            self.each(job, origin, self.full.at[origin], False, True, lambda copy: copy.start())
+            self.each(job, origin, self.block(origin), False, True, lambda copy: copy.start())
 
     def finish(self):
         for row in range(self.long):
@@ -185,15 +188,15 @@
             @pl.when(self.z >= k)
             def _():
                 origin = place - k * wide
-                self.each(k, origin, self.full.at[origin], True, False, stop)
+                self.each(k, origin, self.block(origin), True, False, stop)
 
             @pl.when(self.z + k < self.long)
             def _():
                 origin = place + k * wide
                 job = self.long - 1 + k
-                self.each(job, origin, self.full.at[origin], False, True, stop)
-
-        pltpu.make_async_copy(self.own, self.full.at[place], self.local_sem).wait()
+                self.each(job, origin, self.block(origin), False, True, stop)
+
+        pltpu.make_async_copy(self.own, self.block(place), self.local_sem).wait()
 
 
 class ColumnGather:
@@ -288,7 +291,15 @@
     *sems,
 ):
     spot = Spot(groups, columns)
-    line = LineGather(spot, tokens, tokens_all, *sems[:3])
+    half_rows = tokens.shape[0] // 2
+    lines = [
+        LineGather(spot, tokens.at[rows_at], tokens_all, *line_sems, rows=rows_at)
+        for rows_at, line_sems in (
+            (pl.ds(0, half_rows), sems[:3]),
+            (pl.ds(half_rows, half_rows), sems[3:6]),
+        )
+    ]
+    line, sems = lines[0], sems[3:]
     gains = ColumnGather(spot, gain, gain_sc, *sems[3:8])
     packs = ColumnGather(spot, pack, pack_sc, *sems[8:13])
     outs = ColumnGather(spot, out_weight, out_all, *sems[13:18])
@@ -338,7 +349,8 @@
             store.start()
 
     spot.meet()
-    line.begin()
+    for line in lines:
+        line.begin()
     gains.begin()
     packs.begin()
     outs.begin()
@@ -351,14 +363,17 @@
     keep_gain = pltpu.make_async_copy(gain_sc, gain_all, gain_sem)
     keep_gain.start()
     project(spot.place, tokens)
-    line.hop(1)
+    for line in lines:
+        line.hop(1)
     outs.forward()
     for step in range(1, spot.half):
         side_copy(0, step).start()
-    line.hop(2)
+    for line in lines:
+        line.hop(2)
     for key in early_keys(groups):
         far_copy(key).start()
-    line.hop(3)
+    for line in lines:
+        line.hop(3)
 
     def own_column(row, carry):
         @pl.when(row != line.z)
@@ -382,13 +397,15 @@
         def _():
             for step in range(1, line.wide):
                 origin = row * line.wide + (line.y + step) % line.wide
-                line.arrive(origin)
+                for part in lines:
+                    part.arrive(origin)
                 project(origin, tokens_all.at[origin])
 
         return carry
 
     lax.fori_loop(0, 2 * line.long - 1, other_column, 0)
-    line.settle()
+    for line in lines:
+        line.settle()
     for key in early_keys(groups):
         far_copy(key).wait_send()
     for key in [0] + early_keys(groups):
@@ -435,7 +452,7 @@
             dma(()),
             dma(()),
         ]
-        + LineGather.sems(groups)
+        + LineGather.sems(groups) * 2
         + ColumnGather.sems(columns) * 3
         + [dma((groups,))] * 2
         + [dma((groups, columns // 2))] * 2,
@@ -1280,17 +1297,17 @@
         totals_ref[0, pl.ds(head, 1), :] = tops[head] + jnp.log2(total)
     mixed_ref[...] = jnp.transpose(jnp.concatenate(parts, axis=0)).astype(jnp.bfloat16)
 
-    @pl.when(query_tile == tiles // 4)
+    @pl.when(query_tile == tiles // 2)
     def _():
         for key in job.near:
             job.advance(key)
 
-    @pl.when(query_tile == tiles // 2)
+    @pl.when(query_tile == tiles - 2)
     def _():
         for key in job.near[:1]:
             job.pass_on(key)
 
-    @pl.when(query_tile == tiles - 3)
+    @pl.when(query_tile == tiles - 2)
     def _():
         for key in job.rest:
             job.advance(key)
@@ -2434,6 +2451,10 @@
         jnp.arange(groups * height, dtype=jnp.int32)[:, None] == slots[None, :]
     ).reshape(groups * height, TOP, row_count)
     slot_any = jnp.any(slot_map, axis=1).astype(jnp.bfloat16)
+    token_slots = jnp.any(
+        slots.reshape(TOP, row_count)[:, :, None] == jnp.arange(groups * height, dtype=jnp.int32),
+        axis=0,
+    ).astype(jnp.bfloat16)
     slot_pairs = slot_map.astype(jnp.bfloat16).reshape(groups * height, TOP * row_count)
     grad_low = grad_out.reshape(row_count, D)
     grad_slots = nn_dot(slot_any, grad_low).astype(jnp.bfloat16).reshape(groups, height, D)
@@ -2532,7 +2553,7 @@
         grad_gates = jnp.transpose(
             tn_dot(slot_pairs, grad_returned[:, D:])[:, 0].reshape(TOP, row_count)
         )
-    grad_low_two = tn_dot(slot_any, grad_returned[:, :D])
+    grad_low_two = nn_dot(token_slots, grad_returned[:, :D])
     grad_top = grad_low.astype(jnp.float32)
     grad_logits = router_back((grad_gates, jnp.ones((), jnp.float32)))[0]
     low_logits = grad_logits.astype(jnp.bfloat16)

time: 427 us -> 425 us (level)
  no operation moved by 1% of the time
where the time goes in v5:
time: 425 us; the launch traced here: 423 us
  Pallas kernels  355 us (84%)
  local copies, waits for them, and re-layouts  20.8 us (5%)
  between operations  15.7 us (4%)
  matrix products  15.1 us (4%)
  other arithmetic  11.6 us (3%)
    pallas_call x1, Pallas kernels, experts(): pl.pallas_call(functools.partial(experts_kernel, experts_here, groups, co...  98.8 us
    pallas_call x1, Pallas kernels, entry_gather(): pl.pallas_call(functools.partial(entry_kernel, groups, columns), out_shap...  63.2 us
    pallas_call x1, Pallas kernels, tail_exchange(): pl.pallas_call(functools.partial(tail_kernel, groups, columns, chunks), o...  59.8 us
    pallas_call x1, Pallas kernels, attend_backward(): pl.pallas_call(functools.partial(attend_backward_kernel, heads_here, grou...  51.3 us
    pallas_call x1, Pallas kernels, attend_forward(): pl.pallas_call(functools.partial(attend_forward_kernel, heads_here, group...  35.1 us
    pallas_call x1, Pallas kernels, expert_weight_grads(): pl.pallas_call(functools.partial(expert_weight_kernel, parts, halves), gr...  22.1 us
    pallas_call x1, Pallas kernels, exchange_mixed(): pl.pallas_call(functools.partial(mixed_kernel, groups, columns), out_shap...  14.9 us
    pallas_call x1, Pallas kernels, finish(): pl.pallas_call(functools.partial(finish_kernel, width), grid=(3,), out_sh...  10.1 us
  transfers between devices with their start and end apart: 2, of which 1 were waited for; matrix products, arithmetic and copies ran while one was open for 1% of the time, Pallas kernels for 5%

profile of v5, /device:TPU:0, one launch (start us, length us, event | category | flops | bytes accessed | tf_op | source)
XLA Modules:
  0.0 423.4 jit_solution(33914910876804236)
XLA Ops:
  7.2 0.8 reshape.474
  8.0 0.7 broadcast_add_fusion
  8.7 0.7 broadcast_in_dim.134
  9.3 0.7 convert_element_type.62
  10.0 0.8 slice_bitcast_fusion.2
  10.8 0.7 pad_add_fusion
  11.4 0.3 convert_reduce_fusion
  11.8 0.8 copy.102
  12.7 0.2 fusion.1
  13.0 2.5 convolution_convert_fusion.2
  15.5 0.7 maximum_maximum_fusion.gain
  16.2 0.9 constant_dynamic-slice_fusion.2
  17.1 0.7 fusion.18.pack
  17.9 63.2 %entry_gather.1 = (bf16[8,256,1024]{2,1,0:T(8,128)(2,1)}, bf16[8,256,1024]{2,1,0:T(8,128)(2,1)}, bf16[8,256,384]{2,1,0:T(8,128)(2,1)}, bf16[4,256,512]{2,1,0:T(8...) custom-call(bf16[256,1024]{1,0:T(8,128)(2,1)} %bitcast.109, ...), custom_call_target="tpu_custom_call" | custom-call | tf_op jit(solution)/shard_map/entry_gather/pallas_call | solution.py:429
  81.1 0.7 slice_reduce_fusion.1
  81.9 1.4 fusion.37
  84.0 0.6 convolution_multiply_fusion
  84.9 0.6 reshape.479.base_ref
  85.6 0.6 maximum_multiply_fusion.far_ref
  86.2 35.1 %attend_forward.1 = (bf16[2048,128]{1,0:T(8,128)(2,1)}, f32[8,2,256]{2,1,0:T(2,128)}, bf16[4,8,72,1024]{3,2,1,0:T(8,128)(2,1)}) custom-call(s32[1]{0:T(128)S(6)} %copy.122.prefix_ref, f32[2,2]{1,0:T(2,128)} %maximum_multiply_fusion.far_ref, f32[6,512]{1,0:T(8,128)} %reshape.479.base_ref, bf16[2048,384]{1,0:T(8,128)(2,1)} %bitcast.145, ...), custom_call_target="tpu_custom_call" | custom-call | flops 21474836480 | bytes 2097152 | tf_op jit(solution)/shard_map/attend_forward/pallas_call | solution.py:1328
  121.3 14.9 %exchange_mixed.1 = bf16[256,1024]{1,0:T(8,128)(2,1)} custom-call(bf16[8,256,128]{2,1,0:T(8,128)(2,1)} %bitcast.120), custom_call_target="tpu_custom_call" | custom-call | tf_op jit(solution)/shard_map/exchange_mixed/pallas_call | solution.py:801
  136.2 1.9 multiply_reduce_fusion.2
  138.3 1.0 copy-done.4
  139.3 0.3 fusion.39
  139.7 1.5 convolution_convert_fusion.1
  141.2 0.6 fusion.38
  141.7 0.2 fusion.2
  142.1 0.2 select_reduce_fusion.1
  142.4 0.6 pad.23.gates_in
  143.0 98.8 %experts.1 = (bf16[4,576,704]{2,1,0:T(8,128)(2,1)}, bf16[4,576,704]{2,1,0:T(8,128)(2,1)}, bf16[4,576,704]{2,1,0:T(8,128)(2,1)}, bf16[4,8,72,1024]{3,2,1,0:T(8,12...) custom-call(bf16[8,72,1024]{2,1,0:T(8,128)(2,1)} %bitcast.116, ...), custom_call_target="tpu_custom_call" | custom-call | flops 19931332608 | bytes 36175872 | tf_op jit(solution)/shard_map/experts/pallas_call | solution.py:2259
  241.8 0.8 slice_reduce_fusion
  242.7 0.2 select_reduce_fusion.2
  243.8 1.9 fusion.40
  245.7 0.7 negate_add_fusion
  246.3 0.6 multiply_reduce_fusion
  247.0 0.4 copy-done.5
  247.4 0.3 fusion.6.grad_middle
  247.7 0.7 copy-done.2
  248.4 2.1 convolution_convert_fusion
  250.5 2.3 fusion
  252.9 0.9 copy.121
  253.8 4.1 all-to-all-start
  257.9 0.2 convolution_convert_fusion.4
  258.3 0.2 broadcast_in_dim.135
  258.6 0.8 reduce-precision_convert_fusion
  259.3 22.1 %expert_weight_grads.1 = (f32[4,704,1024]{2,1,0:T(8,128)}, f32[4,704,1024]{2,1,0:T(8,128)}, f32[4,704,1024]{2,1,0:T(8,128)}) custom-call(bf16[4,8,72,1024]{3,2,1,0:T(8,128)(2,1)} %get-tuple-element.70.row_main.row_tail, bf16[4,8,72,1024]{3,2,1,0:T(8,128)(2,1)} %get-tuple-element.70.row_main.row_tail, ...), custom_call_target="tpu_custom_call" | custom-call | flops 9965666304 | bytes 58195968 | tf_op jit(solution)/shard_map/expert_weight_grads/pallas_call | solution.py:2348
  281.4 0.6 reduce-scatter.2.cloned.1.call-done
  282.0 0.2 copy-done.7
  282.2 51.3 %attend_backward.1 = (bf16[2048,384]{1,0:T(8,128)(2,1)}, f32[6,512]{1,0:T(8,128)}, f32[2,2,8,256]{3,2,1,0:T(8,128)}, bf16[8,72,1024]{2,1,0:T(8,128)(2,1)}, bf16[32,1024]{1,0:T(8,128)(2,1)}) custom-call(s32[1]{0:T(128)S(6)} %copy.122.prefix_ref, f32[2,2]{1,0:T(2,128)} %maximum_multiply_fusion.far_ref, f32[6,512]{1,0:T(8,128)} %reshape.479.base_ref, ...), custom_call_target="tpu_custom_call" | custom-call | flops 37580963840 | bytes 4194304 | tf_op jit(solution)/shard_map/attend_backward/pallas_call | solution.py:1553
  333.6 0.9 reduce_sum.181
  334.6 0.7 reshape.494
  335.4 0.2 fusion.5
  335.8 0.2 copy.117
  336.1 1.3 concatenate.77.extra
  337.4 59.8 %tail_exchange.1 = (bf16[256,3072]{1,0:T(8,128)(2,1)}, bf16[8,2,128,512]{3,2,1,0:T(8,128)(2,1)}, bf16[8,32,1024]{2,1,0:T(8,128)(2,1)}, bf16[4,256,3072]{2,1,0:T(8,128)(2,1)}) custom-call(bf16[8,256,384]{2,1,0:T(8,128)(2,1)} %bitcast.115, bf16[2048,1024]{1,0:T(8,128)(2,1)} %bitcast.111, bf16[1024,512]{1,0:T(8,128)(2,1)} %bitcast.112, ...), custom_call_target="tpu_custom_call" | custom-call | tf_op jit(solution)/shard_map/tail_exchange/pallas_call | solution.py:928
  397.2 0.8 slice_convert_fusion
  398.1 10.1 %finish.1 = (f32[256,1024]{1,0:T(8,128)}, f32[256,3072]{1,0:T(8,128)}, f32[256,1024]{1,0:T(8,128)}, f32[128,256]{1,0:T(8,128)}) custom-call(bf16[256,3072]{1,0:T(8,128)(2,1)} %get-tuple-element.62.grads, bf16[4,256,3072]{2,1,0:T(8,128)(2,1)} %get-tuple-element.63.weight, bf16[8,256,512]{2,1,0:T(8,128)(2,1)} %bitcast.103, bf16[8,256,512]{2,1,0:T(8,128)(2,1)} %bitcast.104, ...), custom_call_target="tpu_custom_call" | custom-call | tf_op jit(solution)/shard_map/finish/pallas_call | solution.py:997
  408.2 1.3 fusion.36
  409.5 1.4 slice_bitcast_fusion
  410.9 1.0 fusion.10
  411.9 1.1 fusion.14
  413.3 0.7 copy.114
  413.9 2.0 copy.113
  416.0 0.6 convert_divide_fusion
  (71 shorter events, 2.2 us)
Async XLA Ops:
  7.2 274.9 %reduce-scatter.2.cloned.1.call-start = ((), (), s32[]{:S(2)}) async-start(), calls=%async_computation.2 | async-start | bytes 2621440 | tf_op jit(solution)/shard_map/reduce_scatter | solution.py:2574
  17.1 66.9 %copy-start.14 = (s32[1536]{0:T(1024)S(1)}, s32[1536]{0:T(1024)}, u32[]{:S(2)}) copy-start(s32[1536]{0:T(1024)} %constant.108.clone) | copy-start | bytes 18436
  86.2 50.0 %copy-start.1 = (bf16[4,256,1024]{2,1,0:T(8,128)(2,1)S(1)}, bf16[4,256,1024]{2,1,0:T(8,128)(2,1)}, u32[]{:S(2)}) copy-start(bf16[4,256,1024]{2,1,0:T(8,128)(2,1)} %get-tuple-element.49) | copy-start | bytes 6291460
  86.2 50.0 %copy-start.3 = (bf16[256,1,1024]{2,0,1:T(8,128)(2,1)S(1)}, bf16[256,1,1024]{2,0,1:T(8,128)(2,1)}, u32[]{:S(2)}) copy-start(bf16[256,1,1024]{2,0,1:T(8,128)(2,1)} %param.16) | copy-start | bytes 1572868
  138.1 1.2 copy-start.4
  138.3 2.9 copy-start.10
  138.3 3.7 copy-start.9
  246.3 1.0 copy-start.5
  247.4 1.0 copy-start.2
  248.4 2.1 copy-start
  253.8 27.6 %all-to-all-start = ((bf16[8,256,128]{2,1,0:T(8,128)(2,1)}), bf16[8,256,128]{2,1,0:T(8,128)(2,1)S(1)}, u32[]{:S(2)}, u32[]{:S(2)}) async-start(bf16[8,256,128]{2,1,0:T(8,128)(2,1)} %bitcast.101), calls=%async_computation | async-start | bytes 1048576 | tf_op jit(solution)/shard_map/all_to_all | solution.py:2568
  281.4 0.8 copy-start.7
  282.2 53.1 %copy-start.13 = (s32[3,512]{1,0:T(4,128)S(1)}, s32[3,512]{1,0:T(4,128)}, u32[]{:S(2)}) copy-start(s32[3,512]{1,0:T(4,128)} %constant.125) | copy-start | bytes 18436
  398.1 12.9 %copy-start.8 = (bf16[576,256]{1,0:T(8,128)(2,1)S(1)}, bf16[576,256]{1,0:T(8,128)(2,1)}, u32[]{:S(2)}) copy-start(bf16[576,256]{1,0:T(8,128)(2,1)} %get-tuple-element.158) | copy-start | bytes 884740
  398.1 12.9 %copy-start.12 = (bf16[8,72,1024]{2,1,0:T(8,128)(2,1)S(1)}, bf16[8,72,1024]{2,1,0:T(8,128)(2,1)}, u32[]{:S(2)}) copy-start(bf16[8,72,1024]{2,1,0:T(8,128)(2,1)} %get-tuple-element.56) | copy-start | bytes 3538948
  411.9 2.0 copy-start.6
  413.0 3.0 copy-start.11
Sparse Core Ops, SparseCore 0:
  250.7 31.3 reduce-scatter.1

commit v6 on v5

--- a/solution.py
+++ b/solution.py
@@ -1509,6 +1509,17 @@
     across = jnp.concatenate(grad_queries, axis=0) * score_scale
     out_ref[rows_at(query_tile), :width] = jnp.transpose(across).astype(jnp.bfloat16)
 
+    for step in range(tiles):
+        middles = [key for key in range(groups) if key * 2 // groups == step]
+        lasts = [key for key in range(groups) if min(tiles - 1, 2 + key * 3 // 4) == step]
+
+        @pl.when(query_tile == step)
+        def _():
+            for key in middles:
+                job.middle(key)
+            for key in lasts:
+                job.last(key)
+
     @pl.when(query_tile == tiles - 1)
     def _():
         out_ref[:, width : 2 * width] = (grad_key_sc[...] * score_scale).astype(jnp.bfloat16)
@@ -1520,17 +1531,6 @@
                     [near_sc[head, near], jnp.zeros((tile, tile), jnp.float32)], axis=1
                 )
                 near_ref[pl.ds(head * 3 + near, 1), :] = unskew_sum(wide)
-
-    for step in range(tiles):
-        middles = [key for key in range(groups) if key * 2 // groups == step]
-        lasts = [key for key in range(groups) if min(tiles - 1, 2 + key * 3 // 4) == step]
-
-        @pl.when(query_tile == step)
-        def _():
-            for key in middles:
-                job.middle(key)
-            for key in lasts:
-                job.last(key)
 
     @pl.when(query_tile == tiles - 1)
     def _():

time: 425 us -> 425 us (level)
  no operation moved by 1% of the time
where the time goes in v6:
time: 425 us; the launch traced here: 423 us
  Pallas kernels  355 us (84%)
  local copies, waits for them, and re-layouts  20.8 us (5%)
  between operations  15.7 us (4%)
  matrix products  15.1 us (4%)
  other arithmetic  11.6 us (3%)
    pallas_call x1, Pallas kernels, experts(): pl.pallas_call(functools.partial(experts_kernel, experts_here, groups, co...  98.8 us
    pallas_call x1, Pallas kernels, entry_gather(): pl.pallas_call(functools.partial(entry_kernel, groups, columns), out_shap...  63.2 us
    pallas_call x1, Pallas kernels, tail_exchange(): pl.pallas_call(functools.partial(tail_kernel, groups, columns, chunks), o...  59.8 us
    pallas_call x1, Pallas kernels, attend_backward(): pl.pallas_call(functools.partial(attend_backward_kernel, heads_here, grou...  51.3 us
    pallas_call x1, Pallas kernels, attend_forward(): pl.pallas_call(functools.partial(attend_forward_kernel, heads_here, group...  35.1 us
    pallas_call x1, Pallas kernels, expert_weight_grads(): pl.pallas_call(functools.partial(expert_weight_kernel, parts, halves), gr...  22.1 us
    pallas_call x1, Pallas kernels, exchange_mixed(): pl.pallas_call(functools.partial(mixed_kernel, groups, columns), out_shap...  14.9 us
    pallas_call x1, Pallas kernels, finish(): pl.pallas_call(functools.partial(finish_kernel, width), grid=(3,), out_sh...  10.1 us
  transfers between devices with their start and end apart: 2, of which 1 were waited for; matrix products, arithmetic and copies ran while one was open for 1% of the time, Pallas kernels for 5%

profile of v6, /device:TPU:0, one launch (start us, length us, event | category | flops | bytes accessed | tf_op | source)
XLA Modules:
  0.0 423.4 jit_solution(7146385542058515733)
XLA Ops:
  7.2 0.8 reshape.474
  8.0 0.7 broadcast_add_fusion
  8.7 0.7 broadcast_in_dim.134
  9.3 0.7 convert_element_type.62
  10.0 0.8 slice_bitcast_fusion.2
  10.8 0.7 pad_add_fusion
  11.4 0.3 convert_reduce_fusion
  11.8 0.8 copy.102
  12.7 0.2 fusion.1
  13.0 2.5 convolution_convert_fusion.2
  15.5 0.7 maximum_maximum_fusion.gain
  16.2 0.9 constant_dynamic-slice_fusion.2
  17.1 0.7 fusion.18.pack
  17.9 63.2 %entry_gather.1 = (bf16[8,256,1024]{2,1,0:T(8,128)(2,1)}, bf16[8,256,1024]{2,1,0:T(8,128)(2,1)}, bf16[8,256,384]{2,1,0:T(8,128)(2,1)}, bf16[4,256,512]{2,1,0:T(8...) custom-call(bf16[256,1024]{1,0:T(8,128)(2,1)} %bitcast.109, ...), custom_call_target="tpu_custom_call" | custom-call | tf_op jit(solution)/shard_map/entry_gather/pallas_call | solution.py:429
  81.1 0.7 slice_reduce_fusion.1
  81.9 1.4 fusion.37
  84.0 0.6 convolution_multiply_fusion
  84.9 0.6 reshape.479.base_ref
  85.6 0.6 maximum_multiply_fusion.far_ref
  86.2 35.1 %attend_forward.1 = (bf16[2048,128]{1,0:T(8,128)(2,1)}, f32[8,2,256]{2,1,0:T(2,128)}, bf16[4,8,72,1024]{3,2,1,0:T(8,128)(2,1)}) custom-call(s32[1]{0:T(128)S(6)} %copy.122.prefix_ref, f32[2,2]{1,0:T(2,128)} %maximum_multiply_fusion.far_ref, f32[6,512]{1,0:T(8,128)} %reshape.479.base_ref, bf16[2048,384]{1,0:T(8,128)(2,1)} %bitcast.145, ...), custom_call_target="tpu_custom_call" | custom-call | flops 21474836480 | bytes 2097152 | tf_op jit(solution)/shard_map/attend_forward/pallas_call | solution.py:1328
  121.3 14.9 %exchange_mixed.1 = bf16[256,1024]{1,0:T(8,128)(2,1)} custom-call(bf16[8,256,128]{2,1,0:T(8,128)(2,1)} %bitcast.120), custom_call_target="tpu_custom_call" | custom-call | tf_op jit(solution)/shard_map/exchange_mixed/pallas_call | solution.py:801
  136.2 1.9 multiply_reduce_fusion.2
  138.3 1.0 copy-done.4
  139.3 0.3 fusion.39
  139.7 1.5 convolution_convert_fusion.1
  141.2 0.6 fusion.38
  141.7 0.2 fusion.2
  142.1 0.2 select_reduce_fusion.1
  142.4 0.6 pad.23.gates_in
  143.0 98.8 %experts.1 = (bf16[4,576,704]{2,1,0:T(8,128)(2,1)}, bf16[4,576,704]{2,1,0:T(8,128)(2,1)}, bf16[4,576,704]{2,1,0:T(8,128)(2,1)}, bf16[4,8,72,1024]{3,2,1,0:T(8,12...) custom-call(bf16[8,72,1024]{2,1,0:T(8,128)(2,1)} %bitcast.116, ...), custom_call_target="tpu_custom_call" | custom-call | flops 19931332608 | bytes 36175872 | tf_op jit(solution)/shard_map/experts/pallas_call | solution.py:2259
  241.8 0.8 slice_reduce_fusion
  242.7 0.2 select_reduce_fusion.2
  243.8 1.9 fusion.40
  245.7 0.7 negate_add_fusion
  246.3 0.6 multiply_reduce_fusion
  247.0 0.4 copy-done.5
  247.4 0.3 fusion.6.grad_middle
  247.7 0.7 copy-done.2
  248.4 2.1 convolution_convert_fusion
  250.5 2.3 fusion
  252.9 0.9 copy.121
  253.8 4.1 all-to-all-start
  257.9 0.2 convolution_convert_fusion.4
  258.3 0.2 broadcast_in_dim.135
  258.6 0.8 reduce-precision_convert_fusion
  259.3 22.1 %expert_weight_grads.1 = (f32[4,704,1024]{2,1,0:T(8,128)}, f32[4,704,1024]{2,1,0:T(8,128)}, f32[4,704,1024]{2,1,0:T(8,128)}) custom-call(bf16[4,8,72,1024]{3,2,1,0:T(8,128)(2,1)} %get-tuple-element.70.row_main.row_tail, bf16[4,8,72,1024]{3,2,1,0:T(8,128)(2,1)} %get-tuple-element.70.row_main.row_tail, ...), custom_call_target="tpu_custom_call" | custom-call | flops 9965666304 | bytes 58195968 | tf_op jit(solution)/shard_map/expert_weight_grads/pallas_call | solution.py:2348
  281.4 0.6 reduce-scatter.2.cloned.1.call-done
  282.0 0.2 copy-done.7
  282.2 51.3 %attend_backward.1 = (bf16[2048,384]{1,0:T(8,128)(2,1)}, f32[6,512]{1,0:T(8,128)}, f32[2,2,8,256]{3,2,1,0:T(8,128)}, bf16[8,72,1024]{2,1,0:T(8,128)(2,1)}, bf16[32,1024]{1,0:T(8,128)(2,1)}) custom-call(s32[1]{0:T(128)S(6)} %copy.122.prefix_ref, f32[2,2]{1,0:T(2,128)} %maximum_multiply_fusion.far_ref, f32[6,512]{1,0:T(8,128)} %reshape.479.base_ref, ...), custom_call_target="tpu_custom_call" | custom-call | flops 37580963840 | bytes 4194304 | tf_op jit(solution)/shard_map/attend_backward/pallas_call | solution.py:1553
  333.6 0.9 reduce_sum.181
  334.6 0.7 reshape.494
  335.3 0.2 fusion.5
  335.8 0.2 copy.117
  336.1 1.3 concatenate.77.extra
  337.3 59.8 %tail_exchange.1 = (bf16[256,3072]{1,0:T(8,128)(2,1)}, bf16[8,2,128,512]{3,2,1,0:T(8,128)(2,1)}, bf16[8,32,1024]{2,1,0:T(8,128)(2,1)}, bf16[4,256,3072]{2,1,0:T(8,128)(2,1)}) custom-call(bf16[8,256,384]{2,1,0:T(8,128)(2,1)} %bitcast.115, bf16[2048,1024]{1,0:T(8,128)(2,1)} %bitcast.111, bf16[1024,512]{1,0:T(8,128)(2,1)} %bitcast.112, ...), custom_call_target="tpu_custom_call" | custom-call | tf_op jit(solution)/shard_map/tail_exchange/pallas_call | solution.py:928
  397.2 0.8 slice_convert_fusion
  398.0 10.1 %finish.1 = (f32[256,1024]{1,0:T(8,128)}, f32[256,3072]{1,0:T(8,128)}, f32[256,1024]{1,0:T(8,128)}, f32[128,256]{1,0:T(8,128)}) custom-call(bf16[256,3072]{1,0:T(8,128)(2,1)} %get-tuple-element.62.grads, bf16[4,256,3072]{2,1,0:T(8,128)(2,1)} %get-tuple-element.63.weight, bf16[8,256,512]{2,1,0:T(8,128)(2,1)} %bitcast.103, bf16[8,256,512]{2,1,0:T(8,128)(2,1)} %bitcast.104, ...), custom_call_target="tpu_custom_call" | custom-call | tf_op jit(solution)/shard_map/finish/pallas_call | solution.py:997
  408.2 1.3 fusion.36
  409.5 1.4 slice_bitcast_fusion
  410.9 1.0 fusion.10
  411.9 1.1 fusion.14
  413.3 0.7 copy.114
  413.9 2.0 copy.113
  416.0 0.6 convert_divide_fusion
  (71 shorter events, 2.2 us)
Async XLA Ops:
  7.2 274.9 %reduce-scatter.2.cloned.1.call-start = ((), (), s32[]{:S(2)}) async-start(), calls=%async_computation.2 | async-start | bytes 2621440 | tf_op jit(solution)/shard_map/reduce_scatter | solution.py:2574
  17.1 66.9 %copy-start.14 = (s32[1536]{0:T(1024)S(1)}, s32[1536]{0:T(1024)}, u32[]{:S(2)}) copy-start(s32[1536]{0:T(1024)} %constant.108.clone) | copy-start | bytes 18436
  86.2 50.0 %copy-start.1 = (bf16[4,256,1024]{2,1,0:T(8,128)(2,1)S(1)}, bf16[4,256,1024]{2,1,0:T(8,128)(2,1)}, u32[]{:S(2)}) copy-start(bf16[4,256,1024]{2,1,0:T(8,128)(2,1)} %get-tuple-element.49) | copy-start | bytes 6291460
  86.2 50.0 %copy-start.3 = (bf16[256,1,1024]{2,0,1:T(8,128)(2,1)S(1)}, bf16[256,1,1024]{2,0,1:T(8,128)(2,1)}, u32[]{:S(2)}) copy-start(bf16[256,1,1024]{2,0,1:T(8,128)(2,1)} %param.16) | copy-start | bytes 1572868
  138.1 1.2 copy-start.4
  138.3 2.9 copy-start.10
  138.3 3.7 copy-start.9
  246.3 1.0 copy-start.5
  247.4 1.0 copy-start.2
  248.4 2.1 copy-start
  253.8 27.6 %all-to-all-start = ((bf16[8,256,128]{2,1,0:T(8,128)(2,1)}), bf16[8,256,128]{2,1,0:T(8,128)(2,1)S(1)}, u32[]{:S(2)}, u32[]{:S(2)}) async-start(bf16[8,256,128]{2,1,0:T(8,128)(2,1)} %bitcast.101), calls=%async_computation | async-start | bytes 1048576 | tf_op jit(solution)/shard_map/all_to_all | solution.py:2568
  281.4 0.8 copy-start.7
  282.2 53.1 %copy-start.13 = (s32[3,512]{1,0:T(4,128)S(1)}, s32[3,512]{1,0:T(4,128)}, u32[]{:S(2)}) copy-start(s32[3,512]{1,0:T(4,128)} %constant.125) | copy-start | bytes 18436
  398.0 12.9 %copy-start.8 = (bf16[576,256]{1,0:T(8,128)(2,1)S(1)}, bf16[576,256]{1,0:T(8,128)(2,1)}, u32[]{:S(2)}) copy-start(bf16[576,256]{1,0:T(8,128)(2,1)} %get-tuple-element.158) | copy-start | bytes 884740
  398.0 12.9 %copy-start.12 = (bf16[8,72,1024]{2,1,0:T(8,128)(2,1)S(1)}, bf16[8,72,1024]{2,1,0:T(8,128)(2,1)}, u32[]{:S(2)}) copy-start(bf16[8,72,1024]{2,1,0:T(8,128)(2,1)} %get-tuple-element.56) | copy-start | bytes 3538948
  411.9 2.0 copy-start.6
  413.0 3.0 copy-start.11
Sparse Core Ops, SparseCore 0:
  250.7 31.3 reduce-scatter.1

commit v7 on v6

--- a/solution.py
+++ b/solution.py
@@ -905,9 +905,9 @@
     tail.line.hop(1)
     tail.side.hop(3)
     tail.line.hop(2)
+    tail.line.hop(3)
     for key in late:
         tail.swap.start(key)
-    tail.line.hop(3)
     tail.column.forward()
     tail.side.finish()
     tail.swap.arrive()

time: 425 us -> 425 us (level)
  no operation moved by 1% of the time
where the time goes in v7:
time: 425 us; the launch traced here: 423 us
  Pallas kernels  355 us (84%)
  local copies, waits for them, and re-layouts  20.8 us (5%)
  between operations  15.7 us (4%)
  matrix products  15.1 us (4%)
  other arithmetic  11.6 us (3%)
    pallas_call x1, Pallas kernels, experts(): pl.pallas_call(functools.partial(experts_kernel, experts_here, groups, co...  98.8 us
    pallas_call x1, Pallas kernels, entry_gather(): pl.pallas_call(functools.partial(entry_kernel, groups, columns), out_shap...  63.2 us
    pallas_call x1, Pallas kernels, tail_exchange(): pl.pallas_call(functools.partial(tail_kernel, groups, columns, chunks), o...  59.8 us
    pallas_call x1, Pallas kernels, attend_backward(): pl.pallas_call(functools.partial(attend_backward_kernel, heads_here, grou...  51.3 us
    pallas_call x1, Pallas kernels, attend_forward(): pl.pallas_call(functools.partial(attend_forward_kernel, heads_here, group...  35.1 us
    pallas_call x1, Pallas kernels, expert_weight_grads(): pl.pallas_call(functools.partial(expert_weight_kernel, parts, halves), gr...  22.1 us
    pallas_call x1, Pallas kernels, exchange_mixed(): pl.pallas_call(functools.partial(mixed_kernel, groups, columns), out_shap...  14.9 us
    pallas_call x1, Pallas kernels, finish(): pl.pallas_call(functools.partial(finish_kernel, width), grid=(3,), out_sh...  10.1 us
  transfers between devices with their start and end apart: 2, of which 1 were waited for; matrix products, arithmetic and copies ran while one was open for 1% of the time, Pallas kernels for 5%

profile of v7, /device:TPU:0, one launch (start us, length us, event | category | flops | bytes accessed | tf_op | source)
XLA Modules:
  0.0 423.4 jit_solution(12781472751797809384)
XLA Ops:
  7.2 0.8 reshape.474
  8.0 0.7 broadcast_add_fusion
  8.7 0.7 broadcast_in_dim.134
  9.3 0.7 convert_element_type.62
  10.0 0.8 slice_bitcast_fusion.2
  10.8 0.7 pad_add_fusion
  11.4 0.3 convert_reduce_fusion
  11.8 0.8 copy.102
  12.7 0.2 fusion.1
  13.0 2.5 convolution_convert_fusion.2
  15.5 0.7 maximum_maximum_fusion.gain
  16.2 0.9 constant_dynamic-slice_fusion.2
  17.1 0.7 fusion.18.pack
  17.9 63.2 %entry_gather.1 = (bf16[8,256,1024]{2,1,0:T(8,128)(2,1)}, bf16[8,256,1024]{2,1,0:T(8,128)(2,1)}, bf16[8,256,384]{2,1,0:T(8,128)(2,1)}, bf16[4,256,512]{2,1,0:T(8...) custom-call(bf16[256,1024]{1,0:T(8,128)(2,1)} %bitcast.109, ...), custom_call_target="tpu_custom_call" | custom-call | tf_op jit(solution)/shard_map/entry_gather/pallas_call | solution.py:429
  81.1 0.7 slice_reduce_fusion.1
  81.9 1.4 fusion.37
  84.0 0.6 convolution_multiply_fusion
  84.9 0.6 reshape.479.base_ref
  85.6 0.6 maximum_multiply_fusion.far_ref
  86.2 35.1 %attend_forward.1 = (bf16[2048,128]{1,0:T(8,128)(2,1)}, f32[8,2,256]{2,1,0:T(2,128)}, bf16[4,8,72,1024]{3,2,1,0:T(8,128)(2,1)}) custom-call(s32[1]{0:T(128)S(6)} %copy.122.prefix_ref, f32[2,2]{1,0:T(2,128)} %maximum_multiply_fusion.far_ref, f32[6,512]{1,0:T(8,128)} %reshape.479.base_ref, bf16[2048,384]{1,0:T(8,128)(2,1)} %bitcast.145, ...), custom_call_target="tpu_custom_call" | custom-call | flops 21474836480 | bytes 2097152 | tf_op jit(solution)/shard_map/attend_forward/pallas_call | solution.py:1328
  121.3 14.9 %exchange_mixed.1 = bf16[256,1024]{1,0:T(8,128)(2,1)} custom-call(bf16[8,256,128]{2,1,0:T(8,128)(2,1)} %bitcast.120), custom_call_target="tpu_custom_call" | custom-call | tf_op jit(solution)/shard_map/exchange_mixed/pallas_call | solution.py:801
  136.2 1.9 multiply_reduce_fusion.2
  138.3 1.0 copy-done.4
  139.3 0.3 fusion.39
  139.7 1.5 convolution_convert_fusion.1
  141.2 0.6 fusion.38
  141.7 0.2 fusion.2
  142.1 0.2 select_reduce_fusion.1
  142.4 0.6 pad.23.gates_in
  143.0 98.8 %experts.1 = (bf16[4,576,704]{2,1,0:T(8,128)(2,1)}, bf16[4,576,704]{2,1,0:T(8,128)(2,1)}, bf16[4,576,704]{2,1,0:T(8,128)(2,1)}, bf16[4,8,72,1024]{3,2,1,0:T(8,12...) custom-call(bf16[8,72,1024]{2,1,0:T(8,128)(2,1)} %bitcast.116, ...), custom_call_target="tpu_custom_call" | custom-call | flops 19931332608 | bytes 36175872 | tf_op jit(solution)/shard_map/experts/pallas_call | solution.py:2259
  241.8 0.8 slice_reduce_fusion
  242.7 0.2 select_reduce_fusion.2
  243.8 1.9 fusion.40
  245.7 0.7 negate_add_fusion
  246.3 0.6 multiply_reduce_fusion
  247.0 0.4 copy-done.5
  247.4 0.3 fusion.6.grad_middle
  247.7 0.7 copy-done.2
  248.4 2.1 convolution_convert_fusion
  250.5 2.3 fusion
  252.9 0.9 copy.121
  253.8 4.1 all-to-all-start
  257.9 0.2 convolution_convert_fusion.4
  258.3 0.2 broadcast_in_dim.135
  258.6 0.8 reduce-precision_convert_fusion
  259.3 22.1 %expert_weight_grads.1 = (f32[4,704,1024]{2,1,0:T(8,128)}, f32[4,704,1024]{2,1,0:T(8,128)}, f32[4,704,1024]{2,1,0:T(8,128)}) custom-call(bf16[4,8,72,1024]{3,2,1,0:T(8,128)(2,1)} %get-tuple-element.70.row_main.row_tail, bf16[4,8,72,1024]{3,2,1,0:T(8,128)(2,1)} %get-tuple-element.70.row_main.row_tail, ...), custom_call_target="tpu_custom_call" | custom-call | flops 9965666304 | bytes 58195968 | tf_op jit(solution)/shard_map/expert_weight_grads/pallas_call | solution.py:2348
  281.4 0.6 reduce-scatter.2.cloned.1.call-done
  282.0 0.2 copy-done.7
  282.2 51.3 %attend_backward.1 = (bf16[2048,384]{1,0:T(8,128)(2,1)}, f32[6,512]{1,0:T(8,128)}, f32[2,2,8,256]{3,2,1,0:T(8,128)}, bf16[8,72,1024]{2,1,0:T(8,128)(2,1)}, bf16[32,1024]{1,0:T(8,128)(2,1)}) custom-call(s32[1]{0:T(128)S(6)} %copy.122.prefix_ref, f32[2,2]{1,0:T(2,128)} %maximum_multiply_fusion.far_ref, f32[6,512]{1,0:T(8,128)} %reshape.479.base_ref, ...), custom_call_target="tpu_custom_call" | custom-call | flops 37580963840 | bytes 4194304 | tf_op jit(solution)/shard_map/attend_backward/pallas_call | solution.py:1553
  333.6 0.9 reduce_sum.181
  334.6 0.7 reshape.494
  335.3 0.2 fusion.5
  335.8 0.2 copy.117
  336.1 1.3 concatenate.77.extra
  337.3 59.8 %tail_exchange.1 = (bf16[256,3072]{1,0:T(8,128)(2,1)}, bf16[8,2,128,512]{3,2,1,0:T(8,128)(2,1)}, bf16[8,32,1024]{2,1,0:T(8,128)(2,1)}, bf16[4,256,3072]{2,1,0:T(8,128)(2,1)}) custom-call(bf16[8,256,384]{2,1,0:T(8,128)(2,1)} %bitcast.115, bf16[2048,1024]{1,0:T(8,128)(2,1)} %bitcast.111, bf16[1024,512]{1,0:T(8,128)(2,1)} %bitcast.112, ...), custom_call_target="tpu_custom_call" | custom-call | tf_op jit(solution)/shard_map/tail_exchange/pallas_call | solution.py:928
  397.2 0.8 slice_convert_fusion
  398.0 10.1 %finish.1 = (f32[256,1024]{1,0:T(8,128)}, f32[256,3072]{1,0:T(8,128)}, f32[256,1024]{1,0:T(8,128)}, f32[128,256]{1,0:T(8,128)}) custom-call(bf16[256,3072]{1,0:T(8,128)(2,1)} %get-tuple-element.62.grads, bf16[4,256,3072]{2,1,0:T(8,128)(2,1)} %get-tuple-element.63.weight, bf16[8,256,512]{2,1,0:T(8,128)(2,1)} %bitcast.103, bf16[8,256,512]{2,1,0:T(8,128)(2,1)} %bitcast.104, ...), custom_call_target="tpu_custom_call" | custom-call | tf_op jit(solution)/shard_map/finish/pallas_call | solution.py:997
  408.2 1.3 fusion.36
  409.5 1.4 slice_bitcast_fusion
  410.9 1.0 fusion.10
  411.9 1.1 fusion.14
  413.3 0.7 copy.114
  413.9 2.0 copy.113
  416.0 0.6 convert_divide_fusion
  (71 shorter events, 2.2 us)
Async XLA Ops:
  7.2 274.9 %reduce-scatter.2.cloned.1.call-start = ((), (), s32[]{:S(2)}) async-start(), calls=%async_computation.2 | async-start | bytes 2621440 | tf_op jit(solution)/shard_map/reduce_scatter | solution.py:2574
  17.1 66.9 %copy-start.14 = (s32[1536]{0:T(1024)S(1)}, s32[1536]{0:T(1024)}, u32[]{:S(2)}) copy-start(s32[1536]{0:T(1024)} %constant.108.clone) | copy-start | bytes 18436
  86.2 50.0 %copy-start.1 = (bf16[4,256,1024]{2,1,0:T(8,128)(2,1)S(1)}, bf16[4,256,1024]{2,1,0:T(8,128)(2,1)}, u32[]{:S(2)}) copy-start(bf16[4,256,1024]{2,1,0:T(8,128)(2,1)} %get-tuple-element.49) | copy-start | bytes 6291460
  86.2 50.0 %copy-start.3 = (bf16[256,1,1024]{2,0,1:T(8,128)(2,1)S(1)}, bf16[256,1,1024]{2,0,1:T(8,128)(2,1)}, u32[]{:S(2)}) copy-start(bf16[256,1,1024]{2,0,1:T(8,128)(2,1)} %param.16) | copy-start | bytes 1572868
  138.1 1.2 copy-start.4
  138.3 2.9 copy-start.10
  138.3 3.7 copy-start.9
  246.3 1.0 copy-start.5
  247.4 1.0 copy-start.2
  248.4 2.1 copy-start
  253.8 27.6 %all-to-all-start = ((bf16[8,256,128]{2,1,0:T(8,128)(2,1)}), bf16[8,256,128]{2,1,0:T(8,128)(2,1)S(1)}, u32[]{:S(2)}, u32[]{:S(2)}) async-start(bf16[8,256,128]{2,1,0:T(8,128)(2,1)} %bitcast.101), calls=%async_computation | async-start | bytes 1048576 | tf_op jit(solution)/shard_map/all_to_all | solution.py:2568
  281.4 0.8 copy-start.7
  282.2 53.1 %copy-start.13 = (s32[3,512]{1,0:T(4,128)S(1)}, s32[3,512]{1,0:T(4,128)}, u32[]{:S(2)}) copy-start(s32[3,512]{1,0:T(4,128)} %constant.125) | copy-start | bytes 18436
  398.0 12.9 %copy-start.8 = (bf16[576,256]{1,0:T(8,128)(2,1)S(1)}, bf16[576,256]{1,0:T(8,128)(2,1)}, u32[]{:S(2)}) copy-start(bf16[576,256]{1,0:T(8,128)(2,1)} %get-tuple-element.158) | copy-start | bytes 884740
  398.0 12.9 %copy-start.12 = (bf16[8,72,1024]{2,1,0:T(8,128)(2,1)S(1)}, bf16[8,72,1024]{2,1,0:T(8,128)(2,1)}, u32[]{:S(2)}) copy-start(bf16[8,72,1024]{2,1,0:T(8,128)(2,1)} %get-tuple-element.56) | copy-start | bytes 3538948
  411.9 2.0 copy-start.6
  413.0 3.0 copy-start.11
Sparse Core Ops, SparseCore 0:
  250.7 31.3 reduce-scatter.1
